TPU v7x, 1024 devices: a whole 8x8x8 slice. The times are simulated.
1024 devices in a mesh: aa: 32 (over x, z_lo), col: 4 (over z_hi, core), pb: 8 (over y).
Axes of the slice: x: 8, y: 8, z: 8 (z_hi: 2, z_lo: 4; z = z_hi * 4 + z_lo), core: 2. Of those that a mesh axis runs over, the one named last changes fastest.
Arguments:
- b_ac: bfloat16 [1536, 512, 1024], P('pb', 'aa', 'col'), may hold values from -6 to 6
- b_oc: bfloat16 [1536, 32, 1024], P('pb', None, 'col'), may hold values from -6 to 6
- t1: bfloat16 [32, 512], P(None, 'aa'), may hold values from -0.59765625 to 0.59765625
- f_bd: bfloat16 [1536, 256], P('pb'), may hold values from -0.15625 to 0.15625
- t2: bfloat16 [512, 32768], P('aa', ('col', 'pb')), may hold values from -0.0625 to 0.0625
Outputs:
- residual: float32 [512, 4096], P(('col', 'pb'), 'aa')
All inputs are finite; a program needn't handle non-finite values.
Results may differ from a plain program's by a relative error of at most 0.0041.
Values may be sent and summed in bfloat16 or wider, within the bound.
No kernel may reach another device: no remote copies, remote signals or barrier semaphores. Data moves between devices by JAX's collectives and lax.ppermute only.
A program may use at most 32 MiB of HBM per device.

v0:
```python
import jax
import jax.numpy as jnp
from jax import lax
from jax.sharding import PartitionSpec as P

BB = 8
DB = 32


def shards(b_ac, b_oc, t1, f_bd, t2):
    correction = jnp.einsum("ka,qkc->qac", t1, b_oc, preferred_element_type=jnp.float32)
    dressed = (b_ac - correction).astype(jnp.bfloat16)
    regrouped = lax.all_to_all(dressed, "pb", split_axis=2, concat_axis=0, tiled=True)
    a_width = regrouped.shape[1]
    c_width = regrouped.shape[2]
    flat_factors = regrouped.reshape(regrouped.shape[0], a_width * c_width)
    contract_rows = (((0,), (0,)), ((), ()))
    factor_all = lax.all_gather(f_bd, "pb", axis=0, tiled=True)
    ladder = lax.dot_general(
        flat_factors, factor_all, contract_rows, preferred_element_type=jnp.float32
    )
    ladder = ladder.astype(jnp.bfloat16)
    ladder = (
        ladder.reshape(a_width, c_width, BB, DB)
        .transpose(0, 2, 1, 3)
        .reshape(a_width * BB, c_width * DB)
    )
    partial_sums = lax.dot_general(
        lax.all_gather(t2, "aa", axis=0, tiled=True),
        ladder,
        (((1,), (1,)), ((), ())),
        preferred_element_type=jnp.float32,
    )
    return lax.psum_scatter(partial_sums, ("col", "pb"), scatter_dimension=0, tiled=True)


def solution(mesh):
    placed = (
        P("pb", "aa", "col"),
        P("pb", None, "col"),
        P(None, "aa"),
        P("pb", None),
        P("aa", ("col", "pb")),
    )
    return jax.shard_map(
        shards, mesh=mesh, in_specs=placed, out_specs=P(("col", "pb"), "aa"), check_vma=False
    )
```

profile of v0, /device:TPU:4, one launch (start us, length us, event | category | flops | bytes accessed | tf_op | source)
XLA Modules:
  0.0 343.0 jit_solution(4652989893577019761)
XLA Ops:
  6.5 0.0 copy-start
  6.5 1.9 copy-done
  8.4 3.1 fusion
  11.6 4.7 %copy.16 = bf16[192,16,256]{0,1,2:T(8,128)(2,1)} copy(bf16[192,16,256]{2,1,0:T(8,128)(2,1)} %fusion) | data formatting | bytes 3145728 | tf_op jit(solution)/shard_map/convert_element_type | solution.py:12
  16.2 0.0 copy-start.1
  16.2 7.7 %all-to-all-start = ((bf16[192,16,256]{0,1,2:T(8,128)(2,1)}), bf16[192,16,256]{0,1,2:T(8,128)(2,1)}, u32[]{:S(2)}, u32[]{:S(2)}) async-start(bf16[192,16,256]{0,1,2:T(8,128)(2,1)} %copy.16), calls=%async_computation | async-start | bytes 4194304 | tf_op jit(solution)/shard_map/all_to_all | solution.py:13
  23.9 0.0 all-gather.2.cloned.1.call-start
  24.0 0.7 all-gather.2.cloned.1.call-update
  24.7 0.0 reduce-scatter.4.cloned.1.call-start
  24.7 0.0 copy-done.1
  24.7 70.7 %all_gather.6 = bf16[1536,256]{1,0:T(8,128)(2,1)} all-gather(bf16[192,256]{1,0:T(8,128)(2,1)S(1)} %copy-done.1), channel_id=1, replica_groups=mesh['aa'=32,'col'=4,'pb'=8] {'pb'}, dimensions={0}, use_global_device_ids=true | all-gather | bytes 884736 | tf_op jit(solution)/shard_map/all_gather | solution.py:18
  95.4 0.0 all-to-all-done
  95.4 4.1 %copy.18 = bf16[8,192,16,32]{1,0,3,2:T(8,128)(2,1)} copy(bf16[8,192,16,32]{1,2,3,0:T(8,128)(2,1)} %bitcast.4) | data formatting | bytes 3145728 | tf_op jit(solution)/shard_map/all_to_all | solution.py:13
  99.5 4.3 %reshape.10 = bf16[1536,512]{0,1:T(8,128)(2,1)} reshape(bf16[8,192,16,32]{1,0,3,2:T(8,128)(2,1)} %copy.18) | data formatting | bytes 3145728 | tf_op jit(solution)/shard_map/reshape | solution.py:16
  103.8 2.2 convolution_convert_fusion
  106.0 1.4 reshape.11
  107.4 2.5 copy.25
  109.8 2.3 reshape.12
  112.2 75.4 %all-gather.2.cloned.1.call-done = bf16[512,1024]{1,0:T(8,128)(2,1)} async-done(((bf16[16,1024]{1,0:T(8,128)(2,1)}), bf16[512,1024]{1,0:T(8,128)(2,1)}) %all-gather.2.cloned.1.call-update) | async-done | bytes 1048592 | tf_op jit(solution)/shard_map/all_gather | solution.py:29
  187.6 2.4 convolution_bitcast_fusion
  190.0 1.8 copy.22
  191.8 0.0 reduce-scatter.4.cloned.1.call-update
  191.8 144.3 %reduce-scatter.4.cloned.1.call-done = f32[16,128]{1,0:T(8,128)} async-done(((f32[512,128]{1,0:T(8,128)}), f32[16,128]{1,0:T(8,128)}) %reduce-scatter.4.cloned.1.call-update) | async-done | bytes 8208 | tf_op jit(solution)/shard_map/reduce_scatter | solution.py:34
Async XLA Ops:
  6.5 1.9 copy-start
  16.2 8.5 %copy-start.1 = (bf16[192,256]{1,0:T(8,128)(2,1)S(1)}, bf16[192,256]{1,0:T(8,128)(2,1)}, u32[]{:S(2)}) copy-start(bf16[192,256]{1,0:T(8,128)(2,1)} %param.8) | copy-start | bytes 294916
  16.2 79.2 %all-to-all-start = ((bf16[192,16,256]{0,1,2:T(8,128)(2,1)}), bf16[192,16,256]{0,1,2:T(8,128)(2,1)}, u32[]{:S(2)}, u32[]{:S(2)}) async-start(bf16[192,16,256]{0,1,2:T(8,128)(2,1)} %copy.16), calls=%async_computation | async-start | bytes 4194304 | tf_op jit(solution)/shard_map/all_to_all | solution.py:13
  23.9 163.7 %all-gather.2.cloned.1.call-start = ((), (), s32[]{:S(2)}) async-start(), calls=%async_computation.2 | async-start | bytes 1081344 | tf_op jit(solution)/shard_map/all_gather | solution.py:29
  24.7 311.5 %reduce-scatter.4.cloned.1.call-start = ((), (), s32[]{:S(2)}) async-start(), calls=%async_computation.3 | async-start | bytes 270336 | tf_op jit(solution)/shard_map/reduce_scatter | solution.py:34
Sparse Core Ops, SparseCore 0:
  27.4 160.1 all-gather.1
  193.3 142.8 reduce-scatter.3
where the time goes:
time: 344 us; the launch traced here: 343 us
  waiting for transfers between devices  220 us (64%)
  blocking collectives  70.7 us (21%)
  local copies, waits for them, and re-layouts  22.9 us (7%)
  between operations  13.4 us (4%)
  starting transfers between devices  7.76 us (2%)
  matrix products  7.71 us (2%)
    reduce_scatter x1, waiting for transfers between devices, shards(): lax.psum_scatter(partial_sums, ('col', 'pb'), scatter_dimension=0, tiled=...  144 us
    all_gather x1, waiting for transfers between devices, shards(): lax.all_gather(t2, 'aa', axis=0, tiled=True)  75.4 us
    all_gather x1, blocking collectives, shards(): factor_all = lax.all_gather(f_bd, 'pb', axis=0, tiled=True)  70.7 us
    all_to_all x1, starting transfers between devices, shards(): lax.all_to_all(dressed, 'pb', split_axis=2, concat_axis=0, tiled=True)  7.69 us
  transfers between devices with their start and end apart: 3, of which 2 were waited for; matrix products, arithmetic and copies ran while one was open for 5% of the time, Pallas kernels for 0%

commit v1 on v0

v1 whole, which is shorter than its diff:
```python
import jax
import jax.numpy as jnp
from jax import lax
from jax.experimental import pallas as pl
from jax.experimental.pallas import tpu as pltpu
from jax.sharding import PartitionSpec as P


BB = 8
DB = 32
Z_RUN = 4
LANES = 128
LANE_GROUPS = LANES // DB


def from_aa(array, x_step, z_flip):
    n_x = lax.axis_size("aa") // Z_RUN
    pairs = [
        (x * Z_RUN + z, (x + x_step) % n_x * Z_RUN + (z ^ z_flip))
        for x in range(n_x)
        for z in range(Z_RUN)
    ]
    return lax.ppermute(array, "aa", pairs)


def gather_amplitudes(t2):
    n_x = lax.axis_size("aa") // Z_RUN
    near = [t2] + [from_aa(t2, 0, flip) for flip in range(1, Z_RUN)]
    near = jnp.stack(near)
    far = [near] + [from_aa(near, step, 0) for step in range(1, n_x)]
    return far


def combine_kernel(place_ref, pieces_ref, *refs):
    far_refs, (out_ref, ladder_ref, turned_ref, factor_ref, t2_ref) = refs[:-5], refs[-5:]
    n_far = len(far_refs)
    rows = far_refs[0].shape[1]
    for step_back, far_ref in enumerate(far_refs):
        for flip in range(Z_RUN):
            at = (step_back * Z_RUN + flip) * rows
            t2_ref[at : at + rows, :] = far_ref[flip]
    total = pieces_ref[0].astype(jnp.float32)
    for shard in range(1, pieces_ref.shape[0]):
        total += pieces_ref[shard].astype(jnp.float32)
    for b_high in range(BB // LANE_GROUPS):
        ladder_ref[b_high] = total[:, b_high * LANES : (b_high + 1) * LANES]
    n_rows = total.shape[0] // LANE_GROUPS
    group = lax.broadcasted_iota(jnp.int32, (n_rows, LANES), 1) // DB

    def pick(by_group):
        chosen = by_group[0]
        for lane_group in range(1, LANE_GROUPS):
            chosen = jnp.where(group == lane_group, by_group[lane_group], chosen)
        return chosen

    for b_high in range(BB // LANE_GROUPS):
        by_c = [
            ladder_ref.at[b_high][pl.ds(c_low, n_rows, stride=LANE_GROUPS), :]
            for c_low in range(LANE_GROUPS)
        ]
        skewed = []
        for turn in range(LANE_GROUPS):
            mixed = pick([by_c[(b_low + turn) % LANE_GROUPS] for b_low in range(LANE_GROUPS)])
            skewed.append(pltpu.roll(mixed, turn * DB, 1) if turn else mixed)
        for b_low in range(LANE_GROUPS):
            b = b_high * LANE_GROUPS + b_low
            by_b = pick([skewed[(c_low - b_low) % LANE_GROUPS] for c_low in range(LANE_GROUPS)])
            for a in range(n_rows // BB):
                at = (a * BB + b) * BB
                turned_ref[at : at + BB, :] = by_b[a * BB : (a + 1) * BB]
    for c_high in range(BB):
        tile = turned_ref[pl.ds(c_high, n_rows, stride=BB), :]
        factor_ref[:, c_high * LANES : (c_high + 1) * LANES] = tile.astype(jnp.bfloat16)
    sums = lax.dot_general(
        t2_ref[...],
        factor_ref[...],
        (((1,), (1,)), ((), ())),
        preferred_element_type=jnp.float32,
    )
    x, z = place_ref[0] // Z_RUN, place_ref[0] % Z_RUN
    for step_back in range(n_far):
        source_x = lax.rem(x + (n_far - step_back), n_far)
        for flip in range(Z_RUN):
            at = (step_back * Z_RUN + flip) * rows
            out_ref[source_x * Z_RUN + (z ^ flip)] = sums[at : at + rows]


def combine(pieces, far, a_width, c_block):
    rows, cd_width = far[0].shape[1:]
    n_aa = len(far) * Z_RUN
    ab_width = a_width * BB
    whole = pl.BlockSpec(memory_space=pltpu.VMEM)
    return pl.pallas_call(
        combine_kernel,
        out_shape=jax.ShapeDtypeStruct((n_aa, rows, ab_width), jnp.float32),
        in_specs=[pl.BlockSpec(memory_space=pltpu.SMEM)] + [whole] * (1 + len(far)),
        out_specs=whole,
        scratch_shapes=[
            pltpu.VMEM((BB // LANE_GROUPS, a_width * c_block, LANES), jnp.float32),
            pltpu.VMEM((ab_width * BB, LANES), jnp.float32),
            pltpu.VMEM((ab_width, cd_width), jnp.bfloat16),
            pltpu.VMEM((n_aa * rows, cd_width), jnp.bfloat16),
        ],
        cost_estimate=pl.CostEstimate(
            flops=2 * n_aa * rows * ab_width * cd_width, bytes_accessed=3 << 20, transcendentals=0
        ),
    )(lax.axis_index("aa").astype(jnp.int32).reshape(1), pieces, *far)


def step(b_ac, b_oc, t1, f_bd, t2):
    n_pb = lax.axis_size("pb")
    _, a_width, c_width = b_ac.shape
    c_block = c_width // n_pb

    far = gather_amplitudes(t2)

    correction = jnp.einsum("ka,qkc->qac", t1, b_oc, preferred_element_type=jnp.float32)
    dressed = (b_ac - correction).astype(jnp.bfloat16)
    partial = jnp.einsum("qac,qn->acn", dressed, f_bd, preferred_element_type=jnp.float32)
    partial = (
        partial.astype(jnp.bfloat16)
        .reshape(a_width, n_pb, c_block, BB * DB)
        .transpose(1, 0, 2, 3)
        .reshape(n_pb, a_width * c_block, BB * DB)
    )
    pieces = lax.all_to_all(partial, "pb", 0, 0, tiled=True)
    pieces, *far = lax.optimization_barrier((pieces, *far))
    sums = combine(pieces, far, a_width, c_block)
    shares = lax.all_to_all(sums, ("col", "pb"), 0, 0, tiled=True)
    return jnp.sum(shares, axis=0)


def solution(mesh):
    placed = (
        P("pb", "aa", "col"),
        P("pb", None, "col"),
        P(None, "aa"),
        P("pb", None),
        P("aa", ("col", "pb")),
    )
    return jax.shard_map(
        step, mesh=mesh, in_specs=placed, out_specs=P(("col", "pb"), "aa"), check_vma=False
    )
```

time: 344 us -> 111 us (0.32)
  the two profiles are of different devices: /device:TPU:4 before, /device:TPU:1 now
where the time goes in v1:
time: 111 us; the launch traced here: 110 us
  starting transfers between devices  50.8 us (46%)
  blocking collectives  33.7 us (30%)
  waiting for transfers between devices  15 us (14%)
  Pallas kernels  3.53 us (3%)
  local copies, waits for them, and re-layouts  3.4 us (3%)
  matrix products  3.25 us (3%)
    ppermute x10, starting transfers between devices, from_aa(): return lax.ppermute(array, 'aa', pairs)  42.5 us
    all_to_all x1, blocking collectives, step(): shares = lax.all_to_all(sums, ('col', 'pb'), 0, 0, tiled=True)  33.7 us
    ppermute x10, waiting for transfers between devices, from_aa(): return lax.ppermute(array, 'aa', pairs)  15 us
    all_to_all x1, starting transfers between devices, step(): pieces = lax.all_to_all(partial, 'pb', 0, 0, tiled=True)  8.22 us
    pallas_call x1, Pallas kernels, combine(): pl.pallas_call(combine_kernel, out_shape=jax.ShapeDtypeStruct((n_aa, rows...  3.53 us
  transfers between devices with their start and end apart: 11, of which 6 were waited for; matrix products, arithmetic and copies ran while one was open for 0% of the time, Pallas kernels for 0%

profile of v1, /device:TPU:1, one launch (start us, length us, event | category | flops | bytes accessed | tf_op | source)
XLA Modules:
  0.0 110.4 jit_solution(7990696774756607499)
XLA Ops:
  0.0 1.9 %copy-done = bf16[192,32,256]{2,1,0:T(8,128)(2,1)S(1)} copy-done((bf16[192,32,256]{2,1,0:T(8,128)(2,1)S(1)}, bf16[192,32,256]{2,1,0:T(8,128)(2,1)}, u32[]{:S(2)}) %copy-start) | copy-done | bytes 3145752
  1.9 2.0 %fusion = bf16[192,16,256]{2,1,0:T(8,128)(2,1)S(1)} fusion(bf16[192,16,256]{2,1,0:T(8,128)(2,1)} %param.5, bf16[192,32,256]{2,1,0:T(8,128)(2,1)S(1)} %copy-done, bf16[32,16]{0,1:T(8,128)(2,1)} %param.7), kind=kOutput, calls=%fused_computation.1 | convolution fusion | flops 52690944 | bytes 6292480 | tf_op jit(solution)/shard_map/ka,qkc->qac/dot_general | solution.py:117
  3.9 0.0 copy-done.5
  3.9 1.3 %convolution_convert_fusion = bf16[16,256,256]{2,1,0:T(8,128)(2,1)S(1)} fusion(bf16[192,16,256]{2,1,0:T(8,128)(2,1)S(1)} %fusion, bf16[192,256]{1,0:T(8,128)(2,1)S(1)} %copy-done.5), kind=kOutput, calls=%fused_computation.2 | convolution fusion | flops 403701760 | bytes 3768320 | tf_op jit(solution)/shard_map/qac,qn->acn/dot_general | solution.py:119
  5.2 1.5 %copy.7 = bf16[16,8,32,256]{3,2,0,1:T(8,128)(2,1)} copy(bf16[16,8,32,256]{3,2,1,0:T(8,128)(2,1)S(1)} %bitcast.21) | data formatting | bytes 4194304 | tf_op jit(solution)/shard_map/reshape | solution.py:122
  6.7 8.2 %all-to-all-start = ((bf16[8,512,256]{2,1,0:T(8,128)(2,1)}), bf16[8,512,256]{2,1,0:T(8,128)(2,1)}, u32[]{:S(2)}, u32[]{:S(2)}) async-start(bf16[8,512,256]{2,1,0:T(8,128)(2,1)} %bitcast.20), calls=%async_computation | async-start | bytes 4194304 | tf_op jit(solution)/shard_map/all_to_all | solution.py:126
  14.9 10.3 %collective-permute-start.2 = (bf16[16,1024]{1,0:T(8,128)(2,1)S(1)}, bf16[16,1024]{1,0:T(8,128)(2,1)S(1)}, u32[]{:S(2)}, u32[]{:S(2)}) collective-permute-start(bf16[16,1024]{1,0:T(8,128)(2,1)S(1)} %copy-done.4), channel_id=1, source_target_pairs={{0,96},{32,64},{64,32},{96,0},{128,224},{160,192},{192,160},{224,1... | collective-permute-start | bytes 98312 | tf_op jit(solution)/shard_map/ppermute | solution.py:23
  25.2 1.9 %collective-permute-start.1 = (bf16[16,1024]{1,0:T(8,128)(2,1)S(1)}, bf16[16,1024]{1,0:T(8,128)(2,1)S(1)}, u32[]{:S(2)}, u32[]{:S(2)}) collective-permute-start(bf16[16,1024]{1,0:T(8,128)(2,1)S(1)} %copy-done.4), channel_id=1, source_target_pairs={{0,64},{32,96},{64,0},{96,32},{128,192},{160,224},{192,128},{224,1... | collective-permute-start | bytes 98312 | tf_op jit(solution)/shard_map/ppermute | solution.py:23
  27.2 2.2 %collective-permute-start = (bf16[16,1024]{1,0:T(8,128)(2,1)S(1)}, bf16[16,1024]{1,0:T(8,128)(2,1)S(1)}, u32[]{:S(2)}, u32[]{:S(2)}) collective-permute-start(bf16[16,1024]{1,0:T(8,128)(2,1)S(1)} %copy-done.4), channel_id=1, source_target_pairs={{0,32},{32,0},{64,96},{96,64},{128,160},{160,128},{192,224},{224,1... | collective-permute-start | bytes 98312 | tf_op jit(solution)/shard_map/ppermute | solution.py:23
  29.4 0.0 collective-permute-done.2
  29.4 1.4 %collective-permute-done.1 = bf16[16,1024]{1,0:T(8,128)(2,1)S(1)} collective-permute-done((bf16[16,1024]{1,0:T(8,128)(2,1)S(1)}, bf16[16,1024]{1,0:T(8,128)(2,1)S(1)}, u32[]{:S(2)}, u32[]{:S(2)}) %collective-permute-start.1) | collective-permute-done | bytes 32800 | tf_op jit(solution)/shard_map/ppermute | solution.py:23
  30.8 1.4 %collective-permute-done = bf16[16,1024]{1,0:T(8,128)(2,1)S(1)} collective-permute-done((bf16[16,1024]{1,0:T(8,128)(2,1)S(1)}, bf16[16,1024]{1,0:T(8,128)(2,1)S(1)}, u32[]{:S(2)}, u32[]{:S(2)}) %collective-permute-start) | collective-permute-done | bytes 32800 | tf_op jit(solution)/shard_map/ppermute | solution.py:23
  32.3 3.1 %collective-permute-start.3 = (bf16[4,16,1024]{2,1,0:T(8,128)(2,1)S(1)}, bf16[4,16,1024]{2,1,0:T(8,128)(2,1)S(1)}, u32[]{:S(2)}, u32[]{:S(2)}) collective-permute-start(bf16[4,16,1024]{2,1,0:T(8,128)(2,1)S(1)} %pad_maximum_fusion.refs_0_), channel_id=1, source_target_pairs={{0,128},{32,160},{64,192},{96,224},{128,256},{160,288},{192,320},{... | collective-permute-start | bytes 393224 | tf_op jit(solution)/shard_map/ppermute | solution.py:23
  35.4 4.0 %collective-permute-start.4 = (bf16[4,16,1024]{2,1,0:T(8,128)(2,1)S(1)}, bf16[4,16,1024]{2,1,0:T(8,128)(2,1)S(1)}, u32[]{:S(2)}, u32[]{:S(2)}) collective-permute-start(bf16[4,16,1024]{2,1,0:T(8,128)(2,1)S(1)} %pad_maximum_fusion.refs_0_), channel_id=1, source_target_pairs={{0,256},{32,288},{64,320},{96,352},{128,384},{160,416},{192,448},{... | collective-permute-start | bytes 393224 | tf_op jit(solution)/shard_map/ppermute | solution.py:23
  39.4 4.4 %collective-permute-start.5 = (bf16[4,16,1024]{2,1,0:T(8,128)(2,1)S(1)}, bf16[4,16,1024]{2,1,0:T(8,128)(2,1)}, u32[]{:S(2)}, u32[]{:S(2)}) collective-permute-start(bf16[4,16,1024]{2,1,0:T(8,128)(2,1)S(1)} %pad_maximum_fusion.refs_0_), channel_id=1, source_target_pairs={{0,384},{32,416},{64,448},{96,480},{128,512},{160,544},{192,576},{... | collective-permute-start | bytes 393224 | tf_op jit(solution)/shard_map/ppermute | solution.py:23
  43.8 3.9 %collective-permute-start.6 = (bf16[4,16,1024]{2,1,0:T(8,128)(2,1)S(1)}, bf16[4,16,1024]{2,1,0:T(8,128)(2,1)}, u32[]{:S(2)}, u32[]{:S(2)}) collective-permute-start(bf16[4,16,1024]{2,1,0:T(8,128)(2,1)S(1)} %pad_maximum_fusion.refs_0_), channel_id=1, source_target_pairs={{0,512},{32,544},{64,576},{96,608},{128,640},{160,672},{192,704},{... | collective-permute-start | bytes 393224 | tf_op jit(solution)/shard_map/ppermute | solution.py:23
  47.7 4.4 %collective-permute-start.7 = (bf16[4,16,1024]{2,1,0:T(8,128)(2,1)S(1)}, bf16[4,16,1024]{2,1,0:T(8,128)(2,1)}, u32[]{:S(2)}, u32[]{:S(2)}) collective-permute-start(bf16[4,16,1024]{2,1,0:T(8,128)(2,1)S(1)} %pad_maximum_fusion.refs_0_), channel_id=1, source_target_pairs={{0,640},{32,672},{64,704},{96,736},{128,768},{160,800},{192,832},{... | collective-permute-start | bytes 393224 | tf_op jit(solution)/shard_map/ppermute | solution.py:23
  52.2 0.0 collective-permute-done.3.refs_1_
  52.2 5.1 %collective-permute-start.8 = (bf16[4,16,1024]{2,1,0:T(8,128)(2,1)S(1)}, bf16[4,16,1024]{2,1,0:T(8,128)(2,1)}, u32[]{:S(2)}, u32[]{:S(2)}) collective-permute-start(bf16[4,16,1024]{2,1,0:T(8,128)(2,1)S(1)} %pad_maximum_fusion.refs_0_), channel_id=1, source_target_pairs={{0,768},{32,800},{64,832},{96,864},{128,896},{160,928},{192,960},{... | collective-permute-start | bytes 393224 | tf_op jit(solution)/shard_map/ppermute | solution.py:23
  57.3 0.0 collective-permute-done.4.refs_2_
  57.4 0.0 copy-start.3
  57.4 3.1 %collective-permute-start.9 = (bf16[4,16,1024]{2,1,0:T(8,128)(2,1)S(1)}, bf16[4,16,1024]{2,1,0:T(8,128)(2,1)}, u32[]{:S(2)}, u32[]{:S(2)}) collective-permute-start(bf16[4,16,1024]{2,1,0:T(8,128)(2,1)S(1)} %pad_maximum_fusion.refs_0_), channel_id=1, source_target_pairs={{0,896},{32,928},{64,960},{96,992},{128,0},{160,32},{192,64},{224,... | collective-permute-start | bytes 393224 | tf_op jit(solution)/shard_map/ppermute | solution.py:23
  60.4 0.0 collective-permute-done.5.refs_3_
  60.4 0.3 collective-permute-done.6.refs_4_
  60.7 3.2 %collective-permute-done.7.refs_5_ = bf16[4,16,1024]{2,1,0:T(8,128)(2,1)} collective-permute-done((bf16[4,16,1024]{2,1,0:T(8,128)(2,1)S(1)}, bf16[4,16,1024]{2,1,0:T(8,128)(2,1)}, u32[]{:S(2)}, u32[]{:S(2)}) %collective-permute-start.7) | collective-permute-done | bytes 131104 | tf_op jit(solution)/shard_map/ppermute | solution.py:23
  63.9 7.1 %collective-permute-done.8.refs_6_ = bf16[4,16,1024]{2,1,0:T(8,128)(2,1)} collective-permute-done((bf16[4,16,1024]{2,1,0:T(8,128)(2,1)S(1)}, bf16[4,16,1024]{2,1,0:T(8,128)(2,1)}, u32[]{:S(2)}, u32[]{:S(2)}) %collective-permute-start.8) | collective-permute-done | bytes 131104 | tf_op jit(solution)/shard_map/ppermute | solution.py:23
  71.0 1.5 %collective-permute-done.9.refs_7_ = bf16[4,16,1024]{2,1,0:T(8,128)(2,1)} collective-permute-done((bf16[4,16,1024]{2,1,0:T(8,128)(2,1)S(1)}, bf16[4,16,1024]{2,1,0:T(8,128)(2,1)}, u32[]{:S(2)}, u32[]{:S(2)}) %collective-permute-start.9) | collective-permute-done | bytes 131104 | tf_op jit(solution)/shard_map/ppermute | solution.py:23
  72.5 0.0 all-to-all-done.pieces_ref
  72.6 0.0 copy-done.1
  72.6 3.5 %shard_map.55 = f32[32,16,128]{2,1,0:T(8,128)} custom-call(s32[1]{0:T(128)} %bitcast.place_ref, bf16[8,512,256]{2,1,0:T(8,128)(2,1)} %all-to-all-done.pieces_ref, bf16[4,16,1024]{2,1,0:T(8,128)(2,1)} %copy-done.1, bf16[4,16,1024]{2,1,0:T(8,128)(2,1)} %copy-done.2, bf16[4,16,1024]{2,1,0:T(8,128)(2,1)} %copy-done.3, ...), custom_call_target="tpu_custom_call" | custom-call | flops 134217728 | bytes 3145728 | tf_op jit(solution)/shard_map/pallas_call | solution.py:93
  76.1 33.7 %all_to_all.10 = f32[32,16,128]{2,1,0:T(8,128)S(1)} all-to-all(f32[32,16,128]{2,1,0:T(8,128)} %shard_map.55), channel_id=1, replica_groups=mesh['aa'=32,'col'=4,'pb'=8] {'col','pb'}, dimensions={0} | all-to-all | bytes 524288 | tf_op jit(solution)/shard_map/all_to_all | solution.py:129
  109.8 0.6 reduce_sum.9
  (9 shorter events, 0.0 us)
Async XLA Ops:
  0.0 1.9 %copy-start = (bf16[192,32,256]{2,1,0:T(8,128)(2,1)S(1)}, bf16[192,32,256]{2,1,0:T(8,128)(2,1)}, u32[]{:S(2)}) copy-start(bf16[192,32,256]{2,1,0:T(8,128)(2,1)} %param.6) | copy-start | bytes 9437188
  0.0 3.9 %copy-start.5 = (bf16[192,256]{1,0:T(8,128)(2,1)S(1)}, bf16[192,256]{1,0:T(8,128)(2,1)}, u32[]{:S(2)}) copy-start(bf16[192,256]{1,0:T(8,128)(2,1)} %param.8) | copy-start | bytes 294916
  6.7 8.2 %copy-start.4 = (bf16[16,1024]{1,0:T(8,128)(2,1)S(1)}, bf16[16,1024]{1,0:T(8,128)(2,1)}, u32[]{:S(2)}) copy-start(bf16[16,1024]{1,0:T(8,128)(2,1)} %param.9) | copy-start | bytes 98308
  6.7 65.9 %all-to-all-start = ((bf16[8,512,256]{2,1,0:T(8,128)(2,1)}), bf16[8,512,256]{2,1,0:T(8,128)(2,1)}, u32[]{:S(2)}, u32[]{:S(2)}) async-start(bf16[8,512,256]{2,1,0:T(8,128)(2,1)} %bitcast.20), calls=%async_computation | async-start | bytes 4194304 | tf_op jit(solution)/shard_map/all_to_all | solution.py:126
  14.9 14.5 %collective-permute-start.2 = (bf16[16,1024]{1,0:T(8,128)(2,1)S(1)}, bf16[16,1024]{1,0:T(8,128)(2,1)S(1)}, u32[]{:S(2)}, u32[]{:S(2)}) collective-permute-start(bf16[16,1024]{1,0:T(8,128)(2,1)S(1)} %copy-done.4), channel_id=1, source_target_pairs={{0,96},{32,64},{64,32},{96,0},{128,224},{160,192},{192,160},{224,1... | collective-permute-start | bytes 98312 | tf_op jit(solution)/shard_map/ppermute | solution.py:23
  25.2 5.6 %collective-permute-start.1 = (bf16[16,1024]{1,0:T(8,128)(2,1)S(1)}, bf16[16,1024]{1,0:T(8,128)(2,1)S(1)}, u32[]{:S(2)}, u32[]{:S(2)}) collective-permute-start(bf16[16,1024]{1,0:T(8,128)(2,1)S(1)} %copy-done.4), channel_id=1, source_target_pairs={{0,64},{32,96},{64,0},{96,32},{128,192},{160,224},{192,128},{224,1... | collective-permute-start | bytes 98312 | tf_op jit(solution)/shard_map/ppermute | solution.py:23
  27.2 5.1 %collective-permute-start = (bf16[16,1024]{1,0:T(8,128)(2,1)S(1)}, bf16[16,1024]{1,0:T(8,128)(2,1)S(1)}, u32[]{:S(2)}, u32[]{:S(2)}) collective-permute-start(bf16[16,1024]{1,0:T(8,128)(2,1)S(1)} %copy-done.4), channel_id=1, source_target_pairs={{0,32},{32,0},{64,96},{96,64},{128,160},{160,128},{192,224},{224,1... | collective-permute-start | bytes 98312 | tf_op jit(solution)/shard_map/ppermute | solution.py:23
  32.2 40.3 %copy-start.1 = (bf16[4,16,1024]{2,1,0:T(8,128)(2,1)}, bf16[4,16,1024]{2,1,0:T(8,128)(2,1)S(1)}, u32[]{:S(2)}) copy-start(bf16[4,16,1024]{2,1,0:T(8,128)(2,1)S(1)} %pad_maximum_fusion.refs_0_) | copy-start | bytes 393220
  32.3 19.9 %collective-permute-start.3 = (bf16[4,16,1024]{2,1,0:T(8,128)(2,1)S(1)}, bf16[4,16,1024]{2,1,0:T(8,128)(2,1)S(1)}, u32[]{:S(2)}, u32[]{:S(2)}) collective-permute-start(bf16[4,16,1024]{2,1,0:T(8,128)(2,1)S(1)} %pad_maximum_fusion.refs_0_), channel_id=1, source_target_pairs={{0,128},{32,160},{64,192},{96,224},{128,256},{160,288},{192,320},{... | collective-permute-start | bytes 393224 | tf_op jit(solution)/shard_map/ppermute | solution.py:23
  35.4 22.0 %collective-permute-start.4 = (bf16[4,16,1024]{2,1,0:T(8,128)(2,1)S(1)}, bf16[4,16,1024]{2,1,0:T(8,128)(2,1)S(1)}, u32[]{:S(2)}, u32[]{:S(2)}) collective-permute-start(bf16[4,16,1024]{2,1,0:T(8,128)(2,1)S(1)} %pad_maximum_fusion.refs_0_), channel_id=1, source_target_pairs={{0,256},{32,288},{64,320},{96,352},{128,384},{160,416},{192,448},{... | collective-permute-start | bytes 393224 | tf_op jit(solution)/shard_map/ppermute | solution.py:23
  39.4 21.0 %collective-permute-start.5 = (bf16[4,16,1024]{2,1,0:T(8,128)(2,1)S(1)}, bf16[4,16,1024]{2,1,0:T(8,128)(2,1)}, u32[]{:S(2)}, u32[]{:S(2)}) collective-permute-start(bf16[4,16,1024]{2,1,0:T(8,128)(2,1)S(1)} %pad_maximum_fusion.refs_0_), channel_id=1, source_target_pairs={{0,384},{32,416},{64,448},{96,480},{128,512},{160,544},{192,576},{... | collective-permute-start | bytes 393224 | tf_op jit(solution)/shard_map/ppermute | solution.py:23
  43.8 16.9 %collective-permute-start.6 = (bf16[4,16,1024]{2,1,0:T(8,128)(2,1)S(1)}, bf16[4,16,1024]{2,1,0:T(8,128)(2,1)}, u32[]{:S(2)}, u32[]{:S(2)}) collective-permute-start(bf16[4,16,1024]{2,1,0:T(8,128)(2,1)S(1)} %pad_maximum_fusion.refs_0_), channel_id=1, source_target_pairs={{0,512},{32,544},{64,576},{96,608},{128,640},{160,672},{192,704},{... | collective-permute-start | bytes 393224 | tf_op jit(solution)/shard_map/ppermute | solution.py:23
  47.7 16.2 %collective-permute-start.7 = (bf16[4,16,1024]{2,1,0:T(8,128)(2,1)S(1)}, bf16[4,16,1024]{2,1,0:T(8,128)(2,1)}, u32[]{:S(2)}, u32[]{:S(2)}) collective-permute-start(bf16[4,16,1024]{2,1,0:T(8,128)(2,1)S(1)} %pad_maximum_fusion.refs_0_), channel_id=1, source_target_pairs={{0,640},{32,672},{64,704},{96,736},{128,768},{160,800},{192,832},{... | collective-permute-start | bytes 393224 | tf_op jit(solution)/shard_map/ppermute | solution.py:23
  52.2 20.4 %copy-start.2 = (bf16[4,16,1024]{2,1,0:T(8,128)(2,1)}, bf16[4,16,1024]{2,1,0:T(8,128)(2,1)S(1)}, u32[]{:S(2)}) copy-start(bf16[4,16,1024]{2,1,0:T(8,128)(2,1)S(1)} %collective-permute-done.3.refs_1_) | copy-start | bytes 393220
  52.2 18.8 %collective-permute-start.8 = (bf16[4,16,1024]{2,1,0:T(8,128)(2,1)S(1)}, bf16[4,16,1024]{2,1,0:T(8,128)(2,1)}, u32[]{:S(2)}, u32[]{:S(2)}) collective-permute-start(bf16[4,16,1024]{2,1,0:T(8,128)(2,1)S(1)} %pad_maximum_fusion.refs_0_), channel_id=1, source_target_pairs={{0,768},{32,800},{64,832},{96,864},{128,896},{160,928},{192,960},{... | collective-permute-start | bytes 393224 | tf_op jit(solution)/shard_map/ppermute | solution.py:23
  57.4 15.2 %copy-start.3 = (bf16[4,16,1024]{2,1,0:T(8,128)(2,1)}, bf16[4,16,1024]{2,1,0:T(8,128)(2,1)S(1)}, u32[]{:S(2)}) copy-start(bf16[4,16,1024]{2,1,0:T(8,128)(2,1)S(1)} %collective-permute-done.4.refs_2_) | copy-start | bytes 393220
  57.4 15.2 %collective-permute-start.9 = (bf16[4,16,1024]{2,1,0:T(8,128)(2,1)S(1)}, bf16[4,16,1024]{2,1,0:T(8,128)(2,1)}, u32[]{:S(2)}, u32[]{:S(2)}) collective-permute-start(bf16[4,16,1024]{2,1,0:T(8,128)(2,1)S(1)} %pad_maximum_fusion.refs_0_), channel_id=1, source_target_pairs={{0,896},{32,928},{64,960},{96,992},{128,0},{160,32},{192,64},{224,... | collective-permute-start | bytes 393224 | tf_op jit(solution)/shard_map/ppermute | solution.py:23

commit v2 on v1

v2 whole, which is shorter than its diff:
```python
import jax
import jax.numpy as jnp
from jax import lax
from jax.experimental import pallas as pl
from jax.experimental.pallas import tpu as pltpu
from jax.sharding import PartitionSpec as P


BB = 8
DB = 32
LANES = 128
LANE_GROUPS = LANES // DB
VMEM = pl.BlockSpec(memory_space=pltpu.VMEM)
SMEM = pl.BlockSpec(memory_space=pltpu.SMEM)


def split_kernel(place_ref, ladder_ref, up_ref, down_ref, across_ref, up2_ref, down2_ref, own_ref):
    a_width, c_width, _ = ladder_ref.shape
    c_block = own_ref.shape[0] // a_width
    n_pb = c_width // c_block
    for distance, out_ref in (
        (1, up_ref.at[0]),
        (3, up_ref.at[1]),
        (n_pb - 1, down_ref.at[0]),
        (n_pb - 3, down_ref.at[1]),
        (4, across_ref),
        (2, up2_ref),
        (n_pb - 2, down2_ref),
        (0, own_ref),
    ):
        c_at = pl.multiple_of(lax.rem(place_ref[0] + distance, n_pb) * c_block, c_block)
        for a in range(a_width):
            out_ref[a * c_block : (a + 1) * c_block, :] = ladder_ref[a, pl.ds(c_at, c_block), :]


def split(ladder, place, n_pb):
    a_width, c_width, bd_width = ladder.shape
    block = (a_width * c_width // n_pb, bd_width)
    shapes = [(2, *block)] * 2 + [block] * 4
    return pl.pallas_call(
        split_kernel,
        out_shape=[jax.ShapeDtypeStruct(shape, ladder.dtype) for shape in shapes],
        in_specs=[SMEM, VMEM],
        out_specs=[VMEM] * 6,
        cost_estimate=pl.CostEstimate(flops=0, bytes_accessed=4 << 20, transcendentals=0),
    )(place, ladder)


def merge_kernel(core_ref, up_ref, down_ref, across_ref, up2_ref, down2_ref, up_out, down_out):
    across = across_ref[...].astype(jnp.float32)
    zero = jnp.zeros_like(across)
    for core, passing_ref, own_ref, out_ref in (
        (0, up_ref, up2_ref, up_out),
        (1, down_ref, down2_ref, down_out),
    ):
        total = own_ref[...].astype(jnp.float32) + passing_ref[1].astype(jnp.float32)
        total += jnp.where(core_ref[0] == core, across, zero)
        out_ref[...] = total.astype(out_ref.dtype)


def merge(core, up, down, across, up2, down2):
    return pl.pallas_call(
        merge_kernel,
        out_shape=[jax.ShapeDtypeStruct(up2.shape, up2.dtype)] * 2,
        in_specs=[SMEM] + [VMEM] * 5,
        out_specs=[VMEM] * 2,
        cost_estimate=pl.CostEstimate(flops=4 * up2.size, bytes_accessed=2 << 20, transcendentals=0),
    )(core, up, down, across, up2, down2)


def combine_kernel(
    own_ref, up_ref, down_ref, up2_ref, down2_ref, t2_ref, out_ref, ladder_ref, turned_ref, factor_ref
):
    total = own_ref[...].astype(jnp.float32)
    total += up_ref[0].astype(jnp.float32)
    total += down_ref[0].astype(jnp.float32)
    total += up2_ref[...].astype(jnp.float32)
    total += down2_ref[...].astype(jnp.float32)
    for b_high in range(BB // LANE_GROUPS):
        ladder_ref[b_high] = total[:, b_high * LANES : (b_high + 1) * LANES]
    n_rows = total.shape[0] // LANE_GROUPS
    group = lax.broadcasted_iota(jnp.int32, (n_rows, LANES), 1) // DB

    def pick(by_group):
        chosen = by_group[0]
        for lane_group in range(1, LANE_GROUPS):
            chosen = jnp.where(group == lane_group, by_group[lane_group], chosen)
        return chosen

    for b_high in range(BB // LANE_GROUPS):
        by_c = [
            ladder_ref.at[b_high][pl.ds(c_low, n_rows, stride=LANE_GROUPS), :]
            for c_low in range(LANE_GROUPS)
        ]
        skewed = []
        for turn in range(LANE_GROUPS):
            mixed = pick([by_c[(b_low + turn) % LANE_GROUPS] for b_low in range(LANE_GROUPS)])
            skewed.append(pltpu.roll(mixed, turn * DB, 1) if turn else mixed)
        for b_low in range(LANE_GROUPS):
            b = b_high * LANE_GROUPS + b_low
            by_b = pick([skewed[(c_low - b_low) % LANE_GROUPS] for c_low in range(LANE_GROUPS)])
            for a in range(n_rows // BB):
                at = (a * BB + b) * BB
                turned_ref[at : at + BB, :] = by_b[a * BB : (a + 1) * BB]
    for c_high in range(BB):
        tile = turned_ref[pl.ds(c_high, n_rows, stride=BB), :]
        factor_ref[:, c_high * LANES : (c_high + 1) * LANES] = tile.astype(jnp.bfloat16)
    out_ref[...] = lax.dot_general(
        t2_ref[...],
        factor_ref[...],
        (((1,), (1,)), ((), ())),
        preferred_element_type=jnp.float32,
    )


def combine(parts, t2):
    block_rows, bd_width = parts[0].shape
    pairs, cd_width = t2.shape
    ab_width = block_rows * bd_width // cd_width
    return pl.pallas_call(
        combine_kernel,
        out_shape=jax.ShapeDtypeStruct((pairs, ab_width), jnp.float32),
        in_specs=[VMEM] * 6,
        out_specs=VMEM,
        scratch_shapes=[
            pltpu.VMEM((BB // LANE_GROUPS, block_rows, LANES), jnp.float32),
            pltpu.VMEM((ab_width * BB, LANES), jnp.float32),
            pltpu.VMEM((ab_width, cd_width), jnp.bfloat16),
        ],
        cost_estimate=pl.CostEstimate(
            flops=2 * pairs * ab_width * cd_width, bytes_accessed=3 << 20, transcendentals=0
        ),
    )(*parts, t2)


def along_pb(array, distance):
    n_pb = lax.axis_size("pb")
    return lax.ppermute(array, "pb", [(y, (y + distance) % n_pb) for y in range(n_pb)])


def across_pb(array, distance):
    n_pb = lax.axis_size("pb")
    pairs = []
    for col in range(lax.axis_size("col")):
        way = -distance if col % 2 else distance
        pairs += [(col * n_pb + y, col * n_pb + (y + way) % n_pb) for y in range(n_pb)]
    return lax.ppermute(array, ("col", "pb"), pairs)


def step(b_ac, b_oc, t1, f_bd, t2):
    n_aa = lax.axis_size("aa")
    n_pb = lax.axis_size("pb")
    n_out = lax.axis_size("col") * n_pb
    place = lax.axis_index("pb").astype(jnp.int32).reshape(1)
    core = lax.rem(lax.axis_index("col"), 2).astype(jnp.int32).reshape(1)

    amplitudes = lax.all_to_all(
        jnp.broadcast_to(t2[None], (n_aa, *t2.shape)), "aa", 0, 0, tiled=True
    ).reshape(-1, t2.shape[1])

    correction = jnp.einsum("ka,qkc->qac", t1, b_oc, preferred_element_type=jnp.float32)
    dressed = (b_ac - correction).astype(jnp.bfloat16)
    ladder = jnp.einsum(
        "qac,qn->acn", dressed, f_bd, preferred_element_type=jnp.float32
    ).astype(jnp.bfloat16)
    up, down, across, up2, down2, own = split(ladder, place, n_pb)
    up = along_pb(up, 1)
    down = along_pb(down, -1)
    across = across_pb(across, 2)
    up2, down2 = merge(core, up, down, across, up2, down2)
    up2 = along_pb(up2, 2)
    down2 = along_pb(down2, -2)
    *parts, amplitudes = lax.optimization_barrier((own, up, down, up2, down2, amplitudes))
    sums = combine(parts, amplitudes)
    shares = sums.reshape(n_out, -1, sums.shape[1])
    shares = lax.all_to_all(shares, ("col", "pb"), 0, 0, tiled=True)
    return jnp.sum(shares, axis=0)


def solution(mesh):
    placed = (
        P("pb", "aa", "col"),
        P("pb", None, "col"),
        P(None, "aa"),
        P("pb", None),
        P("aa", ("col", "pb")),
    )
    return jax.shard_map(
        step, mesh=mesh, in_specs=placed, out_specs=P(("col", "pb"), "aa"), check_vma=False
    )
```

time: 111 us -> 108 us (0.973)
  starting transfers between devices: 50.8 us -> 36.9 us
  waiting for transfers between devices: 15 us -> 24.7 us
  Pallas kernels: 3.53 us -> 8.66 us
  blocking collectives: 33.7 us -> 29.5 us
  matrix products: 3.25 us -> 4.59 us
    ppermute x10 -> x5, starting transfers between devices: 42.5 us -> 21 us  [the longest x4 16.9 us: along_pb(): lax.ppermute(array, 'pb', [(y, (y + distance) % n_pb) for y in range(n_pb)])]
    ppermute x10 -> x5, waiting for transfers between devices: 15 us -> 24.7 us  [the longest x1 13.6 us: across_pb(): return lax.ppermute(array, ('col', 'pb'), pairs)]
    all_to_all x1, starting transfers between devices: 8.22 us -> 16 us  [step(): lax.all_to_all(jnp.broadcast_to(t2[None], (n_aa, *t2.shape)), 'aa', 0, 0,...]
    pallas_call x1 -> x3, Pallas kernels: 3.53 us -> 8.66 us  [the longest x1 3.3 us: combine(): pl.pallas_call(combine_kernel, out_shape=jax.ShapeDtypeStruct((pairs, ab_...]
    all_to_all x1, blocking collectives: 33.7 us -> 29.5 us  [step(): shares = lax.all_to_all(shares, ('col', 'pb'), 0, 0, tiled=True)]
    broadcast_in_dim x0 -> x1, local copies, waits for them, and re-layouts: none -> 2.04 us  [step(): jnp.broadcast_to(t2[None], (n_aa, *t2.shape))]
    reshape x1 -> x0, local copies, waits for them, and re-layouts: 1.49 us -> none  [step(): partial = partial.astype(jnp.bfloat16).reshape(a_width, n_pb, c_block, BB...]
    dot_general x1, matrix products: 1.27 us -> 2.6 us  [step(): jnp.einsum('qac,qn->acn', dressed, f_bd, preferred_element_type=jnp.float32)]
  transfers between devices with their start and end apart: 11 -> 6, of which waited for: 6 -> 3; matrix products, arithmetic and copies ran while one was open for 0% -> 4% of each run, Pallas kernels for 0% -> 5%
where the time goes in v2:
time: 108 us
  starting transfers between devices  36.9 us (34%)
  blocking collectives  29.5 us (27%)
  waiting for transfers between devices  24.7 us (23%)
  Pallas kernels  8.66 us (8%)
  matrix products  4.59 us (4%)
  local copies, waits for them, and re-layouts  2.75 us (3%)
    all_to_all x1, blocking collectives, step(): shares = lax.all_to_all(shares, ('col', 'pb'), 0, 0, tiled=True)  29.5 us
    ppermute x4, starting transfers between devices, along_pb(): lax.ppermute(array, 'pb', [(y, (y + distance) % n_pb) for y in range(n_pb)])  16.9 us
    all_to_all x1, starting transfers between devices, step(): lax.all_to_all(jnp.broadcast_to(t2[None], (n_aa, *t2.shape)), 'aa', 0, 0,...  16 us
    ppermute x1, waiting for transfers between devices, across_pb(): return lax.ppermute(array, ('col', 'pb'), pairs)  13.6 us
    ppermute x4, waiting for transfers between devices, along_pb(): lax.ppermute(array, 'pb', [(y, (y + distance) % n_pb) for y in range(n_pb)])  11.1 us
    ppermute x1, starting transfers between devices, across_pb(): return lax.ppermute(array, ('col', 'pb'), pairs)  4.03 us
    pallas_call x1, Pallas kernels, combine(): pl.pallas_call(combine_kernel, out_shape=jax.ShapeDtypeStruct((pairs, ab_...  3.3 us
    pallas_call x1, Pallas kernels, split(): pl.pallas_call(split_kernel, out_shape=[jax.ShapeDtypeStruct(shape, ladde...  3.02 us
  transfers between devices with their start and end apart: 6, of which 3 were waited for; matrix products, arithmetic and copies ran while one was open for 4% of the time, Pallas kernels for 5%

profile of v2, /device:TPU:1, one launch (start us, length us, event | category | flops | bytes accessed | tf_op | source)
XLA Modules:
  0.0 107.9 jit_solution(1606032526576235970)
XLA Ops:
  0.0 0.0 copy-start
  0.0 0.0 copy-start.3
  0.0 2.0 %broadcast_in_dim.2 = bf16[32,16,1024]{2,1,0:T(8,128)(2,1)} broadcast(bf16[16,1024]{1,0:T(8,128)(2,1)} %param.9), dimensions={1,2} | broadcast | bytes 1081344 | tf_op jit(solution)/shard_map/broadcast_in_dim | solution.py:158
  2.0 16.0 %all-to-all-start = ((bf16[32,16,1024]{2,1,0:T(8,128)(2,1)}), bf16[32,16,1024]{2,1,0:T(8,128)(2,1)}, u32[]{:S(2)}, u32[]{:S(2)}) async-start(bf16[32,16,1024]{2,1,0:T(8,128)(2,1)} %broadcast_in_dim.2), calls=%async_computation | async-start | bytes 2097152 | tf_op jit(solution)/shard_map/all_to_all | solution.py:157
  18.0 0.0 copy-done
  18.0 0.0 copy-done.3
  18.0 0.0 copy-start.4
  18.1 2.0 %fusion = bf16[192,16,256]{2,1,0:T(8,128)(2,1)S(1)} fusion(bf16[192,16,256]{2,1,0:T(8,128)(2,1)} %param.5, bf16[192,32,256]{2,1,0:T(8,128)(2,1)S(1)} %copy-done, bf16[32,16]{0,1:T(8,128)(2,1)S(1)} %copy-done.3), kind=kOutput, calls=%fused_computation.1 | convolution fusion | flops 52690944 | bytes 6292480 | tf_op jit(solution)/shard_map/ka,qkc->qac/dot_general | solution.py:161
  20.1 0.0 copy-done.4
  20.1 2.6 %convolution_convert_fusion.ladder_ref = bf16[16,256,256]{2,1,0:T(8,128)(2,1)} fusion(bf16[192,16,256]{2,1,0:T(8,128)(2,1)S(1)} %fusion, bf16[192,256]{1,0:T(8,128)(2,1)S(1)} %copy-done.4), kind=kOutput, calls=%fused_computation.2 | convolution fusion | flops 403701760 | bytes 3768320 | tf_op jit(solution)/shard_map/qac,qn->acn/dot_general | solution.py:163
  22.7 3.0 %shard_map.55 = (bf16[2,512,256]{2,1,0:T(8,128)(2,1)}, bf16[2,512,256]{2,1,0:T(8,128)(2,1)}, bf16[512,256]{1,0:T(8,128)(2,1)}, bf16[512,256]{1,0:T(8,128)(2,1)},...) custom-call(s32[1]{0:T(128)} %bitcast.place_ref, bf16[16,256,256]{2,1,0:T(8,128)(2,1)} %convolution_convert_fusion.ladder_ref), custom_call_target="tpu_custom_call" | custom-call | bytes 4194304 | tf_op jit(solution)/shard_map/pallas_call | solution.py:40
  25.7 3.3 %collective-permute-start = (bf16[2,512,256]{2,1,0:T(8,128)(2,1)}, bf16[2,512,256]{2,1,0:T(8,128)(2,1)}, u32[]{:S(2)}, u32[]{:S(2)}) collective-permute-start(bf16[2,512,256]{2,1,0:T(8,128)(2,1)} %get-tuple-element.20), channel_id=1, source_target_pairs={{0,1},{1,2},{2,3},{3,4},{4,5},{5,6},{6,7},{7,0},{8,9},{9,10},{10,1... | collective-permute-start | bytes 1572872 | tf_op jit(solution)/shard_map/ppermute | solution.py:138
  29.0 4.5 %collective-permute-start.1 = (bf16[2,512,256]{2,1,0:T(8,128)(2,1)}, bf16[2,512,256]{2,1,0:T(8,128)(2,1)}, u32[]{:S(2)}, u32[]{:S(2)}) collective-permute-start(bf16[2,512,256]{2,1,0:T(8,128)(2,1)} %get-tuple-element.21), channel_id=1, source_target_pairs={{0,7},{1,0},{2,1},{3,2},{4,3},{5,4},{6,5},{7,6},{8,15},{9,8},{10,9... | collective-permute-start | bytes 1572872 | tf_op jit(solution)/shard_map/ppermute | solution.py:138
  33.5 4.0 %collective-permute-start.2 = (bf16[512,256]{1,0:T(8,128)(2,1)}, bf16[512,256]{1,0:T(8,128)(2,1)S(1)}, u32[]{:S(2)}, u32[]{:S(2)}) collective-permute-start(bf16[512,256]{1,0:T(8,128)(2,1)} %get-tuple-element.22), channel_id=1, source_target_pairs={{0,2},{1,3},{2,4},{3,5},{4,6},{5,7},{6,0},{7,1},{8,14},{9,15},{10,... | collective-permute-start | bytes 786440 | tf_op jit(solution)/shard_map/ppermute | solution.py:147
  37.6 13.6 %collective-permute-done.2.across_ref = bf16[512,256]{1,0:T(8,128)(2,1)S(1)} collective-permute-done((bf16[512,256]{1,0:T(8,128)(2,1)}, bf16[512,256]{1,0:T(8,128)(2,1)S(1)}, u32[]{:S(2)}, u32[]{:S(2)}) %collective-permute-start.2) | collective-permute-done | bytes 262176 | tf_op jit(solution)/shard_map/ppermute | solution.py:147
  51.2 0.0 copy-start.2
  51.2 0.0 collective-permute-done.up_ref
  51.2 0.0 collective-permute-done.1.down_ref
  51.2 0.7 copy-done.2
  51.9 2.3 %shard_map.56 = (bf16[512,256]{1,0:T(8,128)(2,1)}, bf16[512,256]{1,0:T(8,128)(2,1)}) custom-call(s32[1]{0:T(128)} %bitcast.4.core_ref, bf16[2,512,256]{2,1,0:T(8,128)(2,1)} %collective-permute-done.up_ref, bf16[2,512,256]{2,1,0:T(8,128)(2,1)} %collective-permute-done.1.down_ref, bf16[512,256]{1,0:T(8,128)(2,1)} %copy-done.2, ...), custom_call_target="tpu_custom_call" | custom-call | flops 524288 | bytes 2097152 | tf_op jit(solution)/shard_map/pallas_call | solution.py:62
  54.2 7.2 %collective-permute-start.3 = (bf16[512,256]{1,0:T(8,128)(2,1)}, bf16[512,256]{1,0:T(8,128)(2,1)S(1)}, u32[]{:S(2)}, u32[]{:S(2)}) collective-permute-start(bf16[512,256]{1,0:T(8,128)(2,1)} %get-tuple-element.25), channel_id=1, source_target_pairs={{0,2},{1,3},{2,4},{3,5},{4,6},{5,7},{6,0},{7,1},{8,10},{9,11},{10,... | collective-permute-start | bytes 786440 | tf_op jit(solution)/shard_map/ppermute | solution.py:138
  61.4 1.9 %collective-permute-start.4 = (bf16[512,256]{1,0:T(8,128)(2,1)}, bf16[512,256]{1,0:T(8,128)(2,1)}, u32[]{:S(2)}, u32[]{:S(2)}) collective-permute-start(bf16[512,256]{1,0:T(8,128)(2,1)} %get-tuple-element.26), channel_id=1, source_target_pairs={{0,6},{1,7},{2,0},{3,1},{4,2},{5,3},{6,4},{7,5},{8,14},{9,15},{10,... | collective-permute-start | bytes 786440 | tf_op jit(solution)/shard_map/ppermute | solution.py:138
  63.3 8.1 %collective-permute-done.3.up2_ref = bf16[512,256]{1,0:T(8,128)(2,1)S(1)} collective-permute-done((bf16[512,256]{1,0:T(8,128)(2,1)}, bf16[512,256]{1,0:T(8,128)(2,1)S(1)}, u32[]{:S(2)}, u32[]{:S(2)}) %collective-permute-start.3) | collective-permute-done | bytes 262176 | tf_op jit(solution)/shard_map/ppermute | solution.py:138
  71.5 0.0 copy-start.1
  71.5 2.9 %collective-permute-done.4.down2_ref = bf16[512,256]{1,0:T(8,128)(2,1)} collective-permute-done((bf16[512,256]{1,0:T(8,128)(2,1)}, bf16[512,256]{1,0:T(8,128)(2,1)}, u32[]{:S(2)}, u32[]{:S(2)}) %collective-permute-start.4) | collective-permute-done | bytes 262176 | tf_op jit(solution)/shard_map/ppermute | solution.py:138
  74.4 0.0 all-to-all-done
  74.4 0.0 copy-done.1
  74.4 3.3 %shard_map.57 = f32[512,128]{1,0:T(8,128)} custom-call(bf16[512,256]{1,0:T(8,128)(2,1)} %get-tuple-element.27.own_ref, bf16[2,512,256]{2,1,0:T(8,128)(2,1)} %collective-permute-done.up_ref, bf16[2,512,256]{2,1,0:T(8,128)(2,1)} %collective-permute-done.1.down_ref, bf16[512,256]{1,0:T(8,128)(2,1)} %copy-done.1, ...), custom_call_target="tpu_custom_call" | custom-call | flops 134217728 | bytes 3145728 | tf_op jit(solution)/shard_map/pallas_call | solution.py:120
  77.7 29.5 %all_to_all.10 = f32[32,16,128]{2,1,0:T(8,128)S(1)} all-to-all(f32[32,16,128]{2,1,0:T(8,128)} %bitcast.15), channel_id=1, replica_groups=mesh['aa'=32,'col'=4,'pb'=8] {'col','pb'}, dimensions={0} | all-to-all | bytes 524288 | tf_op jit(solution)/shard_map/all_to_all | solution.py:176
  107.3 0.6 reduce_sum.9
Async XLA Ops:
  0.0 18.0 %copy-start = (bf16[192,32,256]{2,1,0:T(8,128)(2,1)S(1)}, bf16[192,32,256]{2,1,0:T(8,128)(2,1)}, u32[]{:S(2)}) copy-start(bf16[192,32,256]{2,1,0:T(8,128)(2,1)} %param.6) | copy-start | bytes 9437188
  0.0 18.0 %copy-start.3 = (bf16[32,16]{0,1:T(8,128)(2,1)S(1)}, bf16[32,16]{0,1:T(8,128)(2,1)}, u32[]{:S(2)}) copy-start(bf16[32,16]{0,1:T(8,128)(2,1)} %param.7) | copy-start | bytes 3076
  2.0 72.4 %all-to-all-start = ((bf16[32,16,1024]{2,1,0:T(8,128)(2,1)}), bf16[32,16,1024]{2,1,0:T(8,128)(2,1)}, u32[]{:S(2)}, u32[]{:S(2)}) async-start(bf16[32,16,1024]{2,1,0:T(8,128)(2,1)} %broadcast_in_dim.2), calls=%async_computation | async-start | bytes 2097152 | tf_op jit(solution)/shard_map/all_to_all | solution.py:157
  18.0 2.0 %copy-start.4 = (bf16[192,256]{1,0:T(8,128)(2,1)S(1)}, bf16[192,256]{1,0:T(8,128)(2,1)}, u32[]{:S(2)}) copy-start(bf16[192,256]{1,0:T(8,128)(2,1)} %param.8) | copy-start | bytes 294916
  25.7 25.5 %collective-permute-start = (bf16[2,512,256]{2,1,0:T(8,128)(2,1)}, bf16[2,512,256]{2,1,0:T(8,128)(2,1)}, u32[]{:S(2)}, u32[]{:S(2)}) collective-permute-start(bf16[2,512,256]{2,1,0:T(8,128)(2,1)} %get-tuple-element.20), channel_id=1, source_target_pairs={{0,1},{1,2},{2,3},{3,4},{4,5},{5,6},{6,7},{7,0},{8,9},{9,10},{10,1... | collective-permute-start | bytes 1572872 | tf_op jit(solution)/shard_map/ppermute | solution.py:138
  29.0 22.2 %collective-permute-start.1 = (bf16[2,512,256]{2,1,0:T(8,128)(2,1)}, bf16[2,512,256]{2,1,0:T(8,128)(2,1)}, u32[]{:S(2)}, u32[]{:S(2)}) collective-permute-start(bf16[2,512,256]{2,1,0:T(8,128)(2,1)} %get-tuple-element.21), channel_id=1, source_target_pairs={{0,7},{1,0},{2,1},{3,2},{4,3},{5,4},{6,5},{7,6},{8,15},{9,8},{10,9... | collective-permute-start | bytes 1572872 | tf_op jit(solution)/shard_map/ppermute | solution.py:138
  33.5 17.7 %collective-permute-start.2 = (bf16[512,256]{1,0:T(8,128)(2,1)}, bf16[512,256]{1,0:T(8,128)(2,1)S(1)}, u32[]{:S(2)}, u32[]{:S(2)}) collective-permute-start(bf16[512,256]{1,0:T(8,128)(2,1)} %get-tuple-element.22), channel_id=1, source_target_pairs={{0,2},{1,3},{2,4},{3,5},{4,6},{5,7},{6,0},{7,1},{8,14},{9,15},{10,... | collective-permute-start | bytes 786440 | tf_op jit(solution)/shard_map/ppermute | solution.py:147
  51.2 0.7 copy-start.2
  54.2 17.3 %collective-permute-start.3 = (bf16[512,256]{1,0:T(8,128)(2,1)}, bf16[512,256]{1,0:T(8,128)(2,1)S(1)}, u32[]{:S(2)}, u32[]{:S(2)}) collective-permute-start(bf16[512,256]{1,0:T(8,128)(2,1)} %get-tuple-element.25), channel_id=1, source_target_pairs={{0,2},{1,3},{2,4},{3,5},{4,6},{5,7},{6,0},{7,1},{8,10},{9,11},{10,... | collective-permute-start | bytes 786440 | tf_op jit(solution)/shard_map/ppermute | solution.py:138
  61.4 13.0 %collective-permute-start.4 = (bf16[512,256]{1,0:T(8,128)(2,1)}, bf16[512,256]{1,0:T(8,128)(2,1)}, u32[]{:S(2)}, u32[]{:S(2)}) collective-permute-start(bf16[512,256]{1,0:T(8,128)(2,1)} %get-tuple-element.26), channel_id=1, source_target_pairs={{0,6},{1,7},{2,0},{3,1},{4,2},{5,3},{6,4},{7,5},{8,14},{9,15},{10,... | collective-permute-start | bytes 786440 | tf_op jit(solution)/shard_map/ppermute | solution.py:138
  71.5 2.9 %copy-start.1 = (bf16[512,256]{1,0:T(8,128)(2,1)}, bf16[512,256]{1,0:T(8,128)(2,1)S(1)}, u32[]{:S(2)}) copy-start(bf16[512,256]{1,0:T(8,128)(2,1)S(1)} %collective-permute-done.3.up2_ref) | copy-start | bytes 786436

commit v3 on v2

--- a/solution.py
+++ b/solution.py
@@ -10,40 +10,87 @@
 DB = 32
 LANES = 128
 LANE_GROUPS = LANES // DB
+Q_GROUP = 8
+Q_STEPS = 4
 VMEM = pl.BlockSpec(memory_space=pltpu.VMEM)
 SMEM = pl.BlockSpec(memory_space=pltpu.SMEM)
 
 
-def split_kernel(place_ref, ladder_ref, up_ref, down_ref, across_ref, up2_ref, down2_ref, own_ref):
-    a_width, c_width, _ = ladder_ref.shape
-    c_block = own_ref.shape[0] // a_width
-    n_pb = c_width // c_block
-    for distance, out_ref in (
-        (1, up_ref.at[0]),
-        (3, up_ref.at[1]),
-        (n_pb - 1, down_ref.at[0]),
-        (n_pb - 3, down_ref.at[1]),
-        (4, across_ref),
-        (2, up2_ref),
-        (n_pb - 2, down2_ref),
-        (0, own_ref),
-    ):
-        c_at = pl.multiple_of(lax.rem(place_ref[0] + distance, n_pb) * c_block, c_block)
-        for a in range(a_width):
-            out_ref[a * c_block : (a + 1) * c_block, :] = ladder_ref[a, pl.ds(c_at, c_block), :]
-
-
-def split(ladder, place, n_pb):
-    a_width, c_width, bd_width = ladder.shape
+def contract_kernel(place_ref, b_ac_ref, b_oc_ref, singles_ref, f_ref, *refs):
+    out_refs, (dressed_ref, ladder_ref, sems) = refs[:-3], refs[-3:]
+    n_q, a_width, c_width = b_ac_ref.shape
+    n_total = dressed_ref.shape[1] // a_width
+    n_pb, block_rows, _ = ladder_ref.shape
+    c_block = block_rows // a_width
+    size = Q_GROUP * a_width
+    step = pl.program_id(0)
+    for group in range(n_q // Q_GROUP):
+        rows = slice(group * Q_GROUP, (group + 1) * Q_GROUP)
+        occupied = b_oc_ref[rows].reshape(-1, c_width)
+        correction = jnp.dot(singles_ref[...], occupied, preferred_element_type=jnp.float32)
+        block = b_ac_ref[rows].reshape(size, c_width).astype(jnp.float32)
+        dressed = (block - correction).astype(jnp.bfloat16).astype(jnp.float32)
+        at = pl.ds(pl.multiple_of((step * (n_q // Q_GROUP) + group) * size, size), size)
+        for half in range(c_width // LANES):
+            dressed_ref[half, at, :] = dressed[:, half * LANES : (half + 1) * LANES]
+
+    @pl.when(step == pl.num_programs(0) - 1)
+    def _():
+        factors = f_ref[...]
+        for half in range(c_width // LANES):
+            for a in range(a_width):
+                slab = dressed_ref.at[half][pl.ds(a, n_total, stride=a_width), :]
+                part = lax.dot_general(
+                    slab.astype(jnp.bfloat16),
+                    factors,
+                    (((0,), (0,)), ((), ())),
+                    preferred_element_type=jnp.float32,
+                ).astype(ladder_ref.dtype)
+                for c_at in range(0, LANES, c_block):
+                    ladder_ref[(half * LANES + c_at) // c_block, a * c_block : (a + 1) * c_block, :] = (
+                        part[c_at : c_at + c_block]
+                    )
+        copies = [
+            pltpu.make_async_copy(
+                ladder_ref.at[lax.rem(place_ref[0] + distance, n_pb)], out_ref, sems.at[distance]
+            )
+            for distance, out_ref in enumerate(out_refs)
+        ]
+        for copy in copies:
+            copy.start()
+        for copy in copies:
+            copy.wait()
+
+
+def contract(b_ac, b_oc, t1, f_bd, place, n_pb):
+    n_q, a_width, c_width = b_ac.shape
+    n_occ = b_oc.shape[1]
+    bd_width = f_bd.shape[1]
     block = (a_width * c_width // n_pb, bd_width)
-    shapes = [(2, *block)] * 2 + [block] * 4
+    eye = jnp.eye(Q_GROUP, dtype=t1.dtype)
+    singles = jnp.einsum("qr,ka->qark", eye, t1).reshape(Q_GROUP * a_width, Q_GROUP * n_occ)
+    q_step = n_q // Q_STEPS
     return pl.pallas_call(
-        split_kernel,
-        out_shape=[jax.ShapeDtypeStruct(shape, ladder.dtype) for shape in shapes],
-        in_specs=[SMEM, VMEM],
-        out_specs=[VMEM] * 6,
-        cost_estimate=pl.CostEstimate(flops=0, bytes_accessed=4 << 20, transcendentals=0),
-    )(place, ladder)
+        contract_kernel,
+        grid=(Q_STEPS,),
+        out_shape=[jax.ShapeDtypeStruct(block, jnp.bfloat16)] * n_pb,
+        in_specs=[
+            SMEM,
+            pl.BlockSpec((q_step, a_width, c_width), lambda step: (step, 0, 0)),
+            pl.BlockSpec((q_step, n_occ, c_width), lambda step: (step, 0, 0)),
+            pl.BlockSpec(singles.shape, lambda step: (0, 0)),
+            pl.BlockSpec(f_bd.shape, lambda step: (0, 0)),
+        ],
+        out_specs=[pl.BlockSpec(memory_space=pl.ANY)] * n_pb,
+        scratch_shapes=[
+            pltpu.VMEM((c_width // LANES, n_q * a_width, LANES), jnp.float32),
+            pltpu.VMEM((n_pb, *block), jnp.bfloat16),
+            pltpu.SemaphoreType.DMA((n_pb,)),
+        ],
+        cost_estimate=pl.CostEstimate(
+            flops=2 * n_q * a_width * c_width * bd_width, bytes_accessed=7 << 20, transcendentals=0
+        ),
+    )(place, b_ac, b_oc, singles, f_bd)
 
 
 def merge_kernel(core_ref, up_ref, down_ref, across_ref, up2_ref, down2_ref, up_out, down_out):
@@ -53,7 +100,7 @@
         (0, up_ref, up2_ref, up_out),
         (1, down_ref, down2_ref, down_out),
     ):
-        total = own_ref[...].astype(jnp.float32) + passing_ref[1].astype(jnp.float32)
+        total = own_ref[...].astype(jnp.float32) + passing_ref[...].astype(jnp.float32)
         total += jnp.where(core_ref[0] == core, across, zero)
         out_ref[...] = total.astype(out_ref.dtype)
 
@@ -72,8 +119,8 @@
     own_ref, up_ref, down_ref, up2_ref, down2_ref, t2_ref, out_ref, ladder_ref, turned_ref, factor_ref
 ):
     total = own_ref[...].astype(jnp.float32)
-    total += up_ref[0].astype(jnp.float32)
-    total += down_ref[0].astype(jnp.float32)
+    total += up_ref[...].astype(jnp.float32)
+    total += down_ref[...].astype(jnp.float32)
     total += up2_ref[...].astype(jnp.float32)
     total += down2_ref[...].astype(jnp.float32)
     for b_high in range(BB // LANE_GROUPS):
@@ -158,19 +205,16 @@
         jnp.broadcast_to(t2[None], (n_aa, *t2.shape)), "aa", 0, 0, tiled=True
     ).reshape(-1, t2.shape[1])
 
-    correction = jnp.einsum("ka,qkc->qac", t1, b_oc, preferred_element_type=jnp.float32)
-    dressed = (b_ac - correction).astype(jnp.bfloat16)
-    ladder = jnp.einsum(
-        "qac,qn->acn", dressed, f_bd, preferred_element_type=jnp.float32
-    ).astype(jnp.bfloat16)
-    up, down, across, up2, down2, own = split(ladder, place, n_pb)
-    up = along_pb(up, 1)
-    down = along_pb(down, -1)
+    own, up1, up2, up3, across, down3, down2, down1 = contract(b_ac, b_oc, t1, f_bd, place, n_pb)
     across = across_pb(across, 2)
-    up2, down2 = merge(core, up, down, across, up2, down2)
+    up3 = along_pb(up3, 1)
+    down3 = along_pb(down3, -1)
+    up1 = along_pb(up1, 1)
+    down1 = along_pb(down1, -1)
+    up2, down2 = merge(core, up3, down3, across, up2, down2)
     up2 = along_pb(up2, 2)
     down2 = along_pb(down2, -2)
-    *parts, amplitudes = lax.optimization_barrier((own, up, down, up2, down2, amplitudes))
+    *parts, amplitudes = lax.optimization_barrier((own, up1, down1, up2, down2, amplitudes))
     sums = combine(parts, amplitudes)
     shares = sums.reshape(n_out, -1, sums.shape[1])
     shares = lax.all_to_all(shares, ("col", "pb"), 0, 0, tiled=True)

time: 108 us -> 105 us (0.972)
  the two profiles are of different devices: /device:TPU:1 before, /device:TPU:21 now
where the time goes in v3:
time: 105 us; the launch traced here: 104 us
  starting transfers between devices  38.6 us (37%)
  blocking collectives  36.1 us (34%)
  waiting for transfers between devices  12 us (11%)
  Pallas kernels  11.7 us (11%)
  local copies, waits for them, and re-layouts  4.58 us (4%)
    all_to_all x1, blocking collectives, step(): shares = lax.all_to_all(shares, ('col', 'pb'), 0, 0, tiled=True)  36.1 us
    ppermute x6, starting transfers between devices, along_pb(): lax.ppermute(array, 'pb', [(y, (y + distance) % n_pb) for y in range(n_pb)])  17.9 us
    all_to_all x1, starting transfers between devices, step(): lax.all_to_all(jnp.broadcast_to(t2[None], (n_aa, *t2.shape)), 'aa', 0, 0,...  15 us
    ppermute x6, waiting for transfers between devices, along_pb(): lax.ppermute(array, 'pb', [(y, (y + distance) % n_pb) for y in range(n_pb)])  8.63 us
    pallas_call x1, Pallas kernels, contract(): pl.pallas_call(contract_kernel, grid=(Q_STEPS,), out_shape=[jax.ShapeDtyp...  6.38 us
    ppermute x1, starting transfers between devices, across_pb(): return lax.ppermute(array, ('col', 'pb'), pairs)  5.68 us
    ppermute x1, waiting for transfers between devices, across_pb(): return lax.ppermute(array, ('col', 'pb'), pairs)  3.36 us
    pallas_call x1, Pallas kernels, combine(): pl.pallas_call(combine_kernel, out_shape=jax.ShapeDtypeStruct((pairs, ab_...  3.15 us
  transfers between devices with their start and end apart: 8, of which 2 were waited for; matrix products, arithmetic and copies ran while one was open for 1% of the time, Pallas kernels for 8%

profile of v3, /device:TPU:21, one launch (start us, length us, event | category | flops | bytes accessed | tf_op | source)
XLA Modules:
  0.0 103.9 jit_solution(7973740012090317336)
XLA Ops:
  0.0 1.9 %broadcast_in_dim.2 = bf16[32,16,1024]{2,1,0:T(8,128)(2,1)} broadcast(bf16[16,1024]{1,0:T(8,128)(2,1)} %param.9), dimensions={1,2} | broadcast | bytes 1081344 | tf_op jit(solution)/shard_map/broadcast_in_dim | solution.py:205
  1.9 15.0 %all-to-all-start = ((bf16[32,16,1024]{2,1,0:T(8,128)(2,1)}), bf16[32,16,1024]{2,1,0:T(8,128)(2,1)S(1)}, u32[]{:S(2)}, u32[]{:S(2)}) async-start(bf16[32,16,1024]{2,1,0:T(8,128)(2,1)} %broadcast_in_dim.2), calls=%async_computation | async-start | bytes 2097152 | tf_op jit(solution)/shard_map/all_to_all | solution.py:204
  16.9 0.0 copy-done.8
  16.9 0.1 multiply_bitcast_fusion
  17.0 0.8 reshape.17.singles_ref
  17.9 6.4 %shard_map.55 = (bf16[512,256]{1,0:T(8,128)(2,1)}, bf16[512,256]{1,0:T(8,128)(2,1)}, bf16[512,256]{1,0:T(8,128)(2,1)}, bf16[512,256]{1,0:T(8,128)(2,1)}, bf16[51...) custom-call(s32[1]{0:T(128)} %bitcast.place_ref, ...), custom_call_target="tpu_custom_call" | custom-call | flops 402653184 | bytes 7340032 | tf_op jit(solution)/shard_map/pallas_call | solution.py:73
  24.3 3.3 %collective-permute-start.2 = (bf16[512,256]{1,0:T(8,128)(2,1)}, bf16[512,256]{1,0:T(8,128)(2,1)S(1)}, u32[]{:S(2)}, u32[]{:S(2)}) collective-permute-start(bf16[512,256]{1,0:T(8,128)(2,1)} %get-tuple-element.24), channel_id=1, source_target_pairs={{0,1},{1,2},{2,3},{3,4},{4,5},{5,6},{6,7},{7,0},{8,9},{9,10},{10,1... | collective-permute-start | bytes 786440 | tf_op jit(solution)/shard_map/ppermute | solution.py:185
  27.6 1.9 %collective-permute-start.3 = (bf16[512,256]{1,0:T(8,128)(2,1)}, bf16[512,256]{1,0:T(8,128)(2,1)S(1)}, u32[]{:S(2)}, u32[]{:S(2)}) collective-permute-start(bf16[512,256]{1,0:T(8,128)(2,1)} %get-tuple-element.25), channel_id=1, source_target_pairs={{0,7},{1,0},{2,1},{3,2},{4,3},{5,4},{6,5},{7,6},{8,15},{9,8},{10,9... | collective-permute-start | bytes 786440 | tf_op jit(solution)/shard_map/ppermute | solution.py:185
  29.6 5.7 %collective-permute-start.4 = (bf16[512,256]{1,0:T(8,128)(2,1)}, bf16[512,256]{1,0:T(8,128)(2,1)S(1)}, u32[]{:S(2)}, u32[]{:S(2)}) collective-permute-start(bf16[512,256]{1,0:T(8,128)(2,1)} %get-tuple-element.26), channel_id=1, source_target_pairs={{0,2},{1,3},{2,4},{3,5},{4,6},{5,7},{6,0},{7,1},{8,14},{9,15},{10,... | collective-permute-start | bytes 786440 | tf_op jit(solution)/shard_map/ppermute | solution.py:194
  35.2 1.9 %collective-permute-start = (bf16[512,256]{1,0:T(8,128)(2,1)}, bf16[512,256]{1,0:T(8,128)(2,1)S(1)}, u32[]{:S(2)}, u32[]{:S(2)}) collective-permute-start(bf16[512,256]{1,0:T(8,128)(2,1)} %get-tuple-element.22), channel_id=1, source_target_pairs={{0,1},{1,2},{2,3},{3,4},{4,5},{5,6},{6,7},{7,0},{8,9},{9,10},{10,1... | collective-permute-start | bytes 786440 | tf_op jit(solution)/shard_map/ppermute | solution.py:185
  37.2 3.4 %collective-permute-start.1 = (bf16[512,256]{1,0:T(8,128)(2,1)}, bf16[512,256]{1,0:T(8,128)(2,1)S(1)}, u32[]{:S(2)}, u32[]{:S(2)}) collective-permute-start(bf16[512,256]{1,0:T(8,128)(2,1)} %get-tuple-element.23), channel_id=1, source_target_pairs={{0,7},{1,0},{2,1},{3,2},{4,3},{5,4},{6,5},{7,6},{8,15},{9,8},{10,9... | collective-permute-start | bytes 786440 | tf_op jit(solution)/shard_map/ppermute | solution.py:185
  40.5 0.0 collective-permute-done.2.up_ref
  40.6 0.0 copy-start.3
  40.6 0.0 collective-permute-done.3.down_ref
  40.6 0.0 copy-start.4
  40.6 3.4 %collective-permute-done.4.across_ref = bf16[512,256]{1,0:T(8,128)(2,1)S(1)} collective-permute-done((bf16[512,256]{1,0:T(8,128)(2,1)}, bf16[512,256]{1,0:T(8,128)(2,1)S(1)}, u32[]{:S(2)}, u32[]{:S(2)}) %collective-permute-start.4) | collective-permute-done | bytes 262176 | tf_op jit(solution)/shard_map/ppermute | solution.py:194
  44.0 0.0 copy-done.4
  44.0 0.7 copy-done.5
  44.6 2.2 %shard_map.56 = (bf16[512,256]{1,0:T(8,128)(2,1)}, bf16[512,256]{1,0:T(8,128)(2,1)}) custom-call(s32[1]{0:T(128)} %bitcast.2.core_ref, bf16[512,256]{1,0:T(8,128)(2,1)} %copy-done.3, bf16[512,256]{1,0:T(8,128)(2,1)} %copy-done.4, bf16[512,256]{1,0:T(8,128)(2,1)} %copy-done.5, bf16[512,256]{1,0:T(8,128)(2,1)} %get-tuple-element.27.up2_ref, ...), custom_call_target="tpu_custom_call" | custom-call | flops 524288 | bytes 2097152 | tf_op jit(solution)/shard_map/pallas_call | solution.py:109
  46.8 4.0 %collective-permute-start.5 = (bf16[512,256]{1,0:T(8,128)(2,1)}, bf16[512,256]{1,0:T(8,128)(2,1)S(1)}, u32[]{:S(2)}, u32[]{:S(2)}) collective-permute-start(bf16[512,256]{1,0:T(8,128)(2,1)} %get-tuple-element.29), channel_id=1, source_target_pairs={{0,2},{1,3},{2,4},{3,5},{4,6},{5,7},{6,0},{7,1},{8,10},{9,11},{10,... | collective-permute-start | bytes 786440 | tf_op jit(solution)/shard_map/ppermute | solution.py:185
  50.8 3.4 %collective-permute-start.6 = (bf16[512,256]{1,0:T(8,128)(2,1)}, bf16[512,256]{1,0:T(8,128)(2,1)S(1)}, u32[]{:S(2)}, u32[]{:S(2)}) collective-permute-start(bf16[512,256]{1,0:T(8,128)(2,1)} %get-tuple-element.30), channel_id=1, source_target_pairs={{0,6},{1,7},{2,0},{3,1},{4,2},{5,3},{6,4},{7,5},{8,14},{9,15},{10,... | collective-permute-start | bytes 786440 | tf_op jit(solution)/shard_map/ppermute | solution.py:185
  54.2 0.0 collective-permute-done.up_ref
  54.3 0.0 collective-permute-done.1.down_ref
  54.3 8.6 %collective-permute-done.5.up2_ref = bf16[512,256]{1,0:T(8,128)(2,1)S(1)} collective-permute-done((bf16[512,256]{1,0:T(8,128)(2,1)}, bf16[512,256]{1,0:T(8,128)(2,1)S(1)}, u32[]{:S(2)}, u32[]{:S(2)}) %collective-permute-start.5) | collective-permute-done | bytes 262176 | tf_op jit(solution)/shard_map/ppermute | solution.py:185
  62.9 0.0 collective-permute-done.6.down2_ref
  62.9 0.0 all-to-all-done
  62.9 0.7 copy-done.6
  63.6 0.1 copy-done.7
  63.7 0.4 copy-done
  64.1 3.1 %shard_map.57 = f32[512,128]{1,0:T(8,128)} custom-call(bf16[512,256]{1,0:T(8,128)(2,1)} %get-tuple-element.31.own_ref, bf16[512,256]{1,0:T(8,128)(2,1)} %copy-done.1, bf16[512,256]{1,0:T(8,128)(2,1)} %copy-done.2, bf16[512,256]{1,0:T(8,128)(2,1)} %copy-done.6, bf16[512,256]{1,0:T(8,128)(2,1)} %copy-done.7, bf16[512,1024]{1,0:T(8,128)(2,1)} %bitcast.8), custom_call_target="tpu_custom_call" | custom-call | flops 134217728 | bytes 3145728 | tf_op jit(solution)/shard_map/pallas_call | solution.py:167
  67.2 36.1 %all_to_all.10 = f32[32,16,128]{2,1,0:T(8,128)S(1)} all-to-all(f32[32,16,128]{2,1,0:T(8,128)} %bitcast.9), channel_id=1, replica_groups=mesh['aa'=32,'col'=4,'pb'=8] {'col','pb'}, dimensions={0} | all-to-all | bytes 524288 | tf_op jit(solution)/shard_map/all_to_all | solution.py:220
  103.3 0.6 reduce_sum.9
  (11 shorter events, 0.0 us)
Async XLA Ops:
  0.0 16.9 %copy-start.8 = (bf16[32,16]{0,1:T(8,128)(2,1)S(1)}, bf16[32,16]{0,1:T(8,128)(2,1)}, u32[]{:S(2)}) copy-start(bf16[32,16]{0,1:T(8,128)(2,1)} %param.7) | copy-start | bytes 3076
  1.9 61.0 %all-to-all-start = ((bf16[32,16,1024]{2,1,0:T(8,128)(2,1)}), bf16[32,16,1024]{2,1,0:T(8,128)(2,1)S(1)}, u32[]{:S(2)}, u32[]{:S(2)}) async-start(bf16[32,16,1024]{2,1,0:T(8,128)(2,1)} %broadcast_in_dim.2), calls=%async_computation | async-start | bytes 2097152 | tf_op jit(solution)/shard_map/all_to_all | solution.py:204
  24.3 16.3 %collective-permute-start.2 = (bf16[512,256]{1,0:T(8,128)(2,1)}, bf16[512,256]{1,0:T(8,128)(2,1)S(1)}, u32[]{:S(2)}, u32[]{:S(2)}) collective-permute-start(bf16[512,256]{1,0:T(8,128)(2,1)} %get-tuple-element.24), channel_id=1, source_target_pairs={{0,1},{1,2},{2,3},{3,4},{4,5},{5,6},{6,7},{7,0},{8,9},{9,10},{10,1... | collective-permute-start | bytes 786440 | tf_op jit(solution)/shard_map/ppermute | solution.py:185
  27.6 13.0 %collective-permute-start.3 = (bf16[512,256]{1,0:T(8,128)(2,1)}, bf16[512,256]{1,0:T(8,128)(2,1)S(1)}, u32[]{:S(2)}, u32[]{:S(2)}) collective-permute-start(bf16[512,256]{1,0:T(8,128)(2,1)} %get-tuple-element.25), channel_id=1, source_target_pairs={{0,7},{1,0},{2,1},{3,2},{4,3},{5,4},{6,5},{7,6},{8,15},{9,8},{10,9... | collective-permute-start | bytes 786440 | tf_op jit(solution)/shard_map/ppermute | solution.py:185
  29.6 14.4 %collective-permute-start.4 = (bf16[512,256]{1,0:T(8,128)(2,1)}, bf16[512,256]{1,0:T(8,128)(2,1)S(1)}, u32[]{:S(2)}, u32[]{:S(2)}) collective-permute-start(bf16[512,256]{1,0:T(8,128)(2,1)} %get-tuple-element.26), channel_id=1, source_target_pairs={{0,2},{1,3},{2,4},{3,5},{4,6},{5,7},{6,0},{7,1},{8,14},{9,15},{10,... | collective-permute-start | bytes 786440 | tf_op jit(solution)/shard_map/ppermute | solution.py:194
  35.2 19.0 %collective-permute-start = (bf16[512,256]{1,0:T(8,128)(2,1)}, bf16[512,256]{1,0:T(8,128)(2,1)S(1)}, u32[]{:S(2)}, u32[]{:S(2)}) collective-permute-start(bf16[512,256]{1,0:T(8,128)(2,1)} %get-tuple-element.22), channel_id=1, source_target_pairs={{0,1},{1,2},{2,3},{3,4},{4,5},{5,6},{6,7},{7,0},{8,9},{9,10},{10,1... | collective-permute-start | bytes 786440 | tf_op jit(solution)/shard_map/ppermute | solution.py:185
  37.2 17.1 %collective-permute-start.1 = (bf16[512,256]{1,0:T(8,128)(2,1)}, bf16[512,256]{1,0:T(8,128)(2,1)S(1)}, u32[]{:S(2)}, u32[]{:S(2)}) collective-permute-start(bf16[512,256]{1,0:T(8,128)(2,1)} %get-tuple-element.23), channel_id=1, source_target_pairs={{0,7},{1,0},{2,1},{3,2},{4,3},{5,4},{6,5},{7,6},{8,15},{9,8},{10,9... | collective-permute-start | bytes 786440 | tf_op jit(solution)/shard_map/ppermute | solution.py:185
  40.6 3.4 %copy-start.3 = (bf16[512,256]{1,0:T(8,128)(2,1)}, bf16[512,256]{1,0:T(8,128)(2,1)S(1)}, u32[]{:S(2)}) copy-start(bf16[512,256]{1,0:T(8,128)(2,1)S(1)} %collective-permute-done.2.up_ref) | copy-start | bytes 786436
  40.6 3.4 %copy-start.4 = (bf16[512,256]{1,0:T(8,128)(2,1)}, bf16[512,256]{1,0:T(8,128)(2,1)S(1)}, u32[]{:S(2)}) copy-start(bf16[512,256]{1,0:T(8,128)(2,1)S(1)} %collective-permute-done.3.down_ref) | copy-start | bytes 786436
  43.9 0.7 copy-start.5
  46.8 16.0 %collective-permute-start.5 = (bf16[512,256]{1,0:T(8,128)(2,1)}, bf16[512,256]{1,0:T(8,128)(2,1)S(1)}, u32[]{:S(2)}, u32[]{:S(2)}) collective-permute-start(bf16[512,256]{1,0:T(8,128)(2,1)} %get-tuple-element.29), channel_id=1, source_target_pairs={{0,2},{1,3},{2,4},{3,5},{4,6},{5,7},{6,0},{7,1},{8,10},{9,11},{10,... | collective-permute-start | bytes 786440 | tf_op jit(solution)/shard_map/ppermute | solution.py:185
  50.8 12.1 %collective-permute-start.6 = (bf16[512,256]{1,0:T(8,128)(2,1)}, bf16[512,256]{1,0:T(8,128)(2,1)S(1)}, u32[]{:S(2)}, u32[]{:S(2)}) collective-permute-start(bf16[512,256]{1,0:T(8,128)(2,1)} %get-tuple-element.30), channel_id=1, source_target_pairs={{0,6},{1,7},{2,0},{3,1},{4,2},{5,3},{6,4},{7,5},{8,14},{9,15},{10,... | collective-permute-start | bytes 786440 | tf_op jit(solution)/shard_map/ppermute | solution.py:185
  54.2 8.7 %copy-start.1 = (bf16[512,256]{1,0:T(8,128)(2,1)}, bf16[512,256]{1,0:T(8,128)(2,1)S(1)}, u32[]{:S(2)}) copy-start(bf16[512,256]{1,0:T(8,128)(2,1)S(1)} %collective-permute-done.up_ref) | copy-start | bytes 786436
  54.3 8.7 %copy-start.2 = (bf16[512,256]{1,0:T(8,128)(2,1)}, bf16[512,256]{1,0:T(8,128)(2,1)S(1)}, u32[]{:S(2)}) copy-start(bf16[512,256]{1,0:T(8,128)(2,1)S(1)} %collective-permute-done.1.down_ref) | copy-start | bytes 786436
  62.9 0.7 copy-start.6
  62.9 0.8 copy-start.7
  62.9 1.2 %copy-start = (bf16[32,16,1024]{2,1,0:T(8,128)(2,1)}, bf16[32,16,1024]{2,1,0:T(8,128)(2,1)S(1)}, u32[]{:S(2)}) copy-start(bf16[32,16,1024]{2,1,0:T(8,128)(2,1)S(1)} %all-to-all-done) | copy-start | bytes 3145732

commit v4 on v3

--- a/solution.py
+++ b/solution.py
@@ -50,11 +50,22 @@
                     ladder_ref[(half * LANES + c_at) // c_block, a * c_block : (a + 1) * c_block, :] = (
                         part[c_at : c_at + c_block]
                     )
+        own_ref, up_ref, up2_ref, across_ref, down2_ref, down_ref = out_refs
+        by_distance = (
+            own_ref,
+            up_ref.at[0],
+            up2_ref,
+            up_ref.at[1],
+            across_ref,
+            down_ref.at[1],
+            down2_ref,
+            down_ref.at[0],
+        )
         copies = [
             pltpu.make_async_copy(
                 ladder_ref.at[lax.rem(place_ref[0] + distance, n_pb)], out_ref, sems.at[distance]
             )
-            for distance, out_ref in enumerate(out_refs)
+            for distance, out_ref in enumerate(by_distance)
         ]
         for copy in copies:
             copy.start()
@@ -67,13 +78,15 @@
     n_occ = b_oc.shape[1]
     bd_width = f_bd.shape[1]
     block = (a_width * c_width // n_pb, bd_width)
+    pair = (2, *block)
+    shapes = (block, pair, block, block, block, pair)
     eye = jnp.eye(Q_GROUP, dtype=t1.dtype)
     singles = jnp.einsum("qr,ka->qark", eye, t1).reshape(Q_GROUP * a_width, Q_GROUP * n_occ)
     q_step = n_q // Q_STEPS
     return pl.pallas_call(
         contract_kernel,
         grid=(Q_STEPS,),
-        out_shape=[jax.ShapeDtypeStruct(block, jnp.bfloat16)] * n_pb,
+        out_shape=[jax.ShapeDtypeStruct(shape, jnp.bfloat16) for shape in shapes],
         in_specs=[
             SMEM,
             pl.BlockSpec((q_step, a_width, c_width), lambda step: (step, 0, 0)),
@@ -81,7 +94,7 @@
             pl.BlockSpec(singles.shape, lambda step: (0, 0)),
             pl.BlockSpec(f_bd.shape, lambda step: (0, 0)),
         ],
-        out_specs=[pl.BlockSpec(memory_space=pl.ANY)] * n_pb,
+        out_specs=[pl.BlockSpec(memory_space=pl.ANY)] * len(shapes),
         scratch_shapes=[
             pltpu.VMEM((c_width // LANES, n_q * a_width, LANES), jnp.float32),
             pltpu.VMEM((n_pb, *block), jnp.bfloat16),
@@ -100,7 +113,7 @@
         (0, up_ref, up2_ref, up_out),
         (1, down_ref, down2_ref, down_out),
     ):
-        total = own_ref[...].astype(jnp.float32) + passing_ref[...].astype(jnp.float32)
+        total = own_ref[...].astype(jnp.float32) + passing_ref[1].astype(jnp.float32)
         total += jnp.where(core_ref[0] == core, across, zero)
         out_ref[...] = total.astype(out_ref.dtype)
 
@@ -111,16 +124,17 @@
         out_shape=[jax.ShapeDtypeStruct(up2.shape, up2.dtype)] * 2,
         in_specs=[SMEM] + [VMEM] * 5,
         out_specs=[VMEM] * 2,
+        compiler_params=pltpu.CompilerParams(vmem_limit_bytes=8 << 20),
         cost_estimate=pl.CostEstimate(flops=4 * up2.size, bytes_accessed=2 << 20, transcendentals=0),
     )(core, up, down, across, up2, down2)
 
 
 def combine_kernel(
-    own_ref, up_ref, down_ref, up2_ref, down2_ref, t2_ref, out_ref, ladder_ref, turned_ref, factor_ref
+    own_ref, up_ref, down_ref, up2_ref, down2_ref, t2_ref, out_ref, ladder_ref, turned_ref, *factor_refs
 ):
     total = own_ref[...].astype(jnp.float32)
-    total += up_ref[...].astype(jnp.float32)
-    total += down_ref[...].astype(jnp.float32)
+    total += up_ref[0].astype(jnp.float32)
+    total += down_ref[0].astype(jnp.float32)
     total += up2_ref[...].astype(jnp.float32)
     total += down2_ref[...].astype(jnp.float32)
     for b_high in range(BB // LANE_GROUPS):
@@ -151,13 +165,20 @@
                 turned_ref[at : at + BB, :] = by_b[a * BB : (a + 1) * BB]
     for c_high in range(BB):
         tile = turned_ref[pl.ds(c_high, n_rows, stride=BB), :]
-        factor_ref[:, c_high * LANES : (c_high + 1) * LANES] = tile.astype(jnp.bfloat16)
-    out_ref[...] = lax.dot_general(
-        t2_ref[...],
-        factor_ref[...],
-        (((1,), (1,)), ((), ())),
-        preferred_element_type=jnp.float32,
-    )
+        high = tile.astype(jnp.bfloat16)
+        low = (tile - high.astype(jnp.float32)).astype(jnp.bfloat16)
+        for factor_ref, factor in zip(factor_refs, (high, low)):
+            factor_ref[:, c_high * LANES : (c_high + 1) * LANES] = factor
+    sums = [
+        lax.dot_general(
+            t2_ref[...],
+            factor_ref[...],
+            (((1,), (1,)), ((), ())),
+            preferred_element_type=jnp.float32,
+        )
+        for factor_ref in factor_refs
+    ]
+    out_ref[...] = (sums[0] + sums[1]).astype(out_ref.dtype)
 
 
 def combine(parts, t2):
@@ -166,14 +187,16 @@
     ab_width = block_rows * bd_width // cd_width
     return pl.pallas_call(
         combine_kernel,
-        out_shape=jax.ShapeDtypeStruct((pairs, ab_width), jnp.float32),
+        out_shape=jax.ShapeDtypeStruct((pairs, ab_width), jnp.bfloat16),
         in_specs=[VMEM] * 6,
         out_specs=VMEM,
         scratch_shapes=[
             pltpu.VMEM((BB // LANE_GROUPS, block_rows, LANES), jnp.float32),
             pltpu.VMEM((ab_width * BB, LANES), jnp.float32),
             pltpu.VMEM((ab_width, cd_width), jnp.bfloat16),
+            pltpu.VMEM((ab_width, cd_width), jnp.bfloat16),
         ],
+        compiler_params=pltpu.CompilerParams(vmem_limit_bytes=16 << 20),
         cost_estimate=pl.CostEstimate(
             flops=2 * pairs * ab_width * cd_width, bytes_accessed=3 << 20, transcendentals=0
         ),
@@ -205,20 +228,18 @@
         jnp.broadcast_to(t2[None], (n_aa, *t2.shape)), "aa", 0, 0, tiled=True
     ).reshape(-1, t2.shape[1])
 
-    own, up1, up2, up3, across, down3, down2, down1 = contract(b_ac, b_oc, t1, f_bd, place, n_pb)
+    own, up, up2, across, down2, down = contract(b_ac, b_oc, t1, f_bd, place, n_pb)
+    up = along_pb(up, 1)
+    down = along_pb(down, -1)
     across = across_pb(across, 2)
-    up3 = along_pb(up3, 1)
-    down3 = along_pb(down3, -1)
-    up1 = along_pb(up1, 1)
-    down1 = along_pb(down1, -1)
-    up2, down2 = merge(core, up3, down3, across, up2, down2)
+    up2, down2 = merge(core, up, down, across, up2, down2)
     up2 = along_pb(up2, 2)
     down2 = along_pb(down2, -2)
-    *parts, amplitudes = lax.optimization_barrier((own, up1, down1, up2, down2, amplitudes))
+    *parts, amplitudes = lax.optimization_barrier((own, up, down, up2, down2, amplitudes))
     sums = combine(parts, amplitudes)
     shares = sums.reshape(n_out, -1, sums.shape[1])
     shares = lax.all_to_all(shares, ("col", "pb"), 0, 0, tiled=True)
-    return jnp.sum(shares, axis=0)
+    return jnp.sum(shares.astype(jnp.float32), axis=0)
 
 
 def solution(mesh):

time: 105 us -> 104 us (level)
  the two profiles are of different devices: /device:TPU:21 before, /device:TPU:1 now
where the time goes in v4:
time: 104 us
  starting transfers between devices  36.8 us (35%)
  blocking collectives  27.8 us (27%)
  waiting for transfers between devices  25 us (24%)
  Pallas kernels  7.71 us (7%)
  local copies, waits for them, and re-layouts  5.55 us (5%)
    all_to_all x1, blocking collectives, step(): shares = lax.all_to_all(shares, ('col', 'pb'), 0, 0, tiled=True)  27.8 us
    ppermute x4, starting transfers between devices, along_pb(): lax.ppermute(array, 'pb', [(y, (y + distance) % n_pb) for y in range(n_pb)])  17 us
    all_to_all x1, starting transfers between devices, step(): lax.all_to_all(jnp.broadcast_to(t2[None], (n_aa, *t2.shape)), 'aa', 0, 0,...  15.8 us
    ppermute x1, waiting for transfers between devices, across_pb(): return lax.ppermute(array, ('col', 'pb'), pairs)  13.6 us
    ppermute x4, waiting for transfers between devices, along_pb(): lax.ppermute(array, 'pb', [(y, (y + distance) % n_pb) for y in range(n_pb)])  11.4 us
    pallas_call x1, Pallas kernels, contract(): pl.pallas_call(contract_kernel, grid=(Q_STEPS,), out_shape=[jax.ShapeDtyp...  6.41 us
    ppermute x1, starting transfers between devices, across_pb(): return lax.ppermute(array, ('col', 'pb'), pairs)  4.03 us
    unnamed x8, local copies, waits for them, and re-layouts  2.86 us
  transfers between devices with their start and end apart: 6, of which 3 were waited for; matrix products, arithmetic and copies ran while one was open for 1% of the time, Pallas kernels for 6%

profile of v4, /device:TPU:1, one launch (start us, length us, event | category | flops | bytes accessed | tf_op | source)
XLA Modules:
  0.0 103.7 jit_solution(6317118430552668651)
XLA Ops:
  0.0 0.0 copy-start.3
  0.0 1.9 %broadcast_in_dim.2 = bf16[32,16,1024]{2,1,0:T(8,128)(2,1)} broadcast(bf16[16,1024]{1,0:T(8,128)(2,1)} %param.9), dimensions={1,2} | broadcast | bytes 1081344 | tf_op jit(solution)/shard_map/broadcast_in_dim | solution.py:228
  1.9 15.8 %all-to-all-start = ((bf16[32,16,1024]{2,1,0:T(8,128)(2,1)}), bf16[32,16,1024]{2,1,0:T(8,128)(2,1)S(1)}, u32[]{:S(2)}, u32[]{:S(2)}) async-start(bf16[32,16,1024]{2,1,0:T(8,128)(2,1)} %broadcast_in_dim.2), calls=%async_computation | async-start | bytes 2097152 | tf_op jit(solution)/shard_map/all_to_all | solution.py:227
  17.7 0.0 copy-done.3
  17.8 0.1 multiply_bitcast_fusion
  17.8 0.8 reshape.17.singles_ref
  18.7 6.4 %shard_map.55 = (bf16[512,256]{1,0:T(8,128)(2,1)}, bf16[2,512,256]{2,1,0:T(8,128)(2,1)}, bf16[512,256]{1,0:T(8,128)(2,1)}, bf16[512,256]{1,0:T(8,128)(2,1)}, bf1...) custom-call(s32[1]{0:T(128)} %bitcast.place_ref, bf16[192,16,256]{2,1,0:T(8,128)(2,1)} %b_ac_ref.1, ...), custom_call_target="tpu_custom_call" | custom-call | flops 402653184 | bytes 7340032 | tf_op jit(solution)/shard_map/pallas_call | solution.py:86
  25.1 3.3 %collective-permute-start = (bf16[2,512,256]{2,1,0:T(8,128)(2,1)}, bf16[2,512,256]{2,1,0:T(8,128)(2,1)S(1)}, u32[]{:S(2)}, u32[]{:S(2)}) collective-permute-start(bf16[2,512,256]{2,1,0:T(8,128)(2,1)} %get-tuple-element.20), channel_id=1, source_target_pairs={{0,1},{1,2},{2,3},{3,4},{4,5},{5,6},{6,7},{7,0},{8,9},{9,10},{10,1... | collective-permute-start | bytes 1572872 | tf_op jit(solution)/shard_map/ppermute | solution.py:208
  28.4 4.5 %collective-permute-start.1 = (bf16[2,512,256]{2,1,0:T(8,128)(2,1)}, bf16[2,512,256]{2,1,0:T(8,128)(2,1)S(1)}, u32[]{:S(2)}, u32[]{:S(2)}) collective-permute-start(bf16[2,512,256]{2,1,0:T(8,128)(2,1)} %get-tuple-element.21), channel_id=1, source_target_pairs={{0,7},{1,0},{2,1},{3,2},{4,3},{5,4},{6,5},{7,6},{8,15},{9,8},{10,9... | collective-permute-start | bytes 1572872 | tf_op jit(solution)/shard_map/ppermute | solution.py:208
  32.9 4.0 %collective-permute-start.2 = (bf16[512,256]{1,0:T(8,128)(2,1)}, bf16[512,256]{1,0:T(8,128)(2,1)S(1)}, u32[]{:S(2)}, u32[]{:S(2)}) collective-permute-start(bf16[512,256]{1,0:T(8,128)(2,1)} %get-tuple-element.22), channel_id=1, source_target_pairs={{0,2},{1,3},{2,4},{3,5},{4,6},{5,7},{6,0},{7,1},{8,14},{9,15},{10,... | collective-permute-start | bytes 786440 | tf_op jit(solution)/shard_map/ppermute | solution.py:217
  37.0 13.6 %collective-permute-done.2.across_ref = bf16[512,256]{1,0:T(8,128)(2,1)S(1)} collective-permute-done((bf16[512,256]{1,0:T(8,128)(2,1)}, bf16[512,256]{1,0:T(8,128)(2,1)S(1)}, u32[]{:S(2)}, u32[]{:S(2)}) %collective-permute-start.2) | collective-permute-done | bytes 262176 | tf_op jit(solution)/shard_map/ppermute | solution.py:217
  50.6 0.0 collective-permute-done.up_ref
  50.6 0.0 collective-permute-done.1.down_ref
  50.6 0.0 copy-start.1
  50.6 0.9 copy-done.1
  51.6 0.0 copy-start.2
  51.6 0.9 copy-done.2
  52.5 0.2 shard_map.56
  52.7 7.2 %collective-permute-start.3 = (bf16[512,256]{1,0:T(8,128)(2,1)S(1)}, bf16[512,256]{1,0:T(8,128)(2,1)S(1)}, u32[]{:S(2)}, u32[]{:S(2)}) collective-permute-start(bf16[512,256]{1,0:T(8,128)(2,1)S(1)} %get-tuple-element.25), channel_id=1, source_target_pairs={{0,2},{1,3},{2,4},{3,5},{4,6},{5,7},{6,0},{7,1},{8,10},{9,11},{10,... | collective-permute-start | bytes 786440 | tf_op jit(solution)/shard_map/ppermute | solution.py:208
  59.9 1.9 %collective-permute-start.4 = (bf16[512,256]{1,0:T(8,128)(2,1)S(1)}, bf16[512,256]{1,0:T(8,128)(2,1)S(1)}, u32[]{:S(2)}, u32[]{:S(2)}) collective-permute-start(bf16[512,256]{1,0:T(8,128)(2,1)S(1)} %get-tuple-element.26), channel_id=1, source_target_pairs={{0,6},{1,7},{2,0},{3,1},{4,2},{5,3},{6,4},{7,5},{8,14},{9,15},{10,... | collective-permute-start | bytes 786440 | tf_op jit(solution)/shard_map/ppermute | solution.py:208
  61.9 8.0 %collective-permute-done.3.up2_ref = bf16[512,256]{1,0:T(8,128)(2,1)S(1)} collective-permute-done((bf16[512,256]{1,0:T(8,128)(2,1)S(1)}, bf16[512,256]{1,0:T(8,128)(2,1)S(1)}, u32[]{:S(2)}, u32[]{:S(2)}) %collective-permute-start.3) | collective-permute-done | bytes 262176 | tf_op jit(solution)/shard_map/ppermute | solution.py:208
  69.9 3.4 %collective-permute-done.4.down2_ref = bf16[512,256]{1,0:T(8,128)(2,1)S(1)} collective-permute-done((bf16[512,256]{1,0:T(8,128)(2,1)S(1)}, bf16[512,256]{1,0:T(8,128)(2,1)S(1)}, u32[]{:S(2)}, u32[]{:S(2)}) %collective-permute-start.4) | collective-permute-done | bytes 262176 | tf_op jit(solution)/shard_map/ppermute | solution.py:208
  73.3 0.0 all-to-all-done
  73.3 0.0 copy-start
  73.3 0.9 copy-done
  74.2 1.1 %shard_map.57 = bf16[512,128]{1,0:T(8,128)(2,1)S(1)} custom-call(bf16[512,256]{1,0:T(8,128)(2,1)S(1)} %copy-done, bf16[2,512,256]{2,1,0:T(8,128)(2,1)S(1)} %collective-permute-done.up_ref, bf16[2,512,256]{2,1,0:T(8,128)(2,1)S(1)} %collective-permute-done.1.down_ref, bf16[512,256]{1,0:T(8,128)(2,1)S(1)} %collective-permute-done.3.up2_ref, ...), custom_call_target="tpu_custom_call" | custom-call | flops 134217728 | bytes 3145728 | tf_op jit(solution)/shard_map/pallas_call | solution.py:188
  75.3 27.8 %all_to_all.10 = bf16[32,16,128]{2,1,0:T(8,128)(2,1)S(1)} all-to-all(bf16[32,16,128]{2,1,0:T(8,128)(2,1)S(1)} %bitcast.9), channel_id=1, replica_groups=mesh['aa'=32,'col'=4,'pb'=8] {'col','pb'}, dimensions={0} | all-to-all | bytes 262144 | tf_op jit(solution)/shard_map/all_to_all | solution.py:241
  103.1 0.6 convert_reduce_fusion
  (1 shorter events, 0.0 us)
Async XLA Ops:
  0.0 17.7 %copy-start.3 = (bf16[32,16]{0,1:T(8,128)(2,1)S(1)}, bf16[32,16]{0,1:T(8,128)(2,1)}, u32[]{:S(2)}) copy-start(bf16[32,16]{0,1:T(8,128)(2,1)} %param.7) | copy-start | bytes 3076
  1.9 71.4 %all-to-all-start = ((bf16[32,16,1024]{2,1,0:T(8,128)(2,1)}), bf16[32,16,1024]{2,1,0:T(8,128)(2,1)S(1)}, u32[]{:S(2)}, u32[]{:S(2)}) async-start(bf16[32,16,1024]{2,1,0:T(8,128)(2,1)} %broadcast_in_dim.2), calls=%async_computation | async-start | bytes 2097152 | tf_op jit(solution)/shard_map/all_to_all | solution.py:227
  25.1 25.5 %collective-permute-start = (bf16[2,512,256]{2,1,0:T(8,128)(2,1)}, bf16[2,512,256]{2,1,0:T(8,128)(2,1)S(1)}, u32[]{:S(2)}, u32[]{:S(2)}) collective-permute-start(bf16[2,512,256]{2,1,0:T(8,128)(2,1)} %get-tuple-element.20), channel_id=1, source_target_pairs={{0,1},{1,2},{2,3},{3,4},{4,5},{5,6},{6,7},{7,0},{8,9},{9,10},{10,1... | collective-permute-start | bytes 1572872 | tf_op jit(solution)/shard_map/ppermute | solution.py:208
  28.4 22.2 %collective-permute-start.1 = (bf16[2,512,256]{2,1,0:T(8,128)(2,1)}, bf16[2,512,256]{2,1,0:T(8,128)(2,1)S(1)}, u32[]{:S(2)}, u32[]{:S(2)}) collective-permute-start(bf16[2,512,256]{2,1,0:T(8,128)(2,1)} %get-tuple-element.21), channel_id=1, source_target_pairs={{0,7},{1,0},{2,1},{3,2},{4,3},{5,4},{6,5},{7,6},{8,15},{9,8},{10,9... | collective-permute-start | bytes 1572872 | tf_op jit(solution)/shard_map/ppermute | solution.py:208
  32.9 17.7 %collective-permute-start.2 = (bf16[512,256]{1,0:T(8,128)(2,1)}, bf16[512,256]{1,0:T(8,128)(2,1)S(1)}, u32[]{:S(2)}, u32[]{:S(2)}) collective-permute-start(bf16[512,256]{1,0:T(8,128)(2,1)} %get-tuple-element.22), channel_id=1, source_target_pairs={{0,2},{1,3},{2,4},{3,5},{4,6},{5,7},{6,0},{7,1},{8,14},{9,15},{10,... | collective-permute-start | bytes 786440 | tf_op jit(solution)/shard_map/ppermute | solution.py:217
  50.6 1.0 copy-start.1
  51.6 0.9 copy-start.2
  52.7 17.1 %collective-permute-start.3 = (bf16[512,256]{1,0:T(8,128)(2,1)S(1)}, bf16[512,256]{1,0:T(8,128)(2,1)S(1)}, u32[]{:S(2)}, u32[]{:S(2)}) collective-permute-start(bf16[512,256]{1,0:T(8,128)(2,1)S(1)} %get-tuple-element.25), channel_id=1, source_target_pairs={{0,2},{1,3},{2,4},{3,5},{4,6},{5,7},{6,0},{7,1},{8,10},{9,11},{10,... | collective-permute-start | bytes 786440 | tf_op jit(solution)/shard_map/ppermute | solution.py:208
  59.9 13.3 %collective-permute-start.4 = (bf16[512,256]{1,0:T(8,128)(2,1)S(1)}, bf16[512,256]{1,0:T(8,128)(2,1)S(1)}, u32[]{:S(2)}, u32[]{:S(2)}) collective-permute-start(bf16[512,256]{1,0:T(8,128)(2,1)S(1)} %get-tuple-element.26), channel_id=1, source_target_pairs={{0,6},{1,7},{2,0},{3,1},{4,2},{5,3},{6,4},{7,5},{8,14},{9,15},{10,... | collective-permute-start | bytes 786440 | tf_op jit(solution)/shard_map/ppermute | solution.py:208
  73.3 1.0 copy-start

commit v5 on v4

--- a/solution.py
+++ b/solution.py
@@ -11,19 +11,36 @@
 LANES = 128
 LANE_GROUPS = LANES // DB
 Q_GROUP = 8
-Q_STEPS = 4
+Q_STEPS = 6
 VMEM = pl.BlockSpec(memory_space=pltpu.VMEM)
 SMEM = pl.BlockSpec(memory_space=pltpu.SMEM)
 
 
-def contract_kernel(place_ref, b_ac_ref, b_oc_ref, singles_ref, f_ref, *refs):
-    out_refs, (dressed_ref, ladder_ref, sems) = refs[:-3], refs[-3:]
+def contract_kernel(place_ref, b_ac_ref, b_oc_ref, t1_ref, f_ref, *refs):
+    out_refs, (singles_ref, dressed_ref, ladder_ref, sems) = refs[:-4], refs[-4:]
     n_q, a_width, c_width = b_ac_ref.shape
     n_total = dressed_ref.shape[1] // a_width
     n_pb, block_rows, _ = ladder_ref.shape
     c_block = block_rows // a_width
     size = Q_GROUP * a_width
     step = pl.program_id(0)
+
+    @pl.when(step == 0)
+    def _():
+        n_occ = b_oc_ref.shape[1]
+        row = lax.broadcasted_iota(jnp.int32, (size, a_width), 0)
+        column = lax.broadcasted_iota(jnp.int32, (size, a_width), 1)
+        tall = jnp.where(row % a_width == column, 1.0, 0.0).astype(jnp.bfloat16)
+        row = lax.broadcasted_iota(jnp.int32, (n_occ, Q_GROUP * n_occ), 0)
+        column = lax.broadcasted_iota(jnp.int32, (n_occ, Q_GROUP * n_occ), 1)
+        wide = jnp.where(column % n_occ == row, 1.0, 0.0).astype(jnp.bfloat16)
+        rows = jnp.dot(tall, t1_ref[...], preferred_element_type=jnp.float32).astype(jnp.bfloat16)
+        repeated = jnp.dot(rows, wide, preferred_element_type=jnp.float32)
+        row = lax.broadcasted_iota(jnp.int32, repeated.shape, 0)
+        column = lax.broadcasted_iota(jnp.int32, repeated.shape, 1)
+        same = row // a_width == column // n_occ
+        singles_ref[...] = jnp.where(same, repeated, 0.0).astype(jnp.bfloat16)
+
     for group in range(n_q // Q_GROUP):
         rows = slice(group * Q_GROUP, (group + 1) * Q_GROUP)
         occupied = b_oc_ref[rows].reshape(-1, c_width)
@@ -80,8 +97,6 @@
     block = (a_width * c_width // n_pb, bd_width)
     pair = (2, *block)
     shapes = (block, pair, block, block, block, pair)
-    eye = jnp.eye(Q_GROUP, dtype=t1.dtype)
-    singles = jnp.einsum("qr,ka->qark", eye, t1).reshape(Q_GROUP * a_width, Q_GROUP * n_occ)
     q_step = n_q // Q_STEPS
     return pl.pallas_call(
         contract_kernel,
@@ -91,11 +106,12 @@
             SMEM,
             pl.BlockSpec((q_step, a_width, c_width), lambda step: (step, 0, 0)),
             pl.BlockSpec((q_step, n_occ, c_width), lambda step: (step, 0, 0)),
-            pl.BlockSpec(singles.shape, lambda step: (0, 0)),
+            pl.BlockSpec((a_width, n_occ), lambda step: (0, 0)),
             pl.BlockSpec(f_bd.shape, lambda step: (0, 0)),
         ],
         out_specs=[pl.BlockSpec(memory_space=pl.ANY)] * len(shapes),
         scratch_shapes=[
+            pltpu.VMEM((Q_GROUP * a_width, Q_GROUP * n_occ), jnp.bfloat16),
             pltpu.VMEM((c_width // LANES, n_q * a_width, LANES), jnp.float32),
             pltpu.VMEM((n_pb, *block), jnp.bfloat16),
             pltpu.SemaphoreType.DMA((n_pb,)),
@@ -103,36 +119,34 @@
         cost_estimate=pl.CostEstimate(
             flops=2 * n_q * a_width * c_width * bd_width, bytes_accessed=7 << 20, transcendentals=0
         ),
-    )(place, b_ac, b_oc, singles, f_bd)
-
-
-def merge_kernel(core_ref, up_ref, down_ref, across_ref, up2_ref, down2_ref, up_out, down_out):
-    across = across_ref[...].astype(jnp.float32)
-    zero = jnp.zeros_like(across)
-    for core, passing_ref, own_ref, out_ref in (
-        (0, up_ref, up2_ref, up_out),
-        (1, down_ref, down2_ref, down_out),
+    )(place, b_ac, b_oc, t1.T, f_bd)
+
+
+def merge_kernel(up_ref, down_ref, up2_ref, down2_ref, up_out, down_out):
+    for passing_ref, own_ref, out_ref in (
+        (up_ref, up2_ref, up_out),
+        (down_ref, down2_ref, down_out),
     ):
         total = own_ref[...].astype(jnp.float32) + passing_ref[1].astype(jnp.float32)
-        total += jnp.where(core_ref[0] == core, across, zero)
         out_ref[...] = total.astype(out_ref.dtype)
 
 
-def merge(core, up, down, across, up2, down2):
+def merge(up, down, up2, down2):
     return pl.pallas_call(
         merge_kernel,
         out_shape=[jax.ShapeDtypeStruct(up2.shape, up2.dtype)] * 2,
-        in_specs=[SMEM] + [VMEM] * 5,
+        in_specs=[VMEM] * 4,
         out_specs=[VMEM] * 2,
         compiler_params=pltpu.CompilerParams(vmem_limit_bytes=8 << 20),
-        cost_estimate=pl.CostEstimate(flops=4 * up2.size, bytes_accessed=2 << 20, transcendentals=0),
-    )(core, up, down, across, up2, down2)
+        cost_estimate=pl.CostEstimate(flops=2 * up2.size, bytes_accessed=2 << 20, transcendentals=0),
+    )(up, down, up2, down2)
 
 
 def combine_kernel(
-    own_ref, up_ref, down_ref, up2_ref, down2_ref, t2_ref, out_ref, ladder_ref, turned_ref, *factor_refs
+    own_ref, across_ref, up_ref, down_ref, up2_ref, down2_ref, t2_ref, out_ref, ladder_ref, turned_ref, *factor_refs
 ):
     total = own_ref[...].astype(jnp.float32)
+    total += across_ref[...].astype(jnp.float32)
     total += up_ref[0].astype(jnp.float32)
     total += down_ref[0].astype(jnp.float32)
     total += up2_ref[...].astype(jnp.float32)
@@ -188,7 +202,7 @@
     return pl.pallas_call(
         combine_kernel,
         out_shape=jax.ShapeDtypeStruct((pairs, ab_width), jnp.bfloat16),
-        in_specs=[VMEM] * 6,
+        in_specs=[VMEM] * (len(parts) + 1),
         out_specs=VMEM,
         scratch_shapes=[
             pltpu.VMEM((BB // LANE_GROUPS, block_rows, LANES), jnp.float32),
@@ -222,7 +236,6 @@
     n_pb = lax.axis_size("pb")
     n_out = lax.axis_size("col") * n_pb
     place = lax.axis_index("pb").astype(jnp.int32).reshape(1)
-    core = lax.rem(lax.axis_index("col"), 2).astype(jnp.int32).reshape(1)
 
     amplitudes = lax.all_to_all(
         jnp.broadcast_to(t2[None], (n_aa, *t2.shape)), "aa", 0, 0, tiled=True
@@ -231,11 +244,13 @@
     own, up, up2, across, down2, down = contract(b_ac, b_oc, t1, f_bd, place, n_pb)
     up = along_pb(up, 1)
     down = along_pb(down, -1)
-    across = across_pb(across, 2)
-    up2, down2 = merge(core, up, down, across, up2, down2)
+    across = across_pb(across, 4)
+    up2, down2 = merge(up, down, up2, down2)
     up2 = along_pb(up2, 2)
     down2 = along_pb(down2, -2)
-    *parts, amplitudes = lax.optimization_barrier((own, up, down, up2, down2, amplitudes))
+    *parts, amplitudes = lax.optimization_barrier(
+        (own, across, up, down, up2, down2, amplitudes)
+    )
     sums = combine(parts, amplitudes)
     shares = sums.reshape(n_out, -1, sums.shape[1])
     shares = lax.all_to_all(shares, ("col", "pb"), 0, 0, tiled=True)

time: 104 us -> 110 us (1.058)
  blocking collectives: 27.8 us -> 38.2 us
  waiting for transfers between devices: 25 us -> 19.1 us
  Pallas kernels: 7.71 us -> 8.89 us
    ppermute x1, waiting for transfers between devices: 13.6 us -> 0.01 us  [across_pb(): return lax.ppermute(array, ('col', 'pb'), pairs)]
    all_to_all x1, blocking collectives: 27.8 us -> 38.2 us  [step(): shares = lax.all_to_all(shares, ('col', 'pb'), 0, 0, tiled=True)]
    ppermute x4, waiting for transfers between devices: 11.4 us -> 19.1 us  [along_pb(): lax.ppermute(array, 'pb', [(y, (y + distance) % n_pb) for y in range(n_pb)])]
    ppermute x1, starting transfers between devices: 4.03 us -> 6.59 us  [across_pb(): return lax.ppermute(array, ('col', 'pb'), pairs)]
    ppermute x4, starting transfers between devices: 17 us -> 15.2 us  [along_pb(): lax.ppermute(array, 'pb', [(y, (y + distance) % n_pb) for y in range(n_pb)])]
    pallas_call x1, Pallas kernels: 6.41 us -> 7.65 us  [contract(): pl.pallas_call(contract_kernel, grid=(Q_STEPS,), out_shape=[jax.ShapeDtyp...]
    unnamed x8 -> x6, local copies, waits for them, and re-layouts: 2.86 us -> 2.85 us
  transfers between devices with their start and end apart: 6 -> 6, of which waited for: 3 -> 4; matrix products, arithmetic and copies ran while one was open for 1% -> 0% of each run, Pallas kernels for 6% -> 7%
where the time goes in v5:
time: 110 us; the launch traced here: 109 us
  blocking collectives  38.2 us (35%)
  starting transfers between devices  37.6 us (34%)
  waiting for transfers between devices  19.1 us (17%)
  Pallas kernels  8.89 us (8%)
  local copies, waits for them, and re-layouts  4.7 us (4%)
    all_to_all x1, blocking collectives, step(): shares = lax.all_to_all(shares, ('col', 'pb'), 0, 0, tiled=True)  38.2 us
    ppermute x4, waiting for transfers between devices, along_pb(): lax.ppermute(array, 'pb', [(y, (y + distance) % n_pb) for y in range(n_pb)])  19.1 us
    all_to_all x1, starting transfers between devices, step(): lax.all_to_all(jnp.broadcast_to(t2[None], (n_aa, *t2.shape)), 'aa', 0, 0,...  15.8 us
    ppermute x4, starting transfers between devices, along_pb(): lax.ppermute(array, 'pb', [(y, (y + distance) % n_pb) for y in range(n_pb)])  15.2 us
    pallas_call x1, Pallas kernels, contract(): pl.pallas_call(contract_kernel, grid=(Q_STEPS,), out_shape=[jax.ShapeDtyp...  7.65 us
    ppermute x1, starting transfers between devices, across_pb(): return lax.ppermute(array, ('col', 'pb'), pairs)  6.59 us
    unnamed x6, local copies, waits for them, and re-layouts  2.85 us
  transfers between devices with their start and end apart: 6, of which 4 were waited for; matrix products, arithmetic and copies ran while one was open for 0% of the time, Pallas kernels for 7%

profile of v5, /device:TPU:1, one launch (start us, length us, event | category | flops | bytes accessed | tf_op | source)
XLA Modules:
  0.0 109.2 jit_solution(8764851018992451214)
XLA Ops:
  0.0 1.8 %broadcast_in_dim.2 = bf16[32,16,1024]{2,1,0:T(8,128)(2,1)} broadcast(bf16[16,1024]{1,0:T(8,128)(2,1)} %param.9), dimensions={1,2} | broadcast | bytes 1081344 | tf_op jit(solution)/shard_map/broadcast_in_dim | solution.py:241
  1.8 15.8 %all-to-all-start = ((bf16[32,16,1024]{2,1,0:T(8,128)(2,1)}), bf16[32,16,1024]{2,1,0:T(8,128)(2,1)S(1)}, u32[]{:S(2)}, u32[]{:S(2)}) async-start(bf16[32,16,1024]{2,1,0:T(8,128)(2,1)} %broadcast_in_dim.2), calls=%async_computation | async-start | bytes 2097152 | tf_op jit(solution)/shard_map/all_to_all | solution.py:240
  17.7 7.7 %shard_map.55 = (bf16[512,256]{1,0:T(8,128)(2,1)}, bf16[2,512,256]{2,1,0:T(8,128)(2,1)}, bf16[512,256]{1,0:T(8,128)(2,1)}, bf16[512,256]{1,0:T(8,128)(2,1)}, bf1...) custom-call(s32[1]{0:T(128)} %bitcast.place_ref, bf16[192,16,256]{2,1,0:T(8,128)(2,1)} %b_ac_ref.1, ...), custom_call_target="tpu_custom_call" | custom-call | flops 402653184 | bytes 7340032 | tf_op jit(solution)/shard_map/pallas_call | solution.py:101
  25.4 3.3 %collective-permute-start.1 = (bf16[2,512,256]{2,1,0:T(8,128)(2,1)}, bf16[2,512,256]{2,1,0:T(8,128)(2,1)S(1)}, u32[]{:S(2)}, u32[]{:S(2)}) collective-permute-start(bf16[2,512,256]{2,1,0:T(8,128)(2,1)} %get-tuple-element.22), channel_id=1, source_target_pairs={{0,1},{1,2},{2,3},{3,4},{4,5},{5,6},{6,7},{7,0},{8,9},{9,10},{10,1... | collective-permute-start | bytes 1572872 | tf_op jit(solution)/shard_map/ppermute | solution.py:222
  28.7 4.5 %collective-permute-start.2 = (bf16[2,512,256]{2,1,0:T(8,128)(2,1)}, bf16[2,512,256]{2,1,0:T(8,128)(2,1)S(1)}, u32[]{:S(2)}, u32[]{:S(2)}) collective-permute-start(bf16[2,512,256]{2,1,0:T(8,128)(2,1)} %get-tuple-element.23), channel_id=1, source_target_pairs={{0,7},{1,0},{2,1},{3,2},{4,3},{5,4},{6,5},{7,6},{8,15},{9,8},{10,9... | collective-permute-start | bytes 1572872 | tf_op jit(solution)/shard_map/ppermute | solution.py:222
  33.2 6.6 %collective-permute-start = (bf16[512,256]{1,0:T(8,128)(2,1)}, bf16[512,256]{1,0:T(8,128)(2,1)S(1)}, u32[]{:S(2)}, u32[]{:S(2)}) collective-permute-start(bf16[512,256]{1,0:T(8,128)(2,1)} %get-tuple-element.21), channel_id=1, source_target_pairs={{0,4},{1,5},{2,6},{3,7},{4,0},{5,1},{6,2},{7,3},{8,12},{9,13},{10,... | collective-permute-start | bytes 786440 | tf_op jit(solution)/shard_map/ppermute | solution.py:231
  39.8 2.8 %collective-permute-done.1.up_ref = bf16[2,512,256]{2,1,0:T(8,128)(2,1)S(1)} collective-permute-done((bf16[2,512,256]{2,1,0:T(8,128)(2,1)}, bf16[2,512,256]{2,1,0:T(8,128)(2,1)S(1)}, u32[]{:S(2)}, u32[]{:S(2)}) %collective-permute-start.1) | collective-permute-done | bytes 524320 | tf_op jit(solution)/shard_map/ppermute | solution.py:222
  42.6 2.0 %collective-permute-done.2.down_ref = bf16[2,512,256]{2,1,0:T(8,128)(2,1)S(1)} collective-permute-done((bf16[2,512,256]{2,1,0:T(8,128)(2,1)}, bf16[2,512,256]{2,1,0:T(8,128)(2,1)S(1)}, u32[]{:S(2)}, u32[]{:S(2)}) %collective-permute-start.2) | collective-permute-done | bytes 524320 | tf_op jit(solution)/shard_map/ppermute | solution.py:222
  44.6 0.0 copy-start.1
  44.6 0.9 copy-done.1
  45.5 0.0 copy-start.2
  45.5 0.9 copy-done.2
  46.5 0.1 shard_map.56
  46.6 4.3 %collective-permute-start.3 = (bf16[512,256]{1,0:T(8,128)(2,1)S(1)}, bf16[512,256]{1,0:T(8,128)(2,1)S(1)}, u32[]{:S(2)}, u32[]{:S(2)}) collective-permute-start(bf16[512,256]{1,0:T(8,128)(2,1)S(1)} %get-tuple-element.26), channel_id=1, source_target_pairs={{0,2},{1,3},{2,4},{3,5},{4,6},{5,7},{6,0},{7,1},{8,10},{9,11},{10,... | collective-permute-start | bytes 786440 | tf_op jit(solution)/shard_map/ppermute | solution.py:222
  51.0 3.1 %collective-permute-start.4 = (bf16[512,256]{1,0:T(8,128)(2,1)S(1)}, bf16[512,256]{1,0:T(8,128)(2,1)S(1)}, u32[]{:S(2)}, u32[]{:S(2)}) collective-permute-start(bf16[512,256]{1,0:T(8,128)(2,1)S(1)} %get-tuple-element.27), channel_id=1, source_target_pairs={{0,6},{1,7},{2,0},{3,1},{4,2},{5,3},{6,4},{7,5},{8,14},{9,15},{10,... | collective-permute-start | bytes 786440 | tf_op jit(solution)/shard_map/ppermute | solution.py:222
  54.0 0.0 collective-permute-done.across_ref
  54.0 7.7 %collective-permute-done.3.up2_ref = bf16[512,256]{1,0:T(8,128)(2,1)S(1)} collective-permute-done((bf16[512,256]{1,0:T(8,128)(2,1)S(1)}, bf16[512,256]{1,0:T(8,128)(2,1)S(1)}, u32[]{:S(2)}, u32[]{:S(2)}) %collective-permute-start.3) | collective-permute-done | bytes 262176 | tf_op jit(solution)/shard_map/ppermute | solution.py:222
  61.7 6.6 %collective-permute-done.4.down2_ref = bf16[512,256]{1,0:T(8,128)(2,1)S(1)} collective-permute-done((bf16[512,256]{1,0:T(8,128)(2,1)S(1)}, bf16[512,256]{1,0:T(8,128)(2,1)S(1)}, u32[]{:S(2)}, u32[]{:S(2)}) %collective-permute-start.4) | collective-permute-done | bytes 262176 | tf_op jit(solution)/shard_map/ppermute | solution.py:222
  68.3 0.0 all-to-all-done
  68.3 0.0 copy-start
  68.3 0.9 copy-done
  69.3 1.1 %shard_map.57 = bf16[512,128]{1,0:T(8,128)(2,1)S(1)} custom-call(bf16[512,256]{1,0:T(8,128)(2,1)S(1)} %copy-done, bf16[512,256]{1,0:T(8,128)(2,1)S(1)} %collective-permute-done.across_ref, bf16[2,512,256]{2,1,0:T(8,128)(2,1)S(1)} %collective-permute-done.1.up_ref, bf16[2,512,256]{2,1,0:T(8,128)(2,1)S(1)} %collective-permute-done.2.down_ref, ...), custom_call_target="tpu_custom_call" | custom-call | flops 134217728 | bytes 3145728 | tf_op jit(solution)/shard_map/pallas_call | solution.py:202
  70.4 38.2 %all_to_all.10 = bf16[32,16,128]{2,1,0:T(8,128)(2,1)S(1)} all-to-all(bf16[32,16,128]{2,1,0:T(8,128)(2,1)S(1)} %bitcast.5), channel_id=1, replica_groups=mesh['aa'=32,'col'=4,'pb'=8] {'col','pb'}, dimensions={0} | all-to-all | bytes 262144 | tf_op jit(solution)/shard_map/all_to_all | solution.py:256
  108.6 0.6 convert_reduce_fusion
Async XLA Ops:
  1.8 66.5 %all-to-all-start = ((bf16[32,16,1024]{2,1,0:T(8,128)(2,1)}), bf16[32,16,1024]{2,1,0:T(8,128)(2,1)S(1)}, u32[]{:S(2)}, u32[]{:S(2)}) async-start(bf16[32,16,1024]{2,1,0:T(8,128)(2,1)} %broadcast_in_dim.2), calls=%async_computation | async-start | bytes 2097152 | tf_op jit(solution)/shard_map/all_to_all | solution.py:240
  25.4 17.2 %collective-permute-start.1 = (bf16[2,512,256]{2,1,0:T(8,128)(2,1)}, bf16[2,512,256]{2,1,0:T(8,128)(2,1)S(1)}, u32[]{:S(2)}, u32[]{:S(2)}) collective-permute-start(bf16[2,512,256]{2,1,0:T(8,128)(2,1)} %get-tuple-element.22), channel_id=1, source_target_pairs={{0,1},{1,2},{2,3},{3,4},{4,5},{5,6},{6,7},{7,0},{8,9},{9,10},{10,1... | collective-permute-start | bytes 1572872 | tf_op jit(solution)/shard_map/ppermute | solution.py:222
  28.7 15.9 %collective-permute-start.2 = (bf16[2,512,256]{2,1,0:T(8,128)(2,1)}, bf16[2,512,256]{2,1,0:T(8,128)(2,1)S(1)}, u32[]{:S(2)}, u32[]{:S(2)}) collective-permute-start(bf16[2,512,256]{2,1,0:T(8,128)(2,1)} %get-tuple-element.23), channel_id=1, source_target_pairs={{0,7},{1,0},{2,1},{3,2},{4,3},{5,4},{6,5},{7,6},{8,15},{9,8},{10,9... | collective-permute-start | bytes 1572872 | tf_op jit(solution)/shard_map/ppermute | solution.py:222
  33.2 20.8 %collective-permute-start = (bf16[512,256]{1,0:T(8,128)(2,1)}, bf16[512,256]{1,0:T(8,128)(2,1)S(1)}, u32[]{:S(2)}, u32[]{:S(2)}) collective-permute-start(bf16[512,256]{1,0:T(8,128)(2,1)} %get-tuple-element.21), channel_id=1, source_target_pairs={{0,4},{1,5},{2,6},{3,7},{4,0},{5,1},{6,2},{7,3},{8,12},{9,13},{10,... | collective-permute-start | bytes 786440 | tf_op jit(solution)/shard_map/ppermute | solution.py:231
  44.6 0.9 copy-start.1
  45.5 0.9 copy-start.2
  46.6 15.1 %collective-permute-start.3 = (bf16[512,256]{1,0:T(8,128)(2,1)S(1)}, bf16[512,256]{1,0:T(8,128)(2,1)S(1)}, u32[]{:S(2)}, u32[]{:S(2)}) collective-permute-start(bf16[512,256]{1,0:T(8,128)(2,1)S(1)} %get-tuple-element.26), channel_id=1, source_target_pairs={{0,2},{1,3},{2,4},{3,5},{4,6},{5,7},{6,0},{7,1},{8,10},{9,11},{10,... | collective-permute-start | bytes 786440 | tf_op jit(solution)/shard_map/ppermute | solution.py:222
  51.0 17.4 %collective-permute-start.4 = (bf16[512,256]{1,0:T(8,128)(2,1)S(1)}, bf16[512,256]{1,0:T(8,128)(2,1)S(1)}, u32[]{:S(2)}, u32[]{:S(2)}) collective-permute-start(bf16[512,256]{1,0:T(8,128)(2,1)S(1)} %get-tuple-element.27), channel_id=1, source_target_pairs={{0,6},{1,7},{2,0},{3,1},{4,2},{5,3},{6,4},{7,5},{8,14},{9,15},{10,... | collective-permute-start | bytes 786440 | tf_op jit(solution)/shard_map/ppermute | solution.py:222
  68.3 1.0 copy-start

commit v6 on v4

--- a/solution.py
+++ b/solution.py
@@ -11,19 +11,44 @@
 LANES = 128
 LANE_GROUPS = LANES // DB
 Q_GROUP = 8
-Q_STEPS = 4
+Q_STEPS = 6
+A_CHUNK = 4
 VMEM = pl.BlockSpec(memory_space=pltpu.VMEM)
 SMEM = pl.BlockSpec(memory_space=pltpu.SMEM)
 
 
-def contract_kernel(place_ref, b_ac_ref, b_oc_ref, singles_ref, f_ref, *refs):
-    out_refs, (dressed_ref, ladder_ref, sems) = refs[:-3], refs[-3:]
+def contract_kernel(place_ref, b_ac_ref, b_oc_ref, t1_ref, f_ref, t2_ref, *refs):
+    out_refs, (singles_ref, dressed_ref, ladder_ref, sems, t2_sems) = refs[:-5], refs[-5:]
+    own_ref, up_ref, up2_ref, across_ref, down2_ref, down_ref, repeats_ref = out_refs
     n_q, a_width, c_width = b_ac_ref.shape
     n_total = dressed_ref.shape[1] // a_width
     n_pb, block_rows, _ = ladder_ref.shape
     c_block = block_rows // a_width
     size = Q_GROUP * a_width
     step = pl.program_id(0)
+    repeats = [
+        pltpu.make_async_copy(t2_ref, repeats_ref.at[at], t2_sems.at[at])
+        for at in range(repeats_ref.shape[0])
+    ]
+
+    @pl.when(step == 0)
+    def _():
+        for copy in repeats:
+            copy.start()
+        n_occ = b_oc_ref.shape[1]
+        row = lax.broadcasted_iota(jnp.int32, (size, a_width), 0)
+        column = lax.broadcasted_iota(jnp.int32, (size, a_width), 1)
+        tall = jnp.where(row % a_width == column, 1.0, 0.0).astype(jnp.bfloat16)
+        row = lax.broadcasted_iota(jnp.int32, (n_occ, Q_GROUP * n_occ), 0)
+        column = lax.broadcasted_iota(jnp.int32, (n_occ, Q_GROUP * n_occ), 1)
+        wide = jnp.where(column % n_occ == row, 1.0, 0.0).astype(jnp.bfloat16)
+        rows = jnp.dot(tall, t1_ref[...], preferred_element_type=jnp.float32).astype(jnp.bfloat16)
+        repeated = jnp.dot(rows, wide, preferred_element_type=jnp.float32)
+        row = lax.broadcasted_iota(jnp.int32, repeated.shape, 0)
+        column = lax.broadcasted_iota(jnp.int32, repeated.shape, 1)
+        same = row // a_width == column // n_occ
+        singles_ref[...] = jnp.where(same, repeated, 0.0).astype(jnp.bfloat16)
+
     for group in range(n_q // Q_GROUP):
         rows = slice(group * Q_GROUP, (group + 1) * Q_GROUP)
         occupied = b_oc_ref[rows].reshape(-1, c_width)
@@ -37,8 +62,19 @@
     @pl.when(step == pl.num_programs(0) - 1)
     def _():
         factors = f_ref[...]
-        for half in range(c_width // LANES):
-            for a in range(a_width):
+        by_distance = (
+            own_ref,
+            up_ref.at[0],
+            up2_ref,
+            up_ref.at[1],
+            across_ref,
+            down_ref.at[1],
+            down2_ref,
+            down_ref.at[0],
+        )
+        copies = []
+        for a in range(a_width):
+            for half in range(c_width // LANES):
                 slab = dressed_ref.at[half][pl.ds(a, n_total, stride=a_width), :]
                 part = lax.dot_general(
                     slab.astype(jnp.bfloat16),
@@ -50,38 +86,28 @@
                     ladder_ref[(half * LANES + c_at) // c_block, a * c_block : (a + 1) * c_block, :] = (
                         part[c_at : c_at + c_block]
                     )
-        own_ref, up_ref, up2_ref, across_ref, down2_ref, down_ref = out_refs
-        by_distance = (
-            own_ref,
-            up_ref.at[0],
-            up2_ref,
-            up_ref.at[1],
-            across_ref,
-            down_ref.at[1],
-            down2_ref,
-            down_ref.at[0],
-        )
-        copies = [
-            pltpu.make_async_copy(
-                ladder_ref.at[lax.rem(place_ref[0] + distance, n_pb)], out_ref, sems.at[distance]
-            )
-            for distance, out_ref in enumerate(by_distance)
-        ]
-        for copy in copies:
-            copy.start()
-        for copy in copies:
+            if (a + 1) % A_CHUNK == 0:
+                chunk = a // A_CHUNK
+                rows = pl.ds(chunk * A_CHUNK * c_block, A_CHUNK * c_block)
+                for distance, out_ref in enumerate(by_distance):
+                    copy = pltpu.make_async_copy(
+                        ladder_ref.at[lax.rem(place_ref[0] + distance, n_pb), rows],
+                        out_ref.at[rows],
+                        sems.at[chunk, distance],
+                    )
+                    copy.start()
+                    copies.append(copy)
+        for copy in copies + repeats:
             copy.wait()
 
 
-def contract(b_ac, b_oc, t1, f_bd, place, n_pb):
+def contract(b_ac, b_oc, t1, f_bd, t2, place, n_pb, n_aa):
     n_q, a_width, c_width = b_ac.shape
     n_occ = b_oc.shape[1]
     bd_width = f_bd.shape[1]
     block = (a_width * c_width // n_pb, bd_width)
     pair = (2, *block)
-    shapes = (block, pair, block, block, block, pair)
-    eye = jnp.eye(Q_GROUP, dtype=t1.dtype)
-    singles = jnp.einsum("qr,ka->qark", eye, t1).reshape(Q_GROUP * a_width, Q_GROUP * n_occ)
+    shapes = (block, pair, block, block, block, pair, (n_aa, *t2.shape))
     q_step = n_q // Q_STEPS
     return pl.pallas_call(
         contract_kernel,
@@ -91,19 +117,22 @@
             SMEM,
             pl.BlockSpec((q_step, a_width, c_width), lambda step: (step, 0, 0)),
             pl.BlockSpec((q_step, n_occ, c_width), lambda step: (step, 0, 0)),
-            pl.BlockSpec(singles.shape, lambda step: (0, 0)),
+            pl.BlockSpec((a_width, n_occ), lambda step: (0, 0)),
             pl.BlockSpec(f_bd.shape, lambda step: (0, 0)),
+            pl.BlockSpec(t2.shape, lambda step: (0, 0)),
         ],
         out_specs=[pl.BlockSpec(memory_space=pl.ANY)] * len(shapes),
         scratch_shapes=[
+            pltpu.VMEM((Q_GROUP * a_width, Q_GROUP * n_occ), jnp.bfloat16),
             pltpu.VMEM((c_width // LANES, n_q * a_width, LANES), jnp.float32),
             pltpu.VMEM((n_pb, *block), jnp.bfloat16),
-            pltpu.SemaphoreType.DMA((n_pb,)),
+            pltpu.SemaphoreType.DMA((a_width // A_CHUNK, n_pb)),
+            pltpu.SemaphoreType.DMA((n_aa,)),
         ],
         cost_estimate=pl.CostEstimate(
             flops=2 * n_q * a_width * c_width * bd_width, bytes_accessed=7 << 20, transcendentals=0
         ),
-    )(place, b_ac, b_oc, singles, f_bd)
+    )(place, b_ac, b_oc, t1.T, f_bd, t2)
 
 
 def merge_kernel(core_ref, up_ref, down_ref, across_ref, up2_ref, down2_ref, up_out, down_out):
@@ -188,7 +217,7 @@
     return pl.pallas_call(
         combine_kernel,
         out_shape=jax.ShapeDtypeStruct((pairs, ab_width), jnp.bfloat16),
-        in_specs=[VMEM] * 6,
+        in_specs=[VMEM] * (len(parts) + 1),
         out_specs=VMEM,
         scratch_shapes=[
             pltpu.VMEM((BB // LANE_GROUPS, block_rows, LANES), jnp.float32),
@@ -224,11 +253,10 @@
     place = lax.axis_index("pb").astype(jnp.int32).reshape(1)
     core = lax.rem(lax.axis_index("col"), 2).astype(jnp.int32).reshape(1)
 
-    amplitudes = lax.all_to_all(
-        jnp.broadcast_to(t2[None], (n_aa, *t2.shape)), "aa", 0, 0, tiled=True
-    ).reshape(-1, t2.shape[1])
-
-    own, up, up2, across, down2, down = contract(b_ac, b_oc, t1, f_bd, place, n_pb)
+    own, up, up2, across, down2, down, repeats = contract(
+        b_ac, b_oc, t1, f_bd, t2, place, n_pb, n_aa
+    )
+    amplitudes = lax.all_to_all(repeats, "aa", 0, 0, tiled=True).reshape(-1, t2.shape[1])
     up = along_pb(up, 1)
     down = along_pb(down, -1)
     across = across_pb(across, 2)

time: 104 us -> 102 us (0.981)
  local copies, waits for them, and re-layouts: 5.55 us -> 1.9 us
  Pallas kernels: 7.71 us -> 9.39 us
    broadcast_in_dim x1 -> x0, local copies, waits for them, and re-layouts: 1.87 us -> none  [step(): jnp.broadcast_to(t2[None], (n_aa, *t2.shape))]
    pallas_call x1, Pallas kernels: 6.41 us -> 8.09 us  [contract(): pl.pallas_call(contract_kernel, grid=(Q_STEPS,), out_shape=[jax.ShapeDtyp...]
    unnamed x8 -> x6, local copies, waits for them, and re-layouts: 2.86 us -> 1.9 us
  transfers between devices with their start and end apart: 6 -> 6, of which waited for: 3 -> 3; matrix products, arithmetic and copies ran while one was open for 1% -> 0% of each run, Pallas kernels for 6% -> 0%
where the time goes in v6:
time: 102 us
  starting transfers between devices  37.1 us (36%)
  blocking collectives  27.6 us (27%)
  waiting for transfers between devices  24.9 us (24%)
  Pallas kernels  9.39 us (9%)
  local copies, waits for them, and re-layouts  1.9 us (2%)
    all_to_all x1, blocking collectives, step(): shares = lax.all_to_all(shares, ('col', 'pb'), 0, 0, tiled=True)  27.6 us
    ppermute x4, starting transfers between devices, along_pb(): lax.ppermute(array, 'pb', [(y, (y + distance) % n_pb) for y in range(n_pb)])  17.1 us
    all_to_all x1, starting transfers between devices, step(): lax.all_to_all(repeats, 'aa', 0, 0, tiled=True).reshape(-1, t2.shape[1])  16 us
    ppermute x1, waiting for transfers between devices, across_pb(): return lax.ppermute(array, ('col', 'pb'), pairs)  13.8 us
    ppermute x4, waiting for transfers between devices, along_pb(): lax.ppermute(array, 'pb', [(y, (y + distance) % n_pb) for y in range(n_pb)])  11.2 us
    pallas_call x1, Pallas kernels, contract(): pl.pallas_call(contract_kernel, grid=(Q_STEPS,), out_shape=[jax.ShapeDtyp...  8.09 us
    ppermute x1, starting transfers between devices, across_pb(): return lax.ppermute(array, ('col', 'pb'), pairs)  4.04 us
  transfers between devices with their start and end apart: 6, of which 3 were waited for; matrix products, arithmetic and copies ran while one was open for 0% of the time, Pallas kernels for 0%

profile of v6, /device:TPU:1, one launch (start us, length us, event | category | flops | bytes accessed | tf_op | source)
XLA Modules:
  0.0 101.7 jit_solution(18073095684194223543)
XLA Ops:
  0.0 8.1 %shard_map.55 = (bf16[512,256]{1,0:T(8,128)(2,1)}, bf16[2,512,256]{2,1,0:T(8,128)(2,1)}, bf16[512,256]{1,0:T(8,128)(2,1)}, bf16[512,256]{1,0:T(8,128)(2,1)}, bf1...) custom-call(s32[1]{0:T(128)} %bitcast.place_ref, ...), custom_call_target="tpu_custom_call" | custom-call | flops 402653184 | bytes 7340032 | tf_op jit(solution)/shard_map/pallas_call | solution.py:112
  8.1 0.0 copy-start
  8.1 16.0 %all-to-all-start = ((bf16[32,16,1024]{2,1,0:T(8,128)(2,1)}), bf16[32,16,1024]{2,1,0:T(8,128)(2,1)S(1)}, u32[]{:S(2)}, u32[]{:S(2)}) async-start(bf16[32,16,1024]{2,1,0:T(8,128)(2,1)} %get-tuple-element.28), calls=%async_computation | async-start | bytes 2097152 | tf_op jit(solution)/shard_map/all_to_all | solution.py:259
  24.1 3.3 %collective-permute-start = (bf16[2,512,256]{2,1,0:T(8,128)(2,1)}, bf16[2,512,256]{2,1,0:T(8,128)(2,1)S(1)}, u32[]{:S(2)}, u32[]{:S(2)}) collective-permute-start(bf16[2,512,256]{2,1,0:T(8,128)(2,1)} %get-tuple-element.21), channel_id=1, source_target_pairs={{0,1},{1,2},{2,3},{3,4},{4,5},{5,6},{6,7},{7,0},{8,9},{9,10},{10,1... | collective-permute-start | bytes 1572872 | tf_op jit(solution)/shard_map/ppermute | solution.py:237
  27.4 4.5 %collective-permute-start.1 = (bf16[2,512,256]{2,1,0:T(8,128)(2,1)}, bf16[2,512,256]{2,1,0:T(8,128)(2,1)S(1)}, u32[]{:S(2)}, u32[]{:S(2)}) collective-permute-start(bf16[2,512,256]{2,1,0:T(8,128)(2,1)} %get-tuple-element.22), channel_id=1, source_target_pairs={{0,7},{1,0},{2,1},{3,2},{4,3},{5,4},{6,5},{7,6},{8,15},{9,8},{10,9... | collective-permute-start | bytes 1572872 | tf_op jit(solution)/shard_map/ppermute | solution.py:237
  31.9 4.0 %collective-permute-start.2 = (bf16[512,256]{1,0:T(8,128)(2,1)}, bf16[512,256]{1,0:T(8,128)(2,1)S(1)}, u32[]{:S(2)}, u32[]{:S(2)}) collective-permute-start(bf16[512,256]{1,0:T(8,128)(2,1)} %get-tuple-element.23), channel_id=1, source_target_pairs={{0,2},{1,3},{2,4},{3,5},{4,6},{5,7},{6,0},{7,1},{8,14},{9,15},{10,... | collective-permute-start | bytes 786440 | tf_op jit(solution)/shard_map/ppermute | solution.py:246
  36.0 13.8 %collective-permute-done.2.across_ref = bf16[512,256]{1,0:T(8,128)(2,1)S(1)} collective-permute-done((bf16[512,256]{1,0:T(8,128)(2,1)}, bf16[512,256]{1,0:T(8,128)(2,1)S(1)}, u32[]{:S(2)}, u32[]{:S(2)}) %collective-permute-start.2) | collective-permute-done | bytes 262176 | tf_op jit(solution)/shard_map/ppermute | solution.py:246
  49.8 0.0 collective-permute-done.up_ref
  49.8 0.0 collective-permute-done.1.down_ref
  49.8 0.0 copy-start.1
  49.8 0.9 copy-done.1
  50.7 0.0 copy-start.2
  50.7 0.9 copy-done.2
  51.7 0.2 shard_map.56
  51.9 7.3 %collective-permute-start.3 = (bf16[512,256]{1,0:T(8,128)(2,1)S(1)}, bf16[512,256]{1,0:T(8,128)(2,1)S(1)}, u32[]{:S(2)}, u32[]{:S(2)}) collective-permute-start(bf16[512,256]{1,0:T(8,128)(2,1)S(1)} %get-tuple-element.26), channel_id=1, source_target_pairs={{0,2},{1,3},{2,4},{3,5},{4,6},{5,7},{6,0},{7,1},{8,10},{9,11},{10,... | collective-permute-start | bytes 786440 | tf_op jit(solution)/shard_map/ppermute | solution.py:237
  59.2 1.9 %collective-permute-start.4 = (bf16[512,256]{1,0:T(8,128)(2,1)S(1)}, bf16[512,256]{1,0:T(8,128)(2,1)S(1)}, u32[]{:S(2)}, u32[]{:S(2)}) collective-permute-start(bf16[512,256]{1,0:T(8,128)(2,1)S(1)} %get-tuple-element.27), channel_id=1, source_target_pairs={{0,6},{1,7},{2,0},{3,1},{4,2},{5,3},{6,4},{7,5},{8,14},{9,15},{10,... | collective-permute-start | bytes 786440 | tf_op jit(solution)/shard_map/ppermute | solution.py:237
  61.1 7.7 %collective-permute-done.3.up2_ref = bf16[512,256]{1,0:T(8,128)(2,1)S(1)} collective-permute-done((bf16[512,256]{1,0:T(8,128)(2,1)S(1)}, bf16[512,256]{1,0:T(8,128)(2,1)S(1)}, u32[]{:S(2)}, u32[]{:S(2)}) %collective-permute-start.3) | collective-permute-done | bytes 262176 | tf_op jit(solution)/shard_map/ppermute | solution.py:237
  68.9 3.4 %collective-permute-done.4.down2_ref = bf16[512,256]{1,0:T(8,128)(2,1)S(1)} collective-permute-done((bf16[512,256]{1,0:T(8,128)(2,1)S(1)}, bf16[512,256]{1,0:T(8,128)(2,1)S(1)}, u32[]{:S(2)}, u32[]{:S(2)}) %collective-permute-start.4) | collective-permute-done | bytes 262176 | tf_op jit(solution)/shard_map/ppermute | solution.py:237
  72.3 0.0 all-to-all-done
  72.3 0.0 copy-done
  72.3 1.1 %shard_map.57 = bf16[512,128]{1,0:T(8,128)(2,1)S(1)} custom-call(bf16[512,256]{1,0:T(8,128)(2,1)S(1)} %copy-done, bf16[2,512,256]{2,1,0:T(8,128)(2,1)S(1)} %collective-permute-done.up_ref, bf16[2,512,256]{2,1,0:T(8,128)(2,1)S(1)} %collective-permute-done.1.down_ref, bf16[512,256]{1,0:T(8,128)(2,1)S(1)} %collective-permute-done.3.up2_ref, ...), custom_call_target="tpu_custom_call" | custom-call | flops 134217728 | bytes 3145728 | tf_op jit(solution)/shard_map/pallas_call | solution.py:217
  73.4 27.6 %all_to_all.10 = bf16[32,16,128]{2,1,0:T(8,128)(2,1)S(1)} all-to-all(bf16[32,16,128]{2,1,0:T(8,128)(2,1)S(1)} %bitcast.6), channel_id=1, replica_groups=mesh['aa'=32,'col'=4,'pb'=8] {'col','pb'}, dimensions={0} | all-to-all | bytes 262144 | tf_op jit(solution)/shard_map/all_to_all | solution.py:269
  101.0 0.6 convert_reduce_fusion
Async XLA Ops:
  8.1 64.2 %copy-start = (bf16[512,256]{1,0:T(8,128)(2,1)S(1)}, bf16[512,256]{1,0:T(8,128)(2,1)}, u32[]{:S(2)}) copy-start(bf16[512,256]{1,0:T(8,128)(2,1)} %get-tuple-element.29.own_ref) | copy-start | bytes 786436
  8.1 64.2 %all-to-all-start = ((bf16[32,16,1024]{2,1,0:T(8,128)(2,1)}), bf16[32,16,1024]{2,1,0:T(8,128)(2,1)S(1)}, u32[]{:S(2)}, u32[]{:S(2)}) async-start(bf16[32,16,1024]{2,1,0:T(8,128)(2,1)} %get-tuple-element.28), calls=%async_computation | async-start | bytes 2097152 | tf_op jit(solution)/shard_map/all_to_all | solution.py:259
  24.1 25.7 %collective-permute-start = (bf16[2,512,256]{2,1,0:T(8,128)(2,1)}, bf16[2,512,256]{2,1,0:T(8,128)(2,1)S(1)}, u32[]{:S(2)}, u32[]{:S(2)}) collective-permute-start(bf16[2,512,256]{2,1,0:T(8,128)(2,1)} %get-tuple-element.21), channel_id=1, source_target_pairs={{0,1},{1,2},{2,3},{3,4},{4,5},{5,6},{6,7},{7,0},{8,9},{9,10},{10,1... | collective-permute-start | bytes 1572872 | tf_op jit(solution)/shard_map/ppermute | solution.py:237
  27.4 22.3 %collective-permute-start.1 = (bf16[2,512,256]{2,1,0:T(8,128)(2,1)}, bf16[2,512,256]{2,1,0:T(8,128)(2,1)S(1)}, u32[]{:S(2)}, u32[]{:S(2)}) collective-permute-start(bf16[2,512,256]{2,1,0:T(8,128)(2,1)} %get-tuple-element.22), channel_id=1, source_target_pairs={{0,7},{1,0},{2,1},{3,2},{4,3},{5,4},{6,5},{7,6},{8,15},{9,8},{10,9... | collective-permute-start | bytes 1572872 | tf_op jit(solution)/shard_map/ppermute | solution.py:237
  31.9 17.8 %collective-permute-start.2 = (bf16[512,256]{1,0:T(8,128)(2,1)}, bf16[512,256]{1,0:T(8,128)(2,1)S(1)}, u32[]{:S(2)}, u32[]{:S(2)}) collective-permute-start(bf16[512,256]{1,0:T(8,128)(2,1)} %get-tuple-element.23), channel_id=1, source_target_pairs={{0,2},{1,3},{2,4},{3,5},{4,6},{5,7},{6,0},{7,1},{8,14},{9,15},{10,... | collective-permute-start | bytes 786440 | tf_op jit(solution)/shard_map/ppermute | solution.py:246
  49.8 1.0 copy-start.1
  50.7 0.9 copy-start.2
  51.9 17.0 %collective-permute-start.3 = (bf16[512,256]{1,0:T(8,128)(2,1)S(1)}, bf16[512,256]{1,0:T(8,128)(2,1)S(1)}, u32[]{:S(2)}, u32[]{:S(2)}) collective-permute-start(bf16[512,256]{1,0:T(8,128)(2,1)S(1)} %get-tuple-element.26), channel_id=1, source_target_pairs={{0,2},{1,3},{2,4},{3,5},{4,6},{5,7},{6,0},{7,1},{8,10},{9,11},{10,... | collective-permute-start | bytes 786440 | tf_op jit(solution)/shard_map/ppermute | solution.py:237
  59.2 13.1 %collective-permute-start.4 = (bf16[512,256]{1,0:T(8,128)(2,1)S(1)}, bf16[512,256]{1,0:T(8,128)(2,1)S(1)}, u32[]{:S(2)}, u32[]{:S(2)}) collective-permute-start(bf16[512,256]{1,0:T(8,128)(2,1)S(1)} %get-tuple-element.27), channel_id=1, source_target_pairs={{0,6},{1,7},{2,0},{3,1},{4,2},{5,3},{6,4},{7,5},{8,14},{9,15},{10,... | collective-permute-start | bytes 786440 | tf_op jit(solution)/shard_map/ppermute | solution.py:237

commit v7 on v5

--- a/solution.py
+++ b/solution.py
@@ -11,13 +11,15 @@
 LANES = 128
 LANE_GROUPS = LANES // DB
 Q_GROUP = 8
-Q_STEPS = 6
+Q_STEPS = 4
+A_CHUNK = 4
 VMEM = pl.BlockSpec(memory_space=pltpu.VMEM)
 SMEM = pl.BlockSpec(memory_space=pltpu.SMEM)
 
 
 def contract_kernel(place_ref, b_ac_ref, b_oc_ref, t1_ref, f_ref, *refs):
     out_refs, (singles_ref, dressed_ref, ladder_ref, sems) = refs[:-4], refs[-4:]
+    own_ref, up_ref, up2_ref, across_ref, down2_ref, down_ref = out_refs
     n_q, a_width, c_width = b_ac_ref.shape
     n_total = dressed_ref.shape[1] // a_width
     n_pb, block_rows, _ = ladder_ref.shape
@@ -54,8 +56,19 @@
     @pl.when(step == pl.num_programs(0) - 1)
     def _():
         factors = f_ref[...]
-        for half in range(c_width // LANES):
-            for a in range(a_width):
+        by_distance = (
+            own_ref,
+            up_ref.at[0],
+            up2_ref,
+            up_ref.at[1],
+            across_ref,
+            down_ref.at[1],
+            down2_ref,
+            down_ref.at[0],
+        )
+        copies = []
+        for a in range(a_width):
+            for half in range(c_width // LANES):
                 slab = dressed_ref.at[half][pl.ds(a, n_total, stride=a_width), :]
                 part = lax.dot_general(
                     slab.astype(jnp.bfloat16),
@@ -67,25 +80,17 @@
                     ladder_ref[(half * LANES + c_at) // c_block, a * c_block : (a + 1) * c_block, :] = (
                         part[c_at : c_at + c_block]
                     )
-        own_ref, up_ref, up2_ref, across_ref, down2_ref, down_ref = out_refs
-        by_distance = (
-            own_ref,
-            up_ref.at[0],
-            up2_ref,
-            up_ref.at[1],
-            across_ref,
-            down_ref.at[1],
-            down2_ref,
-            down_ref.at[0],
-        )
-        copies = [
-            pltpu.make_async_copy(
-                ladder_ref.at[lax.rem(place_ref[0] + distance, n_pb)], out_ref, sems.at[distance]
-            )
-            for distance, out_ref in enumerate(by_distance)
-        ]
-        for copy in copies:
-            copy.start()
+            if (a + 1) % A_CHUNK == 0:
+                chunk = a // A_CHUNK
+                rows = pl.ds(chunk * A_CHUNK * c_block, A_CHUNK * c_block)
+                for distance, out_ref in enumerate(by_distance):
+                    copy = pltpu.make_async_copy(
+                        ladder_ref.at[lax.rem(place_ref[0] + distance, n_pb), rows],
+                        out_ref.at[rows],
+                        sems.at[chunk, distance],
+                    )
+                    copy.start()
+                    copies.append(copy)
         for copy in copies:
             copy.wait()
 
@@ -114,7 +119,7 @@
             pltpu.VMEM((Q_GROUP * a_width, Q_GROUP * n_occ), jnp.bfloat16),
             pltpu.VMEM((c_width // LANES, n_q * a_width, LANES), jnp.float32),
             pltpu.VMEM((n_pb, *block), jnp.bfloat16),
-            pltpu.SemaphoreType.DMA((n_pb,)),
+            pltpu.SemaphoreType.DMA((a_width // A_CHUNK, n_pb)),
         ],
         cost_estimate=pl.CostEstimate(
             flops=2 * n_q * a_width * c_width * bd_width, bytes_accessed=7 << 20, transcendentals=0

time: 110 us -> 109 us (level)
  transfers between devices with their start and end apart: 6 -> 6, of which waited for: 4 -> 4; matrix products, arithmetic and copies ran while one was open for 0% -> 0% of each run, Pallas kernels for 7% -> 6%
where the time goes in v7:
time: 109 us; the launch traced here: 108 us
  blocking collectives  38.2 us (35%)
  starting transfers between devices  37.6 us (34%)
  waiting for transfers between devices  19.1 us (18%)
  Pallas kernels  8.02 us (7%)
  local copies, waits for them, and re-layouts  4.7 us (4%)
    all_to_all x1, blocking collectives, step(): shares = lax.all_to_all(shares, ('col', 'pb'), 0, 0, tiled=True)  38.2 us
    ppermute x4, waiting for transfers between devices, along_pb(): lax.ppermute(array, 'pb', [(y, (y + distance) % n_pb) for y in range(n_pb)])  19.1 us
    all_to_all x1, starting transfers between devices, step(): lax.all_to_all(jnp.broadcast_to(t2[None], (n_aa, *t2.shape)), 'aa', 0, 0,...  15.8 us
    ppermute x4, starting transfers between devices, along_pb(): lax.ppermute(array, 'pb', [(y, (y + distance) % n_pb) for y in range(n_pb)])  15.2 us
    pallas_call x1, Pallas kernels, contract(): pl.pallas_call(contract_kernel, grid=(Q_STEPS,), out_shape=[jax.ShapeDtyp...  6.78 us
    ppermute x1, starting transfers between devices, across_pb(): return lax.ppermute(array, ('col', 'pb'), pairs)  6.59 us
    unnamed x6, local copies, waits for them, and re-layouts  2.85 us
  transfers between devices with their start and end apart: 6, of which 4 were waited for; matrix products, arithmetic and copies ran while one was open for 0% of the time, Pallas kernels for 6%

profile of v7, /device:TPU:1, one launch (start us, length us, event | category | flops | bytes accessed | tf_op | source)
XLA Modules:
  0.0 108.4 jit_solution(13136857813013937893)
XLA Ops:
  0.0 1.8 %broadcast_in_dim.2 = bf16[32,16,1024]{2,1,0:T(8,128)(2,1)} broadcast(bf16[16,1024]{1,0:T(8,128)(2,1)} %param.9), dimensions={1,2} | broadcast | bytes 1081344 | tf_op jit(solution)/shard_map/broadcast_in_dim | solution.py:246
  1.8 15.8 %all-to-all-start = ((bf16[32,16,1024]{2,1,0:T(8,128)(2,1)}), bf16[32,16,1024]{2,1,0:T(8,128)(2,1)S(1)}, u32[]{:S(2)}, u32[]{:S(2)}) async-start(bf16[32,16,1024]{2,1,0:T(8,128)(2,1)} %broadcast_in_dim.2), calls=%async_computation | async-start | bytes 2097152 | tf_op jit(solution)/shard_map/all_to_all | solution.py:245
  17.7 6.8 %shard_map.55 = (bf16[512,256]{1,0:T(8,128)(2,1)}, bf16[2,512,256]{2,1,0:T(8,128)(2,1)}, bf16[512,256]{1,0:T(8,128)(2,1)}, bf16[512,256]{1,0:T(8,128)(2,1)}, bf1...) custom-call(s32[1]{0:T(128)} %bitcast.place_ref, bf16[192,16,256]{2,1,0:T(8,128)(2,1)} %b_ac_ref.1, ...), custom_call_target="tpu_custom_call" | custom-call | flops 402653184 | bytes 7340032 | tf_op jit(solution)/shard_map/pallas_call | solution.py:106
  24.5 3.3 %collective-permute-start.1 = (bf16[2,512,256]{2,1,0:T(8,128)(2,1)}, bf16[2,512,256]{2,1,0:T(8,128)(2,1)S(1)}, u32[]{:S(2)}, u32[]{:S(2)}) collective-permute-start(bf16[2,512,256]{2,1,0:T(8,128)(2,1)} %get-tuple-element.22), channel_id=1, source_target_pairs={{0,1},{1,2},{2,3},{3,4},{4,5},{5,6},{6,7},{7,0},{8,9},{9,10},{10,1... | collective-permute-start | bytes 1572872 | tf_op jit(solution)/shard_map/ppermute | solution.py:227
  27.8 4.5 %collective-permute-start.2 = (bf16[2,512,256]{2,1,0:T(8,128)(2,1)}, bf16[2,512,256]{2,1,0:T(8,128)(2,1)S(1)}, u32[]{:S(2)}, u32[]{:S(2)}) collective-permute-start(bf16[2,512,256]{2,1,0:T(8,128)(2,1)} %get-tuple-element.23), channel_id=1, source_target_pairs={{0,7},{1,0},{2,1},{3,2},{4,3},{5,4},{6,5},{7,6},{8,15},{9,8},{10,9... | collective-permute-start | bytes 1572872 | tf_op jit(solution)/shard_map/ppermute | solution.py:227
  32.3 6.6 %collective-permute-start = (bf16[512,256]{1,0:T(8,128)(2,1)}, bf16[512,256]{1,0:T(8,128)(2,1)S(1)}, u32[]{:S(2)}, u32[]{:S(2)}) collective-permute-start(bf16[512,256]{1,0:T(8,128)(2,1)} %get-tuple-element.21), channel_id=1, source_target_pairs={{0,4},{1,5},{2,6},{3,7},{4,0},{5,1},{6,2},{7,3},{8,12},{9,13},{10,... | collective-permute-start | bytes 786440 | tf_op jit(solution)/shard_map/ppermute | solution.py:236
  38.9 2.8 %collective-permute-done.1.up_ref = bf16[2,512,256]{2,1,0:T(8,128)(2,1)S(1)} collective-permute-done((bf16[2,512,256]{2,1,0:T(8,128)(2,1)}, bf16[2,512,256]{2,1,0:T(8,128)(2,1)S(1)}, u32[]{:S(2)}, u32[]{:S(2)}) %collective-permute-start.1) | collective-permute-done | bytes 524320 | tf_op jit(solution)/shard_map/ppermute | solution.py:227
  41.7 2.0 %collective-permute-done.2.down_ref = bf16[2,512,256]{2,1,0:T(8,128)(2,1)S(1)} collective-permute-done((bf16[2,512,256]{2,1,0:T(8,128)(2,1)}, bf16[2,512,256]{2,1,0:T(8,128)(2,1)S(1)}, u32[]{:S(2)}, u32[]{:S(2)}) %collective-permute-start.2) | collective-permute-done | bytes 524320 | tf_op jit(solution)/shard_map/ppermute | solution.py:227
  43.7 0.0 copy-start.1
  43.7 0.9 copy-done.1
  44.6 0.0 copy-start.2
  44.6 0.9 copy-done.2
  45.6 0.1 shard_map.56
  45.7 4.4 %collective-permute-start.3 = (bf16[512,256]{1,0:T(8,128)(2,1)S(1)}, bf16[512,256]{1,0:T(8,128)(2,1)S(1)}, u32[]{:S(2)}, u32[]{:S(2)}) collective-permute-start(bf16[512,256]{1,0:T(8,128)(2,1)S(1)} %get-tuple-element.26), channel_id=1, source_target_pairs={{0,2},{1,3},{2,4},{3,5},{4,6},{5,7},{6,0},{7,1},{8,10},{9,11},{10,... | collective-permute-start | bytes 786440 | tf_op jit(solution)/shard_map/ppermute | solution.py:227
  50.1 3.0 %collective-permute-start.4 = (bf16[512,256]{1,0:T(8,128)(2,1)S(1)}, bf16[512,256]{1,0:T(8,128)(2,1)S(1)}, u32[]{:S(2)}, u32[]{:S(2)}) collective-permute-start(bf16[512,256]{1,0:T(8,128)(2,1)S(1)} %get-tuple-element.27), channel_id=1, source_target_pairs={{0,6},{1,7},{2,0},{3,1},{4,2},{5,3},{6,4},{7,5},{8,14},{9,15},{10,... | collective-permute-start | bytes 786440 | tf_op jit(solution)/shard_map/ppermute | solution.py:227
  53.1 0.0 collective-permute-done.across_ref
  53.1 7.7 %collective-permute-done.3.up2_ref = bf16[512,256]{1,0:T(8,128)(2,1)S(1)} collective-permute-done((bf16[512,256]{1,0:T(8,128)(2,1)S(1)}, bf16[512,256]{1,0:T(8,128)(2,1)S(1)}, u32[]{:S(2)}, u32[]{:S(2)}) %collective-permute-start.3) | collective-permute-done | bytes 262176 | tf_op jit(solution)/shard_map/ppermute | solution.py:227
  60.8 6.6 %collective-permute-done.4.down2_ref = bf16[512,256]{1,0:T(8,128)(2,1)S(1)} collective-permute-done((bf16[512,256]{1,0:T(8,128)(2,1)S(1)}, bf16[512,256]{1,0:T(8,128)(2,1)S(1)}, u32[]{:S(2)}, u32[]{:S(2)}) %collective-permute-start.4) | collective-permute-done | bytes 262176 | tf_op jit(solution)/shard_map/ppermute | solution.py:227
  67.5 0.0 all-to-all-done
  67.5 0.0 copy-start
  67.5 0.9 copy-done
  68.4 1.1 %shard_map.57 = bf16[512,128]{1,0:T(8,128)(2,1)S(1)} custom-call(bf16[512,256]{1,0:T(8,128)(2,1)S(1)} %copy-done, bf16[512,256]{1,0:T(8,128)(2,1)S(1)} %collective-permute-done.across_ref, bf16[2,512,256]{2,1,0:T(8,128)(2,1)S(1)} %collective-permute-done.1.up_ref, bf16[2,512,256]{2,1,0:T(8,128)(2,1)S(1)} %collective-permute-done.2.down_ref, ...), custom_call_target="tpu_custom_call" | custom-call | flops 134217728 | bytes 3145728 | tf_op jit(solution)/shard_map/pallas_call | solution.py:207
  69.5 38.2 %all_to_all.10 = bf16[32,16,128]{2,1,0:T(8,128)(2,1)S(1)} all-to-all(bf16[32,16,128]{2,1,0:T(8,128)(2,1)S(1)} %bitcast.5), channel_id=1, replica_groups=mesh['aa'=32,'col'=4,'pb'=8] {'col','pb'}, dimensions={0} | all-to-all | bytes 262144 | tf_op jit(solution)/shard_map/all_to_all | solution.py:261
  107.8 0.6 convert_reduce_fusion
Async XLA Ops:
  1.8 65.6 %all-to-all-start = ((bf16[32,16,1024]{2,1,0:T(8,128)(2,1)}), bf16[32,16,1024]{2,1,0:T(8,128)(2,1)S(1)}, u32[]{:S(2)}, u32[]{:S(2)}) async-start(bf16[32,16,1024]{2,1,0:T(8,128)(2,1)} %broadcast_in_dim.2), calls=%async_computation | async-start | bytes 2097152 | tf_op jit(solution)/shard_map/all_to_all | solution.py:245
  24.5 17.2 %collective-permute-start.1 = (bf16[2,512,256]{2,1,0:T(8,128)(2,1)}, bf16[2,512,256]{2,1,0:T(8,128)(2,1)S(1)}, u32[]{:S(2)}, u32[]{:S(2)}) collective-permute-start(bf16[2,512,256]{2,1,0:T(8,128)(2,1)} %get-tuple-element.22), channel_id=1, source_target_pairs={{0,1},{1,2},{2,3},{3,4},{4,5},{5,6},{6,7},{7,0},{8,9},{9,10},{10,1... | collective-permute-start | bytes 1572872 | tf_op jit(solution)/shard_map/ppermute | solution.py:227
  27.8 15.9 %collective-permute-start.2 = (bf16[2,512,256]{2,1,0:T(8,128)(2,1)}, bf16[2,512,256]{2,1,0:T(8,128)(2,1)S(1)}, u32[]{:S(2)}, u32[]{:S(2)}) collective-permute-start(bf16[2,512,256]{2,1,0:T(8,128)(2,1)} %get-tuple-element.23), channel_id=1, source_target_pairs={{0,7},{1,0},{2,1},{3,2},{4,3},{5,4},{6,5},{7,6},{8,15},{9,8},{10,9... | collective-permute-start | bytes 1572872 | tf_op jit(solution)/shard_map/ppermute | solution.py:227
  32.3 20.8 %collective-permute-start = (bf16[512,256]{1,0:T(8,128)(2,1)}, bf16[512,256]{1,0:T(8,128)(2,1)S(1)}, u32[]{:S(2)}, u32[]{:S(2)}) collective-permute-start(bf16[512,256]{1,0:T(8,128)(2,1)} %get-tuple-element.21), channel_id=1, source_target_pairs={{0,4},{1,5},{2,6},{3,7},{4,0},{5,1},{6,2},{7,3},{8,12},{9,13},{10,... | collective-permute-start | bytes 786440 | tf_op jit(solution)/shard_map/ppermute | solution.py:236
  43.7 0.9 copy-start.1
  44.6 0.9 copy-start.2
  45.7 15.1 %collective-permute-start.3 = (bf16[512,256]{1,0:T(8,128)(2,1)S(1)}, bf16[512,256]{1,0:T(8,128)(2,1)S(1)}, u32[]{:S(2)}, u32[]{:S(2)}) collective-permute-start(bf16[512,256]{1,0:T(8,128)(2,1)S(1)} %get-tuple-element.26), channel_id=1, source_target_pairs={{0,2},{1,3},{2,4},{3,5},{4,6},{5,7},{6,0},{7,1},{8,10},{9,11},{10,... | collective-permute-start | bytes 786440 | tf_op jit(solution)/shard_map/ppermute | solution.py:227
  50.1 17.4 %collective-permute-start.4 = (bf16[512,256]{1,0:T(8,128)(2,1)S(1)}, bf16[512,256]{1,0:T(8,128)(2,1)S(1)}, u32[]{:S(2)}, u32[]{:S(2)}) collective-permute-start(bf16[512,256]{1,0:T(8,128)(2,1)S(1)} %get-tuple-element.27), channel_id=1, source_target_pairs={{0,6},{1,7},{2,0},{3,1},{4,2},{5,3},{6,4},{7,5},{8,14},{9,15},{10,... | collective-permute-start | bytes 786440 | tf_op jit(solution)/shard_map/ppermute | solution.py:227
  67.5 1.0 copy-start

commit v8 on v7

--- a/solution.py
+++ b/solution.py
@@ -66,6 +66,7 @@
             down2_ref,
             down_ref.at[0],
         )
+        here, way = place_ref[0] % n_pb, 1 - 2 * (place_ref[0] // n_pb)
         copies = []
         for a in range(a_width):
             for half in range(c_width // LANES):
@@ -85,7 +86,7 @@
                 rows = pl.ds(chunk * A_CHUNK * c_block, A_CHUNK * c_block)
                 for distance, out_ref in enumerate(by_distance):
                     copy = pltpu.make_async_copy(
-                        ladder_ref.at[lax.rem(place_ref[0] + distance, n_pb), rows],
+                        ladder_ref.at[lax.rem(here + way * distance + n_pb, n_pb), rows],
                         out_ref.at[rows],
                         sems.at[chunk, distance],
                     )
@@ -224,11 +225,6 @@
 
 def along_pb(array, distance):
     n_pb = lax.axis_size("pb")
-    return lax.ppermute(array, "pb", [(y, (y + distance) % n_pb) for y in range(n_pb)])
-
-
-def across_pb(array, distance):
-    n_pb = lax.axis_size("pb")
     pairs = []
     for col in range(lax.axis_size("col")):
         way = -distance if col % 2 else distance
@@ -240,7 +236,8 @@
     n_aa = lax.axis_size("aa")
     n_pb = lax.axis_size("pb")
     n_out = lax.axis_size("col") * n_pb
-    place = lax.axis_index("pb").astype(jnp.int32).reshape(1)
+    core = lax.rem(lax.axis_index("col"), 2)
+    place = (core * n_pb + lax.axis_index("pb")).astype(jnp.int32).reshape(1)
 
     amplitudes = lax.all_to_all(
         jnp.broadcast_to(t2[None], (n_aa, *t2.shape)), "aa", 0, 0, tiled=True
@@ -249,7 +246,7 @@
     own, up, up2, across, down2, down = contract(b_ac, b_oc, t1, f_bd, place, n_pb)
     up = along_pb(up, 1)
     down = along_pb(down, -1)
-    across = across_pb(across, 4)
+    across = along_pb(across, 4)
     up2, down2 = merge(up, down, up2, down2)
     up2 = along_pb(up2, 2)
     down2 = along_pb(down2, -2)

time: 109 us -> 108 us (level)
  the two profiles are of different devices: /device:TPU:1 before, /device:TPU:3 now
where the time goes in v8:
time: 108 us; the launch traced here: 107 us
  starting transfers between devices  39.3 us (36%)
  blocking collectives  29.5 us (27%)
  waiting for transfers between devices  25.1 us (23%)
  Pallas kernels  8.05 us (7%)
  local copies, waits for them, and re-layouts  4.7 us (4%)
    all_to_all x1, blocking collectives, step(): shares = lax.all_to_all(shares, ('col', 'pb'), 0, 0, tiled=True)  29.5 us
    ppermute x5, waiting for transfers between devices, along_pb(): return lax.ppermute(array, ('col', 'pb'), pairs)  25.1 us
    ppermute x5, starting transfers between devices, along_pb(): return lax.ppermute(array, ('col', 'pb'), pairs)  24.3 us
    all_to_all x1, starting transfers between devices, step(): lax.all_to_all(jnp.broadcast_to(t2[None], (n_aa, *t2.shape)), 'aa', 0, 0,...  15 us
    pallas_call x1, Pallas kernels, contract(): pl.pallas_call(contract_kernel, grid=(Q_STEPS,), out_shape=[jax.ShapeDtyp...  6.82 us
    unnamed x6, local copies, waits for them, and re-layouts  2.85 us
  transfers between devices with their start and end apart: 6, of which 4 were waited for; matrix products, arithmetic and copies ran while one was open for 0% of the time, Pallas kernels for 6%

profile of v8, /device:TPU:3, one launch (start us, length us, event | category | flops | bytes accessed | tf_op | source)
XLA Modules:
  0.0 107.4 jit_solution(4938815165702434363)
XLA Ops:
  0.0 1.8 %broadcast_in_dim.2 = bf16[32,16,1024]{2,1,0:T(8,128)(2,1)} broadcast(bf16[16,1024]{1,0:T(8,128)(2,1)} %param.9), dimensions={1,2} | broadcast | bytes 1081344 | tf_op jit(solution)/shard_map/broadcast_in_dim | solution.py:243
  1.8 15.0 %all-to-all-start = ((bf16[32,16,1024]{2,1,0:T(8,128)(2,1)}), bf16[32,16,1024]{2,1,0:T(8,128)(2,1)S(1)}, u32[]{:S(2)}, u32[]{:S(2)}) async-start(bf16[32,16,1024]{2,1,0:T(8,128)(2,1)} %broadcast_in_dim.2), calls=%async_computation | async-start | bytes 2097152 | tf_op jit(solution)/shard_map/all_to_all | solution.py:242
  16.9 6.8 %shard_map.55 = (bf16[512,256]{1,0:T(8,128)(2,1)}, bf16[2,512,256]{2,1,0:T(8,128)(2,1)}, bf16[512,256]{1,0:T(8,128)(2,1)}, bf16[512,256]{1,0:T(8,128)(2,1)}, bf1...) custom-call(s32[1]{0:T(128)} %bitcast.place_ref, bf16[192,16,256]{2,1,0:T(8,128)(2,1)} %b_ac_ref.1, ...), custom_call_target="tpu_custom_call" | custom-call | flops 402653184 | bytes 7340032 | tf_op jit(solution)/shard_map/pallas_call | solution.py:107
  23.7 5.9 %collective-permute-start.1 = (bf16[2,512,256]{2,1,0:T(8,128)(2,1)}, bf16[2,512,256]{2,1,0:T(8,128)(2,1)S(1)}, u32[]{:S(2)}, u32[]{:S(2)}) collective-permute-start(bf16[2,512,256]{2,1,0:T(8,128)(2,1)} %get-tuple-element.22), channel_id=1, source_target_pairs={{0,1},{1,2},{2,3},{3,4},{4,5},{5,6},{6,7},{7,0},{8,15},{9,8},{10,9... | collective-permute-start | bytes 1572872 | tf_op jit(solution)/shard_map/ppermute | solution.py:232
  29.6 1.9 %collective-permute-start.2 = (bf16[2,512,256]{2,1,0:T(8,128)(2,1)}, bf16[2,512,256]{2,1,0:T(8,128)(2,1)S(1)}, u32[]{:S(2)}, u32[]{:S(2)}) collective-permute-start(bf16[2,512,256]{2,1,0:T(8,128)(2,1)} %get-tuple-element.23), channel_id=1, source_target_pairs={{0,7},{1,0},{2,1},{3,2},{4,3},{5,4},{6,5},{7,6},{8,9},{9,10},{10,1... | collective-permute-start | bytes 1572872 | tf_op jit(solution)/shard_map/ppermute | solution.py:232
  31.6 5.4 %collective-permute-start = (bf16[512,256]{1,0:T(8,128)(2,1)}, bf16[512,256]{1,0:T(8,128)(2,1)S(1)}, u32[]{:S(2)}, u32[]{:S(2)}) collective-permute-start(bf16[512,256]{1,0:T(8,128)(2,1)} %get-tuple-element.21), channel_id=1, source_target_pairs={{0,4},{1,5},{2,6},{3,7},{4,0},{5,1},{6,2},{7,3},{8,12},{9,13},{10,... | collective-permute-start | bytes 786440 | tf_op jit(solution)/shard_map/ppermute | solution.py:232
  37.0 1.0 collective-permute-done.1.up_ref
  37.9 5.9 %collective-permute-done.2.down_ref = bf16[2,512,256]{2,1,0:T(8,128)(2,1)S(1)} collective-permute-done((bf16[2,512,256]{2,1,0:T(8,128)(2,1)}, bf16[2,512,256]{2,1,0:T(8,128)(2,1)S(1)}, u32[]{:S(2)}, u32[]{:S(2)}) %collective-permute-start.2) | collective-permute-done | bytes 524320 | tf_op jit(solution)/shard_map/ppermute | solution.py:232
  43.8 0.0 copy-start.1
  43.8 0.9 copy-done.1
  44.8 0.0 copy-start.2
  44.8 0.9 copy-done.2
  45.7 0.1 shard_map.56
  45.9 4.7 %collective-permute-start.3 = (bf16[512,256]{1,0:T(8,128)(2,1)S(1)}, bf16[512,256]{1,0:T(8,128)(2,1)S(1)}, u32[]{:S(2)}, u32[]{:S(2)}) collective-permute-start(bf16[512,256]{1,0:T(8,128)(2,1)S(1)} %get-tuple-element.26), channel_id=1, source_target_pairs={{0,2},{1,3},{2,4},{3,5},{4,6},{5,7},{6,0},{7,1},{8,14},{9,15},{10,... | collective-permute-start | bytes 786440 | tf_op jit(solution)/shard_map/ppermute | solution.py:232
  50.6 6.4 %collective-permute-start.4 = (bf16[512,256]{1,0:T(8,128)(2,1)S(1)}, bf16[512,256]{1,0:T(8,128)(2,1)S(1)}, u32[]{:S(2)}, u32[]{:S(2)}) collective-permute-start(bf16[512,256]{1,0:T(8,128)(2,1)S(1)} %get-tuple-element.27), channel_id=1, source_target_pairs={{0,6},{1,7},{2,0},{3,1},{4,2},{5,3},{6,4},{7,5},{8,10},{9,11},{10,... | collective-permute-start | bytes 786440 | tf_op jit(solution)/shard_map/ppermute | solution.py:232
  57.0 0.0 collective-permute-done.across_ref
  57.0 1.9 %collective-permute-done.3.up2_ref = bf16[512,256]{1,0:T(8,128)(2,1)S(1)} collective-permute-done((bf16[512,256]{1,0:T(8,128)(2,1)S(1)}, bf16[512,256]{1,0:T(8,128)(2,1)S(1)}, u32[]{:S(2)}, u32[]{:S(2)}) %collective-permute-start.3) | collective-permute-done | bytes 262176 | tf_op jit(solution)/shard_map/ppermute | solution.py:232
  58.9 16.3 %collective-permute-done.4.down2_ref = bf16[512,256]{1,0:T(8,128)(2,1)S(1)} collective-permute-done((bf16[512,256]{1,0:T(8,128)(2,1)S(1)}, bf16[512,256]{1,0:T(8,128)(2,1)S(1)}, u32[]{:S(2)}, u32[]{:S(2)}) %collective-permute-start.4) | collective-permute-done | bytes 262176 | tf_op jit(solution)/shard_map/ppermute | solution.py:232
  75.2 0.0 all-to-all-done
  75.2 0.0 copy-start
  75.2 0.9 copy-done
  76.1 1.1 %shard_map.57 = bf16[512,128]{1,0:T(8,128)(2,1)S(1)} custom-call(bf16[512,256]{1,0:T(8,128)(2,1)S(1)} %copy-done, bf16[512,256]{1,0:T(8,128)(2,1)S(1)} %collective-permute-done.across_ref, bf16[2,512,256]{2,1,0:T(8,128)(2,1)S(1)} %collective-permute-done.1.up_ref, bf16[2,512,256]{2,1,0:T(8,128)(2,1)S(1)} %collective-permute-done.2.down_ref, ...), custom_call_target="tpu_custom_call" | custom-call | flops 134217728 | bytes 3145728 | tf_op jit(solution)/shard_map/pallas_call | solution.py:208
  77.3 29.5 %all_to_all.10 = bf16[32,16,128]{2,1,0:T(8,128)(2,1)S(1)} all-to-all(bf16[32,16,128]{2,1,0:T(8,128)(2,1)S(1)} %bitcast.5), channel_id=1, replica_groups=mesh['aa'=32,'col'=4,'pb'=8] {'col','pb'}, dimensions={0} | all-to-all | bytes 262144 | tf_op jit(solution)/shard_map/all_to_all | solution.py:258
  106.8 0.6 convert_reduce_fusion
Async XLA Ops:
  1.8 73.3 %all-to-all-start = ((bf16[32,16,1024]{2,1,0:T(8,128)(2,1)}), bf16[32,16,1024]{2,1,0:T(8,128)(2,1)S(1)}, u32[]{:S(2)}, u32[]{:S(2)}) async-start(bf16[32,16,1024]{2,1,0:T(8,128)(2,1)} %broadcast_in_dim.2), calls=%async_computation | async-start | bytes 2097152 | tf_op jit(solution)/shard_map/all_to_all | solution.py:242
  23.7 14.2 %collective-permute-start.1 = (bf16[2,512,256]{2,1,0:T(8,128)(2,1)}, bf16[2,512,256]{2,1,0:T(8,128)(2,1)S(1)}, u32[]{:S(2)}, u32[]{:S(2)}) collective-permute-start(bf16[2,512,256]{2,1,0:T(8,128)(2,1)} %get-tuple-element.22), channel_id=1, source_target_pairs={{0,1},{1,2},{2,3},{3,4},{4,5},{5,6},{6,7},{7,0},{8,15},{9,8},{10,9... | collective-permute-start | bytes 1572872 | tf_op jit(solution)/shard_map/ppermute | solution.py:232
  29.6 14.2 %collective-permute-start.2 = (bf16[2,512,256]{2,1,0:T(8,128)(2,1)}, bf16[2,512,256]{2,1,0:T(8,128)(2,1)S(1)}, u32[]{:S(2)}, u32[]{:S(2)}) collective-permute-start(bf16[2,512,256]{2,1,0:T(8,128)(2,1)} %get-tuple-element.23), channel_id=1, source_target_pairs={{0,7},{1,0},{2,1},{3,2},{4,3},{5,4},{6,5},{7,6},{8,9},{9,10},{10,1... | collective-permute-start | bytes 1572872 | tf_op jit(solution)/shard_map/ppermute | solution.py:232
  31.6 25.4 %collective-permute-start = (bf16[512,256]{1,0:T(8,128)(2,1)}, bf16[512,256]{1,0:T(8,128)(2,1)S(1)}, u32[]{:S(2)}, u32[]{:S(2)}) collective-permute-start(bf16[512,256]{1,0:T(8,128)(2,1)} %get-tuple-element.21), channel_id=1, source_target_pairs={{0,4},{1,5},{2,6},{3,7},{4,0},{5,1},{6,2},{7,3},{8,12},{9,13},{10,... | collective-permute-start | bytes 786440 | tf_op jit(solution)/shard_map/ppermute | solution.py:232
  43.8 1.0 copy-start.1
  44.8 0.9 copy-start.2
  45.9 13.0 %collective-permute-start.3 = (bf16[512,256]{1,0:T(8,128)(2,1)S(1)}, bf16[512,256]{1,0:T(8,128)(2,1)S(1)}, u32[]{:S(2)}, u32[]{:S(2)}) collective-permute-start(bf16[512,256]{1,0:T(8,128)(2,1)S(1)} %get-tuple-element.26), channel_id=1, source_target_pairs={{0,2},{1,3},{2,4},{3,5},{4,6},{5,7},{6,0},{7,1},{8,14},{9,15},{10,... | collective-permute-start | bytes 786440 | tf_op jit(solution)/shard_map/ppermute | solution.py:232
  50.6 24.6 %collective-permute-start.4 = (bf16[512,256]{1,0:T(8,128)(2,1)S(1)}, bf16[512,256]{1,0:T(8,128)(2,1)S(1)}, u32[]{:S(2)}, u32[]{:S(2)}) collective-permute-start(bf16[512,256]{1,0:T(8,128)(2,1)S(1)} %get-tuple-element.27), channel_id=1, source_target_pairs={{0,6},{1,7},{2,0},{3,1},{4,2},{5,3},{6,4},{7,5},{8,10},{9,11},{10,... | collective-permute-start | bytes 786440 | tf_op jit(solution)/shard_map/ppermute | solution.py:232
  75.2 1.0 copy-start

commit v9 on v8

--- a/solution.py
+++ b/solution.py
@@ -17,9 +17,9 @@
 SMEM = pl.BlockSpec(memory_space=pltpu.SMEM)
 
 
-def contract_kernel(place_ref, b_ac_ref, b_oc_ref, t1_ref, f_ref, *refs):
-    out_refs, (singles_ref, dressed_ref, ladder_ref, sems) = refs[:-4], refs[-4:]
-    own_ref, up_ref, up2_ref, across_ref, down2_ref, down_ref = out_refs
+def contract_kernel(place_ref, b_ac_ref, b_oc_ref, t1_ref, f_ref, t2_ref, *refs):
+    out_refs, (singles_ref, dressed_ref, ladder_ref, sems, t2_sems) = refs[:-5], refs[-5:]
+    own_ref, up_ref, up2_ref, across_ref, down2_ref, down_ref, repeats_ref = out_refs
     n_q, a_width, c_width = b_ac_ref.shape
     n_total = dressed_ref.shape[1] // a_width
     n_pb, block_rows, _ = ladder_ref.shape
@@ -66,6 +66,12 @@
             down2_ref,
             down_ref.at[0],
         )
+        repeats = [
+            pltpu.make_async_copy(t2_ref, repeats_ref.at[at], t2_sems.at[at])
+            for at in range(repeats_ref.shape[0])
+        ]
+        for copy in repeats:
+            copy.start()
         here, way = place_ref[0] % n_pb, 1 - 2 * (place_ref[0] // n_pb)
         copies = []
         for a in range(a_width):
@@ -92,17 +98,17 @@
                     )
                     copy.start()
                     copies.append(copy)
-        for copy in copies:
+        for copy in copies + repeats:
             copy.wait()
 
 
-def contract(b_ac, b_oc, t1, f_bd, place, n_pb):
+def contract(b_ac, b_oc, t1, f_bd, t2, place, n_pb, n_aa):
     n_q, a_width, c_width = b_ac.shape
     n_occ = b_oc.shape[1]
     bd_width = f_bd.shape[1]
     block = (a_width * c_width // n_pb, bd_width)
     pair = (2, *block)
-    shapes = (block, pair, block, block, block, pair)
+    shapes = (block, pair, block, block, block, pair, (n_aa, *t2.shape))
     q_step = n_q // Q_STEPS
     return pl.pallas_call(
         contract_kernel,
@@ -114,6 +120,7 @@
             pl.BlockSpec((q_step, n_occ, c_width), lambda step: (step, 0, 0)),
             pl.BlockSpec((a_width, n_occ), lambda step: (0, 0)),
             pl.BlockSpec(f_bd.shape, lambda step: (0, 0)),
+            pl.BlockSpec(t2.shape, lambda step: (0, 0)),
         ],
         out_specs=[pl.BlockSpec(memory_space=pl.ANY)] * len(shapes),
         scratch_shapes=[
@@ -121,11 +128,12 @@
             pltpu.VMEM((c_width // LANES, n_q * a_width, LANES), jnp.float32),
             pltpu.VMEM((n_pb, *block), jnp.bfloat16),
             pltpu.SemaphoreType.DMA((a_width // A_CHUNK, n_pb)),
+            pltpu.SemaphoreType.DMA((n_aa,)),
         ],
         cost_estimate=pl.CostEstimate(
             flops=2 * n_q * a_width * c_width * bd_width, bytes_accessed=7 << 20, transcendentals=0
         ),
-    )(place, b_ac, b_oc, t1.T, f_bd)
+    )(place, b_ac, b_oc, t1.T, f_bd, t2)
 
 
 def merge_kernel(up_ref, down_ref, up2_ref, down2_ref, up_out, down_out):
@@ -239,11 +247,10 @@
     core = lax.rem(lax.axis_index("col"), 2)
     place = (core * n_pb + lax.axis_index("pb")).astype(jnp.int32).reshape(1)
 
-    amplitudes = lax.all_to_all(
-        jnp.broadcast_to(t2[None], (n_aa, *t2.shape)), "aa", 0, 0, tiled=True
-    ).reshape(-1, t2.shape[1])
-
-    own, up, up2, across, down2, down = contract(b_ac, b_oc, t1, f_bd, place, n_pb)
+    own, up, up2, across, down2, down, repeats = contract(
+        b_ac, b_oc, t1, f_bd, t2, place, n_pb, n_aa
+    )
+    amplitudes = lax.all_to_all(repeats, "aa", 0, 0, tiled=True).reshape(-1, t2.shape[1])
     up = along_pb(up, 1)
     down = along_pb(down, -1)
     across = along_pb(across, 4)

time: 108 us -> 106 us (0.981)
  local copies, waits for them, and re-layouts: 4.7 us -> 1.9 us
    broadcast_in_dim x1 -> x0, local copies, waits for them, and re-layouts: 1.85 us -> none  [step(): jnp.broadcast_to(t2[None], (n_aa, *t2.shape))]
  transfers between devices with their start and end apart: 6 -> 6, of which waited for: 4 -> 4; matrix products, arithmetic and copies ran while one was open for 0% -> 0% of each run, Pallas kernels for 6% -> 0%
where the time goes in v9:
time: 106 us; the launch traced here: 105 us
  starting transfers between devices  39.4 us (37%)
  blocking collectives  29.5 us (28%)
  waiting for transfers between devices  25.1 us (24%)
  Pallas kernels  8.66 us (8%)
  local copies, waits for them, and re-layouts  1.9 us (2%)
    all_to_all x1, blocking collectives, step(): shares = lax.all_to_all(shares, ('col', 'pb'), 0, 0, tiled=True)  29.5 us
    ppermute x5, waiting for transfers between devices, along_pb(): return lax.ppermute(array, ('col', 'pb'), pairs)  25.1 us
    ppermute x5, starting transfers between devices, along_pb(): return lax.ppermute(array, ('col', 'pb'), pairs)  24.3 us
    all_to_all x1, starting transfers between devices, step(): lax.all_to_all(repeats, 'aa', 0, 0, tiled=True).reshape(-1, t2.shape[1])  15.2 us
    pallas_call x1, Pallas kernels, contract(): pl.pallas_call(contract_kernel, grid=(Q_STEPS,), out_shape=[jax.ShapeDtyp...  7.42 us
  transfers between devices with their start and end apart: 6, of which 4 were waited for; matrix products, arithmetic and copies ran while one was open for 0% of the time, Pallas kernels for 0%

profile of v9, /device:TPU:3, one launch (start us, length us, event | category | flops | bytes accessed | tf_op | source)
XLA Modules:
  0.0 105.4 jit_solution(7477400062874506629)
XLA Ops:
  0.0 7.4 %shard_map.55 = (bf16[512,256]{1,0:T(8,128)(2,1)}, bf16[2,512,256]{2,1,0:T(8,128)(2,1)}, bf16[512,256]{1,0:T(8,128)(2,1)}, bf16[512,256]{1,0:T(8,128)(2,1)}, bf1...) custom-call(s32[1]{0:T(128)} %bitcast.place_ref, ...), custom_call_target="tpu_custom_call" | custom-call | flops 402653184 | bytes 7340032 | tf_op jit(solution)/shard_map/pallas_call | solution.py:113
  7.4 0.0 copy-start
  7.4 15.2 %all-to-all-start = ((bf16[32,16,1024]{2,1,0:T(8,128)(2,1)}), bf16[32,16,1024]{2,1,0:T(8,128)(2,1)S(1)}, u32[]{:S(2)}, u32[]{:S(2)}) async-start(bf16[32,16,1024]{2,1,0:T(8,128)(2,1)} %get-tuple-element.29), calls=%async_computation | async-start | bytes 2097152 | tf_op jit(solution)/shard_map/all_to_all | solution.py:253
  22.6 5.9 %collective-permute-start.1 = (bf16[2,512,256]{2,1,0:T(8,128)(2,1)}, bf16[2,512,256]{2,1,0:T(8,128)(2,1)S(1)}, u32[]{:S(2)}, u32[]{:S(2)}) collective-permute-start(bf16[2,512,256]{2,1,0:T(8,128)(2,1)} %get-tuple-element.23), channel_id=1, source_target_pairs={{0,1},{1,2},{2,3},{3,4},{4,5},{5,6},{6,7},{7,0},{8,15},{9,8},{10,9... | collective-permute-start | bytes 1572872 | tf_op jit(solution)/shard_map/ppermute | solution.py:240
  28.5 1.9 %collective-permute-start.2 = (bf16[2,512,256]{2,1,0:T(8,128)(2,1)}, bf16[2,512,256]{2,1,0:T(8,128)(2,1)S(1)}, u32[]{:S(2)}, u32[]{:S(2)}) collective-permute-start(bf16[2,512,256]{2,1,0:T(8,128)(2,1)} %get-tuple-element.24), channel_id=1, source_target_pairs={{0,7},{1,0},{2,1},{3,2},{4,3},{5,4},{6,5},{7,6},{8,9},{9,10},{10,1... | collective-permute-start | bytes 1572872 | tf_op jit(solution)/shard_map/ppermute | solution.py:240
  30.5 5.4 %collective-permute-start = (bf16[512,256]{1,0:T(8,128)(2,1)}, bf16[512,256]{1,0:T(8,128)(2,1)S(1)}, u32[]{:S(2)}, u32[]{:S(2)}) collective-permute-start(bf16[512,256]{1,0:T(8,128)(2,1)} %get-tuple-element.22), channel_id=1, source_target_pairs={{0,4},{1,5},{2,6},{3,7},{4,0},{5,1},{6,2},{7,3},{8,12},{9,13},{10,... | collective-permute-start | bytes 786440 | tf_op jit(solution)/shard_map/ppermute | solution.py:240
  35.8 1.0 collective-permute-done.1.up_ref
  36.8 5.9 %collective-permute-done.2.down_ref = bf16[2,512,256]{2,1,0:T(8,128)(2,1)S(1)} collective-permute-done((bf16[2,512,256]{2,1,0:T(8,128)(2,1)}, bf16[2,512,256]{2,1,0:T(8,128)(2,1)S(1)}, u32[]{:S(2)}, u32[]{:S(2)}) %collective-permute-start.2) | collective-permute-done | bytes 524320 | tf_op jit(solution)/shard_map/ppermute | solution.py:240
  42.7 0.0 copy-start.1
  42.7 0.9 copy-done.1
  43.7 0.0 copy-start.2
  43.7 0.9 copy-done.2
  44.6 0.1 shard_map.56
  44.8 4.7 %collective-permute-start.3 = (bf16[512,256]{1,0:T(8,128)(2,1)S(1)}, bf16[512,256]{1,0:T(8,128)(2,1)S(1)}, u32[]{:S(2)}, u32[]{:S(2)}) collective-permute-start(bf16[512,256]{1,0:T(8,128)(2,1)S(1)} %get-tuple-element.27), channel_id=1, source_target_pairs={{0,2},{1,3},{2,4},{3,5},{4,6},{5,7},{6,0},{7,1},{8,14},{9,15},{10,... | collective-permute-start | bytes 786440 | tf_op jit(solution)/shard_map/ppermute | solution.py:240
  49.5 6.4 %collective-permute-start.4 = (bf16[512,256]{1,0:T(8,128)(2,1)S(1)}, bf16[512,256]{1,0:T(8,128)(2,1)S(1)}, u32[]{:S(2)}, u32[]{:S(2)}) collective-permute-start(bf16[512,256]{1,0:T(8,128)(2,1)S(1)} %get-tuple-element.28), channel_id=1, source_target_pairs={{0,6},{1,7},{2,0},{3,1},{4,2},{5,3},{6,4},{7,5},{8,10},{9,11},{10,... | collective-permute-start | bytes 786440 | tf_op jit(solution)/shard_map/ppermute | solution.py:240
  55.8 0.0 collective-permute-done.across_ref
  55.9 1.9 %collective-permute-done.3.up2_ref = bf16[512,256]{1,0:T(8,128)(2,1)S(1)} collective-permute-done((bf16[512,256]{1,0:T(8,128)(2,1)S(1)}, bf16[512,256]{1,0:T(8,128)(2,1)S(1)}, u32[]{:S(2)}, u32[]{:S(2)}) %collective-permute-start.3) | collective-permute-done | bytes 262176 | tf_op jit(solution)/shard_map/ppermute | solution.py:240
  57.8 16.3 %collective-permute-done.4.down2_ref = bf16[512,256]{1,0:T(8,128)(2,1)S(1)} collective-permute-done((bf16[512,256]{1,0:T(8,128)(2,1)S(1)}, bf16[512,256]{1,0:T(8,128)(2,1)S(1)}, u32[]{:S(2)}, u32[]{:S(2)}) %collective-permute-start.4) | collective-permute-done | bytes 262176 | tf_op jit(solution)/shard_map/ppermute | solution.py:240
  74.1 0.0 all-to-all-done
  74.1 0.0 copy-done
  74.1 1.1 %shard_map.57 = bf16[512,128]{1,0:T(8,128)(2,1)S(1)} custom-call(bf16[512,256]{1,0:T(8,128)(2,1)S(1)} %copy-done, bf16[512,256]{1,0:T(8,128)(2,1)S(1)} %collective-permute-done.across_ref, bf16[2,512,256]{2,1,0:T(8,128)(2,1)S(1)} %collective-permute-done.1.up_ref, bf16[2,512,256]{2,1,0:T(8,128)(2,1)S(1)} %collective-permute-done.2.down_ref, ...), custom_call_target="tpu_custom_call" | custom-call | flops 134217728 | bytes 3145728 | tf_op jit(solution)/shard_map/pallas_call | solution.py:216
  75.2 29.5 %all_to_all.10 = bf16[32,16,128]{2,1,0:T(8,128)(2,1)S(1)} all-to-all(bf16[32,16,128]{2,1,0:T(8,128)(2,1)S(1)} %bitcast.5), channel_id=1, replica_groups=mesh['aa'=32,'col'=4,'pb'=8] {'col','pb'}, dimensions={0} | all-to-all | bytes 262144 | tf_op jit(solution)/shard_map/all_to_all | solution.py:265
  104.7 0.6 convert_reduce_fusion
Async XLA Ops:
  7.4 66.6 %copy-start = (bf16[512,256]{1,0:T(8,128)(2,1)S(1)}, bf16[512,256]{1,0:T(8,128)(2,1)}, u32[]{:S(2)}) copy-start(bf16[512,256]{1,0:T(8,128)(2,1)} %get-tuple-element.30.own_ref) | copy-start | bytes 786436
  7.4 66.6 %all-to-all-start = ((bf16[32,16,1024]{2,1,0:T(8,128)(2,1)}), bf16[32,16,1024]{2,1,0:T(8,128)(2,1)S(1)}, u32[]{:S(2)}, u32[]{:S(2)}) async-start(bf16[32,16,1024]{2,1,0:T(8,128)(2,1)} %get-tuple-element.29), calls=%async_computation | async-start | bytes 2097152 | tf_op jit(solution)/shard_map/all_to_all | solution.py:253
  22.6 14.2 %collective-permute-start.1 = (bf16[2,512,256]{2,1,0:T(8,128)(2,1)}, bf16[2,512,256]{2,1,0:T(8,128)(2,1)S(1)}, u32[]{:S(2)}, u32[]{:S(2)}) collective-permute-start(bf16[2,512,256]{2,1,0:T(8,128)(2,1)} %get-tuple-element.23), channel_id=1, source_target_pairs={{0,1},{1,2},{2,3},{3,4},{4,5},{5,6},{6,7},{7,0},{8,15},{9,8},{10,9... | collective-permute-start | bytes 1572872 | tf_op jit(solution)/shard_map/ppermute | solution.py:240
  28.5 14.2 %collective-permute-start.2 = (bf16[2,512,256]{2,1,0:T(8,128)(2,1)}, bf16[2,512,256]{2,1,0:T(8,128)(2,1)S(1)}, u32[]{:S(2)}, u32[]{:S(2)}) collective-permute-start(bf16[2,512,256]{2,1,0:T(8,128)(2,1)} %get-tuple-element.24), channel_id=1, source_target_pairs={{0,7},{1,0},{2,1},{3,2},{4,3},{5,4},{6,5},{7,6},{8,9},{9,10},{10,1... | collective-permute-start | bytes 1572872 | tf_op jit(solution)/shard_map/ppermute | solution.py:240
  30.5 25.4 %collective-permute-start = (bf16[512,256]{1,0:T(8,128)(2,1)}, bf16[512,256]{1,0:T(8,128)(2,1)S(1)}, u32[]{:S(2)}, u32[]{:S(2)}) collective-permute-start(bf16[512,256]{1,0:T(8,128)(2,1)} %get-tuple-element.22), channel_id=1, source_target_pairs={{0,4},{1,5},{2,6},{3,7},{4,0},{5,1},{6,2},{7,3},{8,12},{9,13},{10,... | collective-permute-start | bytes 786440 | tf_op jit(solution)/shard_map/ppermute | solution.py:240
  42.7 1.0 copy-start.1
  43.7 0.9 copy-start.2
  44.8 13.0 %collective-permute-start.3 = (bf16[512,256]{1,0:T(8,128)(2,1)S(1)}, bf16[512,256]{1,0:T(8,128)(2,1)S(1)}, u32[]{:S(2)}, u32[]{:S(2)}) collective-permute-start(bf16[512,256]{1,0:T(8,128)(2,1)S(1)} %get-tuple-element.27), channel_id=1, source_target_pairs={{0,2},{1,3},{2,4},{3,5},{4,6},{5,7},{6,0},{7,1},{8,14},{9,15},{10,... | collective-permute-start | bytes 786440 | tf_op jit(solution)/shard_map/ppermute | solution.py:240
  49.5 24.6 %collective-permute-start.4 = (bf16[512,256]{1,0:T(8,128)(2,1)S(1)}, bf16[512,256]{1,0:T(8,128)(2,1)S(1)}, u32[]{:S(2)}, u32[]{:S(2)}) collective-permute-start(bf16[512,256]{1,0:T(8,128)(2,1)S(1)} %get-tuple-element.28), channel_id=1, source_target_pairs={{0,6},{1,7},{2,0},{3,1},{4,2},{5,3},{6,4},{7,5},{8,10},{9,11},{10,... | collective-permute-start | bytes 786440 | tf_op jit(solution)/shard_map/ppermute | solution.py:240
